TPU v7x, 256 devices: a whole 4x4x8 slice. The times are simulated.
256 devices in a mesh: dp: 2 (over core), pipe: 8 (over y, x_lo), tensor: 16 (over x_hi, z).
Axes of the slice: x: 4 (x_hi: 2, x_lo: 2; x = x_hi * 2 + x_lo), y: 4, z: 8, core: 2. Of those that a mesh axis runs over, the one named last changes fastest.
Arguments:
- forward_acts: bfloat16 [1024, 8192], P(('dp', 'tensor'), 'pipe'), parts along dimension 0, may hold values from -6 to 6
- backward_grad: bfloat16 [1024, 8192], P(('dp', 'tensor'), 'pipe'), parts along dimension 0, may hold values from -6 to 6
- stored_gate: bfloat16 [1024, 14336], P(('dp', 'pipe'), 'tensor'), parts along dimension 0, may hold values from -8 to 8
- stored_up: bfloat16 [1024, 14336], P(('dp', 'pipe'), 'tensor'), parts along dimension 0, may hold values from -6 to 6
- gate_weight: bfloat16 [8192, 14336], P('pipe', 'tensor'), may hold values from -0.0625 to 0.0625
- up_weight: bfloat16 [8192, 14336], P('pipe', 'tensor'), may hold values from -0.0625 to 0.0625
- down_weight: bfloat16 [14336, 8192], P('tensor', 'pipe'), may hold values from -0.046875 to 0.046875
Outputs:
- layer_output: bfloat16 [1024, 8192], P(('dp', 'tensor'), 'pipe'), parts along dimension 0
- input_grad: bfloat16 [1024, 8192], P(('dp', 'tensor'), 'pipe'), parts along dimension 0
There are 2 independent parts, one for each index of `dp`. A program takes and returns all parts, laid end to end along the dimension named above; an argument that names none is the same for every part. Nothing has to cross between parts.
All inputs are finite; a program needn't handle non-finite values.
Results may differ from a plain program's by a relative error of at most 0.005.
Values may be sent and summed in bfloat16 or wider, within the bound.
A program may use at most 64 MiB of HBM per device.

v0:
```python
import jax
import jax.numpy as jnp
from jax import lax
from jax.sharding import PartitionSpec as P


def make_slopes(hidden_grad, gate_vals, up_vals):
    gate_wide = gate_vals.astype(jnp.float32)
    up_wide = up_vals.astype(jnp.float32)
    sigma = jax.nn.sigmoid(gate_wide)
    gate_slope = (hidden_grad * up_wide * sigma * (1.0 + gate_wide * (1.0 - sigma))).astype(
        jnp.bfloat16
    )
    up_slope = (hidden_grad * gate_wide * sigma).astype(jnp.bfloat16)
    return jnp.concatenate([gate_slope, up_slope], axis=1)


def per_device(
    forward_acts, backward_grad, stored_gate, stored_up, gate_weight, up_weight, down_weight
):
    hidden_width = gate_weight.shape[1]
    contract_last = (((1,), (1,)), ((), ()))
    paired = jnp.concatenate([gate_weight, up_weight], axis=1)
    whole_acts = lax.all_gather(forward_acts, "tensor", axis=0, tiled=True)
    picked = whole_acts
    summed = lax.psum_scatter(
        jnp.dot(picked, paired, preferred_element_type=jnp.float32),
        "pipe",
        scatter_dimension=0,
        tiled=True,
    )
    hidden_part = (jax.nn.silu(summed[:, :hidden_width]) * summed[:, hidden_width:]).astype(
        jnp.bfloat16
    )
    hidden = lax.all_gather(hidden_part, "pipe", axis=0, tiled=True)
    picked = hidden
    layer_output = lax.psum_scatter(
        jnp.dot(picked, down_weight, preferred_element_type=jnp.float32),
        "tensor",
        scatter_dimension=0,
        tiled=True,
    ).astype(jnp.bfloat16)
    whole_grad = lax.all_gather(backward_grad, "tensor", axis=0, tiled=True)
    picked = whole_grad
    hidden_grad = lax.psum_scatter(
        lax.dot_general(picked, down_weight, contract_last, preferred_element_type=jnp.float32),
        "pipe",
        scatter_dimension=0,
        tiled=True,
    )
    local_slopes = make_slopes(hidden_grad, stored_gate, stored_up)
    all_slopes = lax.all_gather(local_slopes, "pipe", axis=0, tiled=True)
    picked = all_slopes
    input_grad = lax.psum_scatter(
        lax.dot_general(picked, paired, contract_last, preferred_element_type=jnp.float32),
        "tensor",
        scatter_dimension=0,
        tiled=True,
    ).astype(jnp.bfloat16)
    return (layer_output, input_grad)


def solution(mesh):
    in_specs = (
        P(("dp", "tensor"), "pipe"),
        P(("dp", "tensor"), "pipe"),
        P(("dp", "pipe"), "tensor"),
        P(("dp", "pipe"), "tensor"),
        P("pipe", "tensor"),
        P("pipe", "tensor"),
        P("tensor", "pipe"),
    )
    out_specs = (P(("dp", "tensor"), "pipe"), P(("dp", "tensor"), "pipe"))
    return jax.shard_map(
        per_device, mesh=mesh, in_specs=in_specs, out_specs=out_specs, check_vma=False
    )
```

profile of v0, /device:TPU:32, one launch (start us, length us, event | category | flops | bytes accessed | tf_op | source)
XLA Modules:
  0.0 778.3 jit_solution(1164099196765025358)
XLA Ops:
  7.2 0.7 all-gather.6.cloned.1.call-update
  8.0 83.3 %all-gather.6.cloned.1.call-done = bf16[512,1024]{1,0:T(8,128)(2,1)} async-done(((bf16[32,1024]{1,0:T(8,128)(2,1)}), bf16[512,1024]{1,0:T(8,128)(2,1)}) %all-gather.6.cloned.1.call-update) | async-done | bytes 1048592 | tf_op jit(solution)/shard_map/all_gather | solution.py:43
  91.2 3.8 fusion.10
  95.1 0.7 all-gather.4.cloned.1.call-update
  95.8 46.9 %reduce-scatter.15.cloned.1.call-done = f32[64,896]{1,0:T(8,128)} async-done(((f32[512,896]{1,0:T(8,128)}), f32[64,896]{1,0:T(8,128)}) %reduce-scatter.15.cloned.1.call-update) | async-done | bytes 229392 | tf_op jit(solution)/shard_map/reduce_scatter | solution.py:45
  142.7 1.1 fusion.5
  143.8 0.7 pad_maximum_fusion
  144.6 0.0 reduce-scatter.13.cloned.1.call-start
  144.6 3.1 constant_dynamic-update-slice_fusion.1
  147.7 1.4 constant_dynamic-update-slice_fusion
  149.1 73.5 %all-gather.4.cloned.1.call-done = bf16[512,1024]{1,0:T(8,128)(2,1)} async-done(((bf16[32,1024]{1,0:T(8,128)(2,1)}), bf16[512,1024]{1,0:T(8,128)(2,1)}) %all-gather.4.cloned.1.call-update) | async-done | bytes 1048592 | tf_op jit(solution)/shard_map/all_gather | solution.py:24
  222.6 6.3 convolution_bitcast_fusion
  228.9 5.1 copy.23
  234.1 37.4 %all-gather.8.cloned.1.call-done = bf16[512,1792]{1,0:T(8,128)(2,1)} async-done(((bf16[64,1792]{1,0:T(8,128)(2,1)}), bf16[512,1792]{1,0:T(8,128)(2,1)}) %all-gather.8.cloned.1.call-update) | async-done | bytes 1835024 | tf_op jit(solution)/shard_map/all_gather | solution.py:52
  271.5 6.0 fusion.11
  277.5 0.0 reduce-scatter.9.cloned.1.call-start
  277.6 79.6 %reduce-scatter.13.cloned.1.call-done = f32[64,1792]{1,0:T(8,128)} async-done(((f32[512,1792]{1,0:T(8,128)}), f32[64,1792]{1,0:T(8,128)}) %reduce-scatter.13.cloned.1.call-update) | async-done | bytes 458768 | tf_op jit(solution)/shard_map/reduce_scatter | solution.py:26
  357.2 1.1 fusion.8
  358.3 32.2 %all_gather.13 = bf16[512,896]{1,0:T(8,128)(2,1)S(1)} all-gather(bf16[64,896]{1,0:T(8,128)(2,1)S(1)} %fusion.8), channel_id=1, replica_groups=mesh['dp'=2,'pipe'=8,'tensor'=16] {'pipe'}, dimensions={0}, use_global_device_ids=true | all-gather | bytes 1032192 | tf_op jit(solution)/shard_map/all_gather | solution.py:35
  390.5 2.6 fusion.9
  393.1 171.0 %reduce-scatter.11.cloned.1.call-done = f32[32,1024]{1,0:T(8,128)} async-done(((f32[512,1024]{1,0:T(8,128)}), f32[32,1024]{1,0:T(8,128)}) %reduce-scatter.11.cloned.1.call-update) | async-done | bytes 131088 | tf_op jit(solution)/shard_map/reduce_scatter | solution.py:54
  564.1 1.5 convert_element_type.27
  565.6 204.3 %reduce-scatter.9.cloned.1.call-done = f32[32,1024]{1,0:T(8,128)} async-done(((f32[512,1024]{1,0:T(8,128)}), f32[32,1024]{1,0:T(8,128)}) %reduce-scatter.9.cloned.1.call-update) | async-done | bytes 131088 | tf_op jit(solution)/shard_map/reduce_scatter | solution.py:37
  769.9 1.5 convert_element_type.22
  (18 shorter events, 0.3 us)
Async XLA Ops:
  7.2 84.1 %copy-start = (bf16[896,1024]{1,0:T(8,128)(2,1)S(1)}, bf16[896,1024]{1,0:T(8,128)(2,1)}, u32[]{:S(2)}) copy-start(bf16[896,1024]{1,0:T(8,128)(2,1)} %param.13) | copy-start | bytes 5505028
  7.2 84.1 %all-gather.6.cloned.1.call-start = ((), (), s32[]{:S(2)}) async-start(), calls=%async_computation.6 | async-start | bytes 1114112 | tf_op jit(solution)/shard_map/all_gather | solution.py:43
  7.9 134.8 %copy-start.2 = (bf16[64,896]{1,0:T(8,128)(2,1)S(1)}, bf16[64,896]{1,0:T(8,128)(2,1)}, u32[]{:S(2)}) copy-start(bf16[64,896]{1,0:T(8,128)(2,1)} %param.9) | copy-start | bytes 344068
  7.9 134.8 %copy-start.3 = (bf16[64,896]{1,0:T(8,128)(2,1)S(1)}, bf16[64,896]{1,0:T(8,128)(2,1)}, u32[]{:S(2)}) copy-start(bf16[64,896]{1,0:T(8,128)(2,1)} %param.10) | copy-start | bytes 344068
  7.9 134.8 %reduce-scatter.15.cloned.1.call-start = ((), (), s32[]{:S(2)}) async-start(), calls=%async_computation.10 | async-start | bytes 2064384 | tf_op jit(solution)/shard_map/reduce_scatter | solution.py:45
  95.1 127.5 %all-gather.4.cloned.1.call-start = ((), (), s32[]{:S(2)}) async-start(), calls=%async_computation.4 | async-start | bytes 1114112 | tf_op jit(solution)/shard_map/all_gather | solution.py:24
  95.8 175.7 %all-gather.8.cloned.1.call-start = ((), (), s32[]{:S(2)}) async-start(), calls=%async_computation.7 | async-start | bytes 2064384 | tf_op jit(solution)/shard_map/all_gather | solution.py:52
  144.6 212.7 %reduce-scatter.13.cloned.1.call-start = ((), (), s32[]{:S(2)}) async-start(), calls=%async_computation.9 | async-start | bytes 4128768 | tf_op jit(solution)/shard_map/reduce_scatter | solution.py:26
  144.6 3.1 copy-start.1
  234.1 330.0 %reduce-scatter.11.cloned.1.call-start = ((), (), s32[]{:S(2)}) async-start(), calls=%async_computation.8 | async-start | bytes 2228224 | tf_op jit(solution)/shard_map/reduce_scatter | solution.py:54
  277.5 492.4 %reduce-scatter.9.cloned.1.call-start = ((), (), s32[]{:S(2)}) async-start(), calls=%async_computation.5 | async-start | bytes 2228224 | tf_op jit(solution)/shard_map/reduce_scatter | solution.py:37
Sparse Core Ops, SparseCore 0:
  10.6 80.5 all-gather.5
  95.2 47.5 reduce-scatter.14
  145.3 77.2 all-gather.3
  224.2 47.2 all-gather.7
  273.9 83.2 reduce-scatter.12
  361.0 203.0 reduce-scatter.10
  568.0 201.8 reduce-scatter.8
where the time goes:
time: 780 us; the launch traced here: 778 us
  waiting for transfers between devices  697 us (89%)
  blocking collectives  32.2 us (4%)
  matrix products  18.7 us (2%)
  between operations  14.2 us (2%)
  local copies, waits for them, and re-layouts  9.64 us (1%)
    reduce_scatter x1, waiting for transfers between devices, per_device(): lax.psum_scatter(jnp.dot(picked, down_weight, preferred_element_type=jnp....  204 us
    reduce_scatter x1, waiting for transfers between devices, per_device(): lax.psum_scatter(lax.dot_general(picked, paired, contract_last, preferred...  171 us
    all_gather x1, waiting for transfers between devices, per_device(): whole_grad = lax.all_gather(backward_grad, 'tensor', axis=0, tiled=True)  83.3 us
    reduce_scatter x1, waiting for transfers between devices, per_device(): lax.psum_scatter(jnp.dot(picked, paired, preferred_element_type=jnp.float...  79.6 us
    all_gather x1, waiting for transfers between devices, per_device(): whole_acts = lax.all_gather(forward_acts, 'tensor', axis=0, tiled=True)  73.5 us
    reduce_scatter x1, waiting for transfers between devices, per_device(): lax.psum_scatter(lax.dot_general(picked, down_weight, contract_last, pref...  46.9 us
    all_gather x1, waiting for transfers between devices, per_device(): all_slopes = lax.all_gather(local_slopes, 'pipe', axis=0, tiled=True)  37.4 us
    all_gather x1, blocking collectives, per_device(): hidden = lax.all_gather(hidden_part, 'pipe', axis=0, tiled=True)  32.2 us
  transfers between devices with their start and end apart: 7, of which 7 were waited for; matrix products, arithmetic and copies ran while one was open for 4% of the time, Pallas kernels for 0%

commit v1 on v0

v1 whole, which is shorter than its diff:
```python
import jax
import jax.numpy as jnp
from jax import lax
from jax.sharding import PartitionSpec as P


def make_slopes(hidden_grad, gate_vals, up_vals):
    gate_wide = gate_vals.astype(jnp.float32)
    up_wide = up_vals.astype(jnp.float32)
    sigma = jax.nn.sigmoid(gate_wide)
    gate_slope = (hidden_grad * up_wide * sigma * (1.0 + gate_wide * (1.0 - sigma))).astype(
        jnp.bfloat16
    )
    up_slope = (hidden_grad * gate_wide * sigma).astype(jnp.bfloat16)
    return jnp.concatenate([gate_slope, up_slope], axis=1)


def gather_rows(block, axis, count):
    sent = jnp.broadcast_to(block[None], (count,) + block.shape)
    got = lax.all_to_all(sent, axis, 0, 0, tiled=False)
    return got.reshape((count * block.shape[0],) + block.shape[1:])


def scatter_sum_rows(partial, axis, count):
    rows = partial.shape[0] // count
    sent = partial.reshape((count, rows) + partial.shape[1:]).astype(jnp.bfloat16)
    got = lax.all_to_all(sent, axis, 0, 0, tiled=False)
    return got.astype(jnp.float32).sum(axis=0)


def per_device(
    forward_acts, backward_grad, stored_gate, stored_up, gate_weight, up_weight, down_weight
):
    n_pipe = lax.axis_size("pipe")
    n_tensor = lax.axis_size("tensor")
    hidden_width = gate_weight.shape[1]
    contract_last = (((1,), (1,)), ((), ()))

    whole_acts = gather_rows(forward_acts, "tensor", n_tensor)
    gate_part = jnp.dot(whole_acts, gate_weight, preferred_element_type=jnp.float32)
    up_part = jnp.dot(whole_acts, up_weight, preferred_element_type=jnp.float32)
    summed = scatter_sum_rows(jnp.concatenate([gate_part, up_part], axis=1), "pipe", n_pipe)
    hidden_part = (jax.nn.silu(summed[:, :hidden_width]) * summed[:, hidden_width:]).astype(
        jnp.bfloat16
    )
    hidden = gather_rows(hidden_part, "pipe", n_pipe)
    layer_output = scatter_sum_rows(
        jnp.dot(hidden, down_weight, preferred_element_type=jnp.float32), "tensor", n_tensor
    ).astype(jnp.bfloat16)

    whole_grad = gather_rows(backward_grad, "tensor", n_tensor)
    hidden_grad = scatter_sum_rows(
        lax.dot_general(whole_grad, down_weight, contract_last, preferred_element_type=jnp.float32),
        "pipe",
        n_pipe,
    )
    local_slopes = make_slopes(hidden_grad, stored_gate, stored_up)
    all_slopes = gather_rows(local_slopes, "pipe", n_pipe)
    input_grad_part = lax.dot_general(
        all_slopes[:, :hidden_width], gate_weight, contract_last, preferred_element_type=jnp.float32
    ) + lax.dot_general(
        all_slopes[:, hidden_width:], up_weight, contract_last, preferred_element_type=jnp.float32
    )
    input_grad = scatter_sum_rows(input_grad_part, "tensor", n_tensor).astype(jnp.bfloat16)
    return (layer_output, input_grad)


def solution(mesh):
    in_specs = (
        P(("dp", "tensor"), "pipe"),
        P(("dp", "tensor"), "pipe"),
        P(("dp", "pipe"), "tensor"),
        P(("dp", "pipe"), "tensor"),
        P("pipe", "tensor"),
        P("pipe", "tensor"),
        P("tensor", "pipe"),
    )
    out_specs = (P(("dp", "tensor"), "pipe"), P(("dp", "tensor"), "pipe"))
    return jax.shard_map(
        per_device, mesh=mesh, in_specs=in_specs, out_specs=out_specs, check_vma=False
    )
```

time: 780 us -> 237 us (0.30)
  waiting for transfers between devices: 697 us -> 117 us
  starting transfers between devices: 0.28 us -> 46.1 us
  between operations: 14.2 us -> 0.79 us
    reduce_scatter x4 -> x0, waiting for transfers between devices: 502 us -> none  [the longest x1 204 us: per_device(): lax.psum_scatter(jnp.dot(picked, down_weight, preferred_element_type=jnp....]
    all_gather x3 -> x0, waiting for transfers between devices: 194 us -> none  [the longest x1 83.3 us: per_device(): whole_grad = lax.all_gather(backward_grad, 'tensor', axis=0, tiled=True)]
    all_to_all x0 -> x7, waiting for transfers between devices: none -> 117 us  [the longest x4 72.2 us: scatter_sum_rows(): got = lax.all_to_all(sent, axis, 0, 0, tiled=False)]
    all_to_all x0 -> x7, starting transfers between devices: none -> 46.1 us  [the longest x4 32.8 us: scatter_sum_rows(): got = lax.all_to_all(sent, axis, 0, 0, tiled=False)]
    all_to_all x0 -> x1, blocking collectives: none -> 38.5 us  [gather_rows(): got = lax.all_to_all(sent, axis, 0, 0, tiled=False)]
    all_gather x1 -> x0, blocking collectives: 32.2 us -> none  [per_device(): hidden = lax.all_gather(hidden_part, 'pipe', axis=0, tiled=True)]
    dot_general x3 -> x6, matrix products: 14.9 us -> 18.5 us  [the longest x1 4.06 us: per_device(): lax.dot_general(whole_grad, down_weight, contract_last, preferred_element...]
  transfers between devices with their start and end apart: 7 -> 7, of which waited for: 7 -> 7; matrix products, arithmetic and copies ran while one was open for 4% -> 10% of each run, Pallas kernels for 0% -> 0%
where the time goes in v1:
time: 237 us; the launch traced here: 234 us
  waiting for transfers between devices  117 us (49%)
  starting transfers between devices  46.1 us (19%)
  blocking collectives  38.5 us (16%)
  matrix products  18.5 us (8%)
  local copies, waits for them, and re-layouts  6.56 us (3%)
  other arithmetic  6.42 us (3%)
    all_to_all x4, waiting for transfers between devices, scatter_sum_rows(): got = lax.all_to_all(sent, axis, 0, 0, tiled=False)  72.2 us
    all_to_all x3, waiting for transfers between devices, gather_rows(): got = lax.all_to_all(sent, axis, 0, 0, tiled=False)  45 us
    all_to_all x1, blocking collectives, gather_rows(): got = lax.all_to_all(sent, axis, 0, 0, tiled=False)  38.5 us
    all_to_all x4, starting transfers between devices, scatter_sum_rows(): got = lax.all_to_all(sent, axis, 0, 0, tiled=False)  32.8 us
    all_to_all x3, starting transfers between devices, gather_rows(): got = lax.all_to_all(sent, axis, 0, 0, tiled=False)  13.3 us
    reduce_sum x4, other arithmetic, scatter_sum_rows(): return got.astype(jnp.float32).sum(axis=0)  4.81 us
  transfers between devices with their start and end apart: 7, of which 7 were waited for; matrix products, arithmetic and copies ran while one was open for 10% of the time, Pallas kernels for 0%

profile of v1, /device:TPU:32, one launch (start us, length us, event | category | flops | bytes accessed | tf_op | source)
XLA Modules:
  0.0 234.1 jit_solution(12174290372329034980)
XLA Ops:
  1.8 38.5 %all_to_all.40 = bf16[16,32,1024]{2,1,0:T(8,128)(2,1)} all-to-all(bf16[16,32,1024]{2,1,0:T(8,128)(2,1)S(1)} %broadcast_in_dim.10), channel_id=1, replica_groups=mesh['dp'=2,'pipe'=8,'tensor'=16] {'tensor'}, dimensions={0} | all-to-all | bytes 2097152 | tf_op jit(solution)/shard_map/all_to_all | solution.py:20
  41.4 5.4 %all-to-all-start = ((bf16[16,32,1024]{2,1,0:T(8,128)(2,1)}), bf16[16,32,1024]{2,1,0:T(8,128)(2,1)S(1)}, u32[]{:S(2)}, u32[]{:S(2)}) async-start(bf16[16,32,1024]{2,1,0:T(8,128)(2,1)} %broadcast_in_dim.8), calls=%async_computation | async-start | bytes 2097152 | tf_op jit(solution)/shard_map/all_to_all | solution.py:20
  46.8 4.1 %fusion.7 = bf16[8,64,896]{2,1,0:T(8,128)(2,1)} fusion(bf16[8,64,1024]{2,1,0:T(8,128)(2,1)} %bitcast.27, bf16[896,1024]{1,0:T(8,128)(2,1)} %param.13), kind=kOutput, calls=%fused_computation.9 | convolution fusion | flops 939982848 | bytes 3801088 | tf_op jit(solution)/shard_map/dot_general | solution.py:53
  50.9 23.3 %all-to-all-done = bf16[16,32,1024]{2,1,0:T(8,128)(2,1)S(1)} async-done(((bf16[16,32,1024]{2,1,0:T(8,128)(2,1)}), bf16[16,32,1024]{2,1,0:T(8,128)(2,1)S(1)}, u32[]{:S(2)}, u32[]{:S(2)}) %all-to-all-start) | async-done | bytes 1048608 | tf_op jit(solution)/shard_map/all_to_all | solution.py:20
  75.1 4.5 %all-to-all-start.5 = ((bf16[8,64,896]{2,1,0:T(8,128)(2,1)}), bf16[8,64,896]{2,1,0:T(8,128)(2,1)S(1)}, u32[]{:S(2)}, u32[]{:S(2)}) async-start(bf16[8,64,896]{2,1,0:T(8,128)(2,1)} %fusion.7), calls=%async_computation.5 | async-start | bytes 1835008 | tf_op jit(solution)/shard_map/all_to_all | solution.py:27
  79.6 3.2 %convolution_convert_fusion = bf16[512,896]{1,0:T(8,128)(2,1)S(1)} fusion(bf16[512,1024]{1,0:T(8,128)(2,1)} %bitcast.24, bf16[1024,896]{1,0:T(8,128)(2,1)} %param.12), kind=kOutput, calls=%fused_computation.10 | convolution fusion | flops 939982848 | bytes 3801088 | tf_op jit(solution)/shard_map/dot_general | solution.py:41
  84.1 1.4 pad_maximum_fusion
  85.5 5.6 %all-to-all-done.5 = bf16[8,64,896]{2,1,0:T(8,128)(2,1)S(1)} async-done(((bf16[8,64,896]{2,1,0:T(8,128)(2,1)}), bf16[8,64,896]{2,1,0:T(8,128)(2,1)S(1)}, u32[]{:S(2)}, u32[]{:S(2)}) %all-to-all-start.5) | async-done | bytes 917536 | tf_op jit(solution)/shard_map/all_to_all | solution.py:27
  91.0 4.5 %all-to-all-start.1 = ((bf16[8,64,1792]{2,1,0:T(8,128)(2,1)}), bf16[8,64,1792]{2,1,0:T(8,128)(2,1)}, u32[]{:S(2)}, u32[]{:S(2)}) async-start(bf16[8,64,1792]{2,1,0:T(8,128)(2,1)} %bitcast.23), calls=%async_computation.1 | async-start | bytes 3670016 | tf_op jit(solution)/shard_map/all_to_all | solution.py:27
  95.8 19.5 %all-to-all-done.1 = bf16[8,64,1792]{2,1,0:T(8,128)(2,1)} async-done(((bf16[8,64,1792]{2,1,0:T(8,128)(2,1)}), bf16[8,64,1792]{2,1,0:T(8,128)(2,1)}, u32[]{:S(2)}, u32[]{:S(2)}) %all-to-all-start.1) | async-done | bytes 1835040 | tf_op jit(solution)/shard_map/all_to_all | solution.py:27
  115.3 1.4 broadcast_in_dim.11
  116.7 4.3 %all-to-all-start.6 = ((bf16[8,64,1792]{2,1,0:T(8,128)(2,1)}), bf16[8,64,1792]{2,1,0:T(8,128)(2,1)}, u32[]{:S(2)}, u32[]{:S(2)}) async-start(bf16[8,64,1792]{2,1,0:T(8,128)(2,1)} %broadcast_in_dim.11), calls=%async_computation.6 | async-start | bytes 3670016 | tf_op jit(solution)/shard_map/all_to_all | solution.py:20
  121.1 1.8 convert_reduce_fusion
  123.0 17.0 %all-to-all-done.6 = bf16[8,64,1792]{2,1,0:T(8,128)(2,1)} async-done(((bf16[8,64,1792]{2,1,0:T(8,128)(2,1)}), bf16[8,64,1792]{2,1,0:T(8,128)(2,1)}, u32[]{:S(2)}, u32[]{:S(2)}) %all-to-all-start.6) | async-done | bytes 1835040 | tf_op jit(solution)/shard_map/all_to_all | solution.py:20
  141.0 3.6 %all-to-all-start.2 = ((bf16[8,64,896]{2,1,0:T(8,128)(2,1)}), bf16[8,64,896]{2,1,0:T(8,128)(2,1)S(1)}, u32[]{:S(2)}, u32[]{:S(2)}) async-start(bf16[8,64,896]{2,1,0:T(8,128)(2,1)} %broadcast_in_dim.9), calls=%async_computation.2 | async-start | bytes 1835008 | tf_op jit(solution)/shard_map/all_to_all | solution.py:20
  144.6 2.6 %fusion.11 = f32[512,1024]{1,0:T(8,128)S(1)} fusion(bf16[1024,896]{1,0:T(8,128)(2,1)S(1)} %copy-done, bf16[512,1792]{1,0:T(8,128)(2,1)} %bitcast.5), kind=kOutput, calls=%fused_computation.13 | convolution fusion | flops 939524096 | bytes 4849664 | tf_op jit(solution)/shard_map/dot_general | solution.py:59
  147.2 3.5 %add_convert_fusion = bf16[512,1024]{1,0:T(8,128)(2,1)} fusion(f32[512,1024]{1,0:T(8,128)S(1)} %fusion.11, bf16[1024,896]{1,0:T(8,128)(2,1)S(1)} %copy-done.7, bf16[512,1792]{1,0:T(8,128)(2,1)} %bitcast.5), kind=kOutput, calls=%fused_computation.1 | convolution fusion | flops 940572672 | bytes 5898240 | tf_op jit(solution)/shard_map/dot_general | solution.py:61
  150.6 4.7 %all-to-all-done.2 = bf16[8,64,896]{2,1,0:T(8,128)(2,1)S(1)} async-done(((bf16[8,64,896]{2,1,0:T(8,128)(2,1)}), bf16[8,64,896]{2,1,0:T(8,128)(2,1)S(1)}, u32[]{:S(2)}, u32[]{:S(2)}) %all-to-all-start.2) | async-done | bytes 917536 | tf_op jit(solution)/shard_map/all_to_all | solution.py:20
  156.3 18.7 %all-to-all-start.7 = ((bf16[16,32,1024]{2,1,0:T(8,128)(2,1)}), bf16[16,32,1024]{2,1,0:T(8,128)(2,1)S(1)}, u32[]{:S(2)}, u32[]{:S(2)}) async-start(bf16[16,32,1024]{2,1,0:T(8,128)(2,1)} %bitcast.26), calls=%async_computation.7 | async-start | bytes 2097152 | tf_op jit(solution)/shard_map/all_to_all | solution.py:27
  175.0 4.0 %fusion.4 = bf16[16,32,1024]{2,1,0:T(8,128)(2,1)} fusion(bf16[16,32,896]{2,1,0:T(8,128)(2,1)} %bitcast.28, bf16[896,1024]{1,0:T(8,128)(2,1)} %param.13), kind=kOutput, calls=%fused_computation.8 | convolution fusion | flops 940048384 | bytes 3801088 | tf_op jit(solution)/shard_map/dot_general | solution.py:48
  179.0 21.8 %all-to-all-done.7 = bf16[16,32,1024]{2,1,0:T(8,128)(2,1)S(1)} async-done(((bf16[16,32,1024]{2,1,0:T(8,128)(2,1)}), bf16[16,32,1024]{2,1,0:T(8,128)(2,1)S(1)}, u32[]{:S(2)}, u32[]{:S(2)}) %all-to-all-start.7) | async-done | bytes 1048608 | tf_op jit(solution)/shard_map/all_to_all | solution.py:27
  200.8 5.2 %all-to-all-start.3 = ((bf16[16,32,1024]{2,1,0:T(8,128)(2,1)}), bf16[16,32,1024]{2,1,0:T(8,128)(2,1)}, u32[]{:S(2)}, u32[]{:S(2)}) async-start(bf16[16,32,1024]{2,1,0:T(8,128)(2,1)} %fusion.4), calls=%async_computation.3 | async-start | bytes 2097152 | tf_op jit(solution)/shard_map/all_to_all | solution.py:27
  206.8 25.3 %all-to-all-done.3 = bf16[16,32,1024]{2,1,0:T(8,128)(2,1)} async-done(((bf16[16,32,1024]{2,1,0:T(8,128)(2,1)}), bf16[16,32,1024]{2,1,0:T(8,128)(2,1)}, u32[]{:S(2)}, u32[]{:S(2)}) %all-to-all-start.3) | async-done | bytes 1048608 | tf_op jit(solution)/shard_map/all_to_all | solution.py:27
  232.1 2.1 reduce_sum.43
  (25 shorter events, 7.6 us)
Async XLA Ops:
  0.6 82.2 %copy-start = (bf16[1024,896]{1,0:T(8,128)(2,1)S(1)}, bf16[1024,896]{1,0:T(8,128)(2,1)}, u32[]{:S(2)}) copy-start(bf16[1024,896]{1,0:T(8,128)(2,1)} %param.11) | copy-start | bytes 5505028
  0.6 39.6 %copy-start.6 = (bf16[32,1024]{1,0:T(8,128)(2,1)S(1)}, bf16[32,1024]{1,0:T(8,128)(2,1)}, u32[]{:S(2)}) copy-start(bf16[32,1024]{1,0:T(8,128)(2,1)} %param.7) | copy-start | bytes 196612
  41.4 32.8 %all-to-all-start = ((bf16[16,32,1024]{2,1,0:T(8,128)(2,1)}), bf16[16,32,1024]{2,1,0:T(8,128)(2,1)S(1)}, u32[]{:S(2)}, u32[]{:S(2)}) async-start(bf16[16,32,1024]{2,1,0:T(8,128)(2,1)} %broadcast_in_dim.8), calls=%async_computation | async-start | bytes 2097152 | tf_op jit(solution)/shard_map/all_to_all | solution.py:20
  74.1 1.0 copy-start.1
  75.1 15.9 %all-to-all-start.5 = ((bf16[8,64,896]{2,1,0:T(8,128)(2,1)}), bf16[8,64,896]{2,1,0:T(8,128)(2,1)S(1)}, u32[]{:S(2)}, u32[]{:S(2)}) async-start(bf16[8,64,896]{2,1,0:T(8,128)(2,1)} %fusion.7), calls=%async_computation.5 | async-start | bytes 1835008 | tf_op jit(solution)/shard_map/all_to_all | solution.py:27
  79.6 3.2 %copy-start.2 = (bf16[16,32,1024]{2,1,0:T(8,128)(2,1)S(1)}, bf16[16,32,1024]{2,1,0:T(8,128)(2,1)}, u32[]{:S(2)}) copy-start(bf16[16,32,1024]{2,1,0:T(8,128)(2,1)} %copy-done.1) | copy-start | bytes 3145732
  91.0 4.6 %copy-start.4 = (bf16[64,896]{1,0:T(8,128)(2,1)S(1)}, bf16[64,896]{1,0:T(8,128)(2,1)}, u32[]{:S(2)}) copy-start(bf16[64,896]{1,0:T(8,128)(2,1)} %param.9) | copy-start | bytes 344068
  91.0 4.6 %copy-start.5 = (bf16[64,896]{1,0:T(8,128)(2,1)S(1)}, bf16[64,896]{1,0:T(8,128)(2,1)}, u32[]{:S(2)}) copy-start(bf16[64,896]{1,0:T(8,128)(2,1)} %param.10) | copy-start | bytes 344068
  91.0 24.3 %all-to-all-start.1 = ((bf16[8,64,1792]{2,1,0:T(8,128)(2,1)}), bf16[8,64,1792]{2,1,0:T(8,128)(2,1)}, u32[]{:S(2)}, u32[]{:S(2)}) async-start(bf16[8,64,1792]{2,1,0:T(8,128)(2,1)} %bitcast.23), calls=%async_computation.1 | async-start | bytes 3670016 | tf_op jit(solution)/shard_map/all_to_all | solution.py:27
  116.7 23.2 %all-to-all-start.6 = ((bf16[8,64,1792]{2,1,0:T(8,128)(2,1)}), bf16[8,64,1792]{2,1,0:T(8,128)(2,1)}, u32[]{:S(2)}, u32[]{:S(2)}) async-start(bf16[8,64,1792]{2,1,0:T(8,128)(2,1)} %broadcast_in_dim.11), calls=%async_computation.6 | async-start | bytes 3670016 | tf_op jit(solution)/shard_map/all_to_all | solution.py:20
  141.0 14.3 %all-to-all-start.2 = ((bf16[8,64,896]{2,1,0:T(8,128)(2,1)}), bf16[8,64,896]{2,1,0:T(8,128)(2,1)S(1)}, u32[]{:S(2)}, u32[]{:S(2)}) async-start(bf16[8,64,896]{2,1,0:T(8,128)(2,1)} %broadcast_in_dim.9), calls=%async_computation.2 | async-start | bytes 1835008 | tf_op jit(solution)/shard_map/all_to_all | solution.py:20
  144.6 2.6 %copy-start.7 = (bf16[1024,896]{1,0:T(8,128)(2,1)S(1)}, bf16[1024,896]{1,0:T(8,128)(2,1)}, u32[]{:S(2)}) copy-start(bf16[1024,896]{1,0:T(8,128)(2,1)} %param.12) | copy-start | bytes 5505028
  155.3 0.9 copy-start.3
  156.3 44.5 %all-to-all-start.7 = ((bf16[16,32,1024]{2,1,0:T(8,128)(2,1)}), bf16[16,32,1024]{2,1,0:T(8,128)(2,1)S(1)}, u32[]{:S(2)}, u32[]{:S(2)}) async-start(bf16[16,32,1024]{2,1,0:T(8,128)(2,1)} %bitcast.26), calls=%async_computation.7 | async-start | bytes 2097152 | tf_op jit(solution)/shard_map/all_to_all | solution.py:27
  200.8 31.3 %all-to-all-start.3 = ((bf16[16,32,1024]{2,1,0:T(8,128)(2,1)}), bf16[16,32,1024]{2,1,0:T(8,128)(2,1)}, u32[]{:S(2)}, u32[]{:S(2)}) async-start(bf16[16,32,1024]{2,1,0:T(8,128)(2,1)} %fusion.4), calls=%async_computation.3 | async-start | bytes 2097152 | tf_op jit(solution)/shard_map/all_to_all | solution.py:27

commit v2 on v1

v2 whole, which is shorter than its diff:
```python
import jax
import jax.numpy as jnp
from jax import lax
from jax.sharding import PartitionSpec as P

PIPE_LINK = jnp.float32
TENSOR_LINK = jnp.bfloat16


def make_slopes(hidden_grad, gate_vals, up_vals):
    gate_wide = gate_vals.astype(jnp.float32)
    up_wide = up_vals.astype(jnp.float32)
    sigma = jax.nn.sigmoid(gate_wide)
    gate_slope = (hidden_grad * up_wide * sigma * (1.0 + gate_wide * (1.0 - sigma))).astype(
        jnp.bfloat16
    )
    up_slope = (hidden_grad * gate_wide * sigma).astype(jnp.bfloat16)
    return jnp.concatenate([gate_slope, up_slope], axis=1)


def gather_rows(block, axis, count):
    sent = jnp.broadcast_to(block[None], (count,) + block.shape)
    got = lax.all_to_all(sent, axis, 0, 0, tiled=False)
    return got.reshape((count * block.shape[0],) + block.shape[1:])


def scatter_sum_rows(partial, axis, count, link_dtype):
    rows = partial.shape[0] // count
    sent = partial.reshape((count, rows) + partial.shape[1:]).astype(link_dtype)
    got = lax.all_to_all(sent, axis, 0, 0, tiled=False)
    return got.astype(jnp.float32).sum(axis=0)


def per_device(
    forward_acts, backward_grad, stored_gate, stored_up, gate_weight, up_weight, down_weight
):
    n_pipe = lax.axis_size("pipe")
    n_tensor = lax.axis_size("tensor")
    hidden_width = gate_weight.shape[1]
    model_width = forward_acts.shape[1]
    contract_last = (((1,), (1,)), ((), ()))

    both = gather_rows(jnp.concatenate([forward_acts, backward_grad], axis=1), "tensor", n_tensor)
    whole_acts = both[:, :model_width]
    whole_grad = both[:, model_width:]

    gate_part = jnp.dot(whole_acts, gate_weight, preferred_element_type=jnp.float32)
    up_part = jnp.dot(whole_acts, up_weight, preferred_element_type=jnp.float32)
    grad_part = lax.dot_general(
        whole_grad, down_weight, contract_last, preferred_element_type=jnp.float32
    )
    summed = scatter_sum_rows(
        jnp.concatenate([gate_part, up_part, grad_part], axis=1), "pipe", n_pipe, PIPE_LINK
    )
    gate_pre = summed[:, :hidden_width]
    up_pre = summed[:, hidden_width : 2 * hidden_width]
    hidden_grad = summed[:, 2 * hidden_width :]
    hidden_part = (jax.nn.silu(gate_pre) * up_pre).astype(jnp.bfloat16)
    local_slopes = make_slopes(hidden_grad, stored_gate, stored_up)

    rows = gather_rows(jnp.concatenate([hidden_part, local_slopes], axis=1), "pipe", n_pipe)
    hidden = rows[:, :hidden_width]
    gate_slopes = rows[:, hidden_width : 2 * hidden_width]
    up_slopes = rows[:, 2 * hidden_width :]

    out_part = jnp.dot(hidden, down_weight, preferred_element_type=jnp.float32)
    in_part = lax.dot_general(
        gate_slopes, gate_weight, contract_last, preferred_element_type=jnp.float32
    ) + lax.dot_general(up_slopes, up_weight, contract_last, preferred_element_type=jnp.float32)
    finished = scatter_sum_rows(
        jnp.concatenate([out_part, in_part], axis=1), "tensor", n_tensor, TENSOR_LINK
    ).astype(jnp.bfloat16)
    return (finished[:, :model_width], finished[:, model_width:])


def solution(mesh):
    in_specs = (
        P(("dp", "tensor"), "pipe"),
        P(("dp", "tensor"), "pipe"),
        P(("dp", "pipe"), "tensor"),
        P(("dp", "pipe"), "tensor"),
        P("pipe", "tensor"),
        P("pipe", "tensor"),
        P("tensor", "pipe"),
    )
    out_specs = (P(("dp", "tensor"), "pipe"), P(("dp", "tensor"), "pipe"))
    return jax.shard_map(
        per_device, mesh=mesh, in_specs=in_specs, out_specs=out_specs, check_vma=False
    )
```

time: 237 us -> 235 us (level)
  blocking collectives: 38.5 us -> 218 us
  waiting for transfers between devices: 117 us -> 0 us
  starting transfers between devices: 46.1 us -> 0 us
  matrix products: 18.5 us -> 7.64 us
  local copies, waits for them, and re-layouts: 6.56 us -> 1.74 us
    all_to_all x0 -> x2, blocking collectives: none -> 122 us  [scatter_sum_rows(): got = lax.all_to_all(sent, axis, 0, 0, tiled=False)]
    all_to_all x7 -> x0, waiting for transfers between devices: 117 us -> none  [the longest x4 72.2 us: scatter_sum_rows(): got = lax.all_to_all(sent, axis, 0, 0, tiled=False)]
    all_to_all x1 -> x2, blocking collectives: 38.5 us -> 95.2 us  [gather_rows(): got = lax.all_to_all(sent, axis, 0, 0, tiled=False)]
    all_to_all x7 -> x0, starting transfers between devices: 46.1 us -> none  [the longest x4 32.8 us: scatter_sum_rows(): got = lax.all_to_all(sent, axis, 0, 0, tiled=False)]
    dot_general x3, matrix products: 10.1 us -> 3.86 us  [the longest x1 1.29 us: per_device(): lax.dot_general(gate_slopes, gate_weight, contract_last, preferred_elemen...]
    broadcast_in_dim x4 -> x2, local copies, waits for them, and re-layouts: 4.64 us -> 0.45 us  [gather_rows(): sent = jnp.broadcast_to(block[None], (count,) + block.shape)]
    dot_general x1, matrix products: 4.06 us -> 1.28 us  [per_device(): lax.dot_general(whole_grad, down_weight, contract_last, preferred_element...]
    reduce_sum x4 -> x2, other arithmetic: 4.81 us -> 4.94 us  [scatter_sum_rows(): return got.astype(jnp.float32).sum(axis=0)]
  transfers between devices with their start and end apart: 7 -> 0, of which waited for: 7 -> 0; matrix products, arithmetic and copies ran while one was open for 10% -> 0% of each run, Pallas kernels for 0% -> 0%
where the time goes in v2:
time: 235 us; the launch traced here: 234 us
  blocking collectives  218 us (93%)
  matrix products  7.64 us (3%)
  other arithmetic  6.7 us (3%)
    all_to_all x2, blocking collectives, scatter_sum_rows(): got = lax.all_to_all(sent, axis, 0, 0, tiled=False)  122 us
    all_to_all x2, blocking collectives, gather_rows(): got = lax.all_to_all(sent, axis, 0, 0, tiled=False)  95.2 us
    reduce_sum x2, other arithmetic, scatter_sum_rows(): return got.astype(jnp.float32).sum(axis=0)  4.94 us

profile of v2, /device:TPU:32, one launch (start us, length us, event | category | flops | bytes accessed | tf_op | source)
XLA Modules:
  0.0 234.4 jit_solution(9557581329703833652)
XLA Ops:
  0.6 0.0 copy-start
  0.6 1.0 pad_maximum_fusion.3
  1.7 0.2 broadcast_in_dim.4
  1.9 61.0 %all_to_all.20 = bf16[16,32,2048]{2,1,0:T(8,128)(2,1)S(1)} all-to-all(bf16[16,32,2048]{2,1,0:T(8,128)(2,1)S(1)} %broadcast_in_dim.4), channel_id=1, replica_groups=mesh['dp'=2,'pipe'=8,'tensor'=16] {'tensor'}, dimensions={0} | all-to-all | bytes 4194304 | tf_op jit(solution)/shard_map/all_to_all | solution.py:23
  62.9 1.3 fusion.2
  64.2 0.0 copy-start.3
  64.2 1.3 fusion
  65.5 0.2 copy-done.3
  65.7 1.2 fusion.4
  67.0 0.4 pad_maximum_fusion
  67.3 66.1 %all_to_all.21 = f32[8,64,2688]{2,1,0:T(8,128)} all-to-all(f32[8,64,2688]{2,1,0:T(8,128)S(1)} %bitcast.10), channel_id=1, replica_groups=mesh['dp'=2,'pipe'=8,'tensor'=16] {'pipe'}, dimensions={0} | all-to-all | bytes 11010048 | tf_op jit(solution)/shard_map/all_to_all | solution.py:30
  133.4 3.0 %reduce_sum.21 = f32[64,2688]{1,0:T(8,128)S(1)} reduce(f32[8,64,2688]{2,1,0:T(8,128)} %all_to_all.21, f32[]{:T(128)} %constant.2.clone.1), dimensions={0}, to_apply=%region_0.0 | reduce | flops 1204224 | bytes 6193156 | tf_op jit(solution)/shard_map/reduce_sum | solution.py:31
  136.4 0.2 fusion.15
  136.6 0.2 broadcast_in_dim.5
  136.8 34.2 %all_to_all.22 = bf16[8,64,2688]{2,1,0:T(8,128)(2,1)S(1)} all-to-all(bf16[8,64,2688]{2,1,0:T(8,128)(2,1)S(1)} %broadcast_in_dim.5), channel_id=1, replica_groups=mesh['dp'=2,'pipe'=8,'tensor'=16] {'pipe'}, dimensions={0} | all-to-all | bytes 5505024 | tf_op jit(solution)/shard_map/all_to_all | solution.py:23
  171.0 1.3 convolution_convert_fusion
  172.3 0.2 copy-done.4
  172.5 1.3 fusion.7
  173.8 0.2 copy-done.6
  174.0 1.3 add_convert_fusion
  175.3 0.2 pad_maximum_fusion.1
  175.5 56.3 %all_to_all.23 = bf16[16,32,2048]{2,1,0:T(8,128)(2,1)} all-to-all(bf16[16,32,2048]{2,1,0:T(8,128)(2,1)S(1)} %bitcast.11), channel_id=1, replica_groups=mesh['dp'=2,'pipe'=8,'tensor'=16] {'tensor'}, dimensions={0} | all-to-all | bytes 4194304 | tf_op jit(solution)/shard_map/all_to_all | solution.py:30
  231.8 2.0 reduce_sum.22
  233.8 0.7 fusion.19
  (10 shorter events, 0.0 us)
Async XLA Ops:
  0.6 63.6 %copy-start = (bf16[896,1024]{1,0:T(8,128)(2,1)S(1)}, bf16[896,1024]{1,0:T(8,128)(2,1)}, u32[]{:S(2)}) copy-start(bf16[896,1024]{1,0:T(8,128)(2,1)} %param.13) | copy-start | bytes 5505028
  1.9 61.0 %copy-start.5 = (bf16[1024,896]{1,0:T(8,128)(2,1)S(1)}, bf16[1024,896]{1,0:T(8,128)(2,1)}, u32[]{:S(2)}) copy-start(bf16[1024,896]{1,0:T(8,128)(2,1)} %param.12) | copy-start | bytes 5505028
  64.2 1.5 copy-start.3
  133.4 3.0 %copy-start.1 = (bf16[64,896]{1,0:T(8,128)(2,1)S(1)}, bf16[64,896]{1,0:T(8,128)(2,1)}, u32[]{:S(2)}) copy-start(bf16[64,896]{1,0:T(8,128)(2,1)} %param.9) | copy-start | bytes 344068
  133.4 3.0 %copy-start.2 = (bf16[64,896]{1,0:T(8,128)(2,1)S(1)}, bf16[64,896]{1,0:T(8,128)(2,1)}, u32[]{:S(2)}) copy-start(bf16[64,896]{1,0:T(8,128)(2,1)} %param.10) | copy-start | bytes 344068
  171.0 1.5 copy-start.4
  172.5 1.5 copy-start.6

commit v3 on v2

--- a/solution.py
+++ b/solution.py
@@ -31,6 +31,38 @@
     return got.astype(jnp.float32).sum(axis=0)
 
 
+def ring_gather_tensor(first, second, count):
+    ring = count // 2
+    me = lax.axis_index("tensor")
+    z = me % ring
+    high = me // ring
+    swap = [(h * ring + k, (1 - h) * ring + k) for h in range(2) for k in range(ring)]
+    up = [(h * ring + k, h * ring + (k + 1) % ring) for h in range(2) for k in range(ring)]
+    down = [(h * ring + k, h * ring + (k - 1) % ring) for h in range(2) for k in range(ring)]
+    mine = jnp.stack([first, second])
+    theirs = lax.ppermute(mine, "tensor", swap)
+    pair = jnp.where(high == 0, jnp.stack([mine, theirs]), jnp.stack([theirs, mine]))
+    rows, width = first.shape
+    out_first = jnp.zeros((2, ring, rows, width), first.dtype)
+    out_second = jnp.zeros((2, ring, rows, width), second.dtype)
+    going_up = pair[:, 0]
+    going_down = pair[:, 1]
+    zero = jnp.int32(0)
+    for step in range(ring):
+        if step > 0:
+            going_up = lax.ppermute(going_up, "tensor", up)
+            going_down = lax.ppermute(going_down, "tensor", down)
+        src_up = (z - step) % ring
+        src_down = (z + step) % ring
+        out_first = lax.dynamic_update_slice(out_first, going_up[:, None], (zero, src_up, zero, zero))
+        out_second = lax.dynamic_update_slice(
+            out_second, going_down[:, None], (zero, src_down, zero, zero)
+        )
+    return jnp.concatenate(
+        [out_first.reshape(count * rows, width), out_second.reshape(count * rows, width)], axis=1
+    )
+
+
 def per_device(
     forward_acts, backward_grad, stored_gate, stored_up, gate_weight, up_weight, down_weight
 ):
@@ -40,7 +72,7 @@
     model_width = forward_acts.shape[1]
     contract_last = (((1,), (1,)), ((), ()))
 
-    both = gather_rows(jnp.concatenate([forward_acts, backward_grad], axis=1), "tensor", n_tensor)
+    both = ring_gather_tensor(forward_acts, backward_grad, n_tensor)
     whole_acts = both[:, :model_width]
     whole_grad = both[:, model_width:]
 

time: 235 us -> 208 us (0.89)
  blocking collectives: 218 us -> 139 us
  waiting for transfers between devices: 0 us -> 30.4 us
  starting transfers between devices: 0 us -> 20.9 us
    all_to_all x2 -> x1, blocking collectives: 95.2 us -> 27.8 us  [gather_rows(): got = lax.all_to_all(sent, axis, 0, 0, tiled=False)]
    ppermute x0 -> x15, waiting for transfers between devices: none -> 30.4 us  [the longest x7 22.2 us: ring_gather_tensor(): going_up = lax.ppermute(going_up, 'tensor', up)]
    ppermute x0 -> x15, starting transfers between devices: none -> 20.9 us  [the longest x7 13 us: ring_gather_tensor(): going_down = lax.ppermute(going_down, 'tensor', down)]
    all_to_all x2, blocking collectives: 122 us -> 111 us  [scatter_sum_rows(): got = lax.all_to_all(sent, axis, 0, 0, tiled=False)]
  transfers between devices with their start and end apart: 0 -> 15, of which waited for: 0 -> 13; matrix products, arithmetic and copies ran while one was open for 0% -> 1% of each run, Pallas kernels for 0% -> 0%
where the time goes in v3:
time: 208 us
  blocking collectives  139 us (67%)
  waiting for transfers between devices  30.4 us (15%)
  starting transfers between devices  20.9 us (10%)
  matrix products  7.61 us (4%)
  other arithmetic  6.73 us (3%)
  local copies, waits for them, and re-layouts  2.25 us (1%)
    all_to_all x2, blocking collectives, scatter_sum_rows(): got = lax.all_to_all(sent, axis, 0, 0, tiled=False)  111 us
    all_to_all x1, blocking collectives, gather_rows(): got = lax.all_to_all(sent, axis, 0, 0, tiled=False)  27.8 us
    ppermute x7, waiting for transfers between devices, ring_gather_tensor(): going_up = lax.ppermute(going_up, 'tensor', up)  22.2 us
    ppermute x7, starting transfers between devices, ring_gather_tensor(): going_down = lax.ppermute(going_down, 'tensor', down)  13 us
    reduce_sum x2, other arithmetic, scatter_sum_rows(): return got.astype(jnp.float32).sum(axis=0)  4.94 us
    ppermute x7, starting transfers between devices, ring_gather_tensor(): going_up = lax.ppermute(going_up, 'tensor', up)  4.86 us
    ppermute x7, waiting for transfers between devices, ring_gather_tensor(): going_down = lax.ppermute(going_down, 'tensor', down)  4.47 us
  transfers between devices with their start and end apart: 15, of which 13 were waited for; matrix products, arithmetic and copies ran while one was open for 1% of the time, Pallas kernels for 0%

profile of v3, /device:TPU:32, one launch (start us, length us, event | category | flops | bytes accessed | tf_op | source)
XLA Modules:
  0.0 207.7 jit_solution(3978069480686497800)
XLA Ops:
  1.7 3.1 %collective-permute-start = (bf16[2,32,1024]{2,1,0:T(8,128)(2,1)S(1)}, bf16[2,32,1024]{2,1,0:T(8,128)(2,1)S(1)}, u32[]{:S(2)}, u32[]{:S(2)}) collective-permute-start(bf16[2,32,1024]{2,1,0:T(8,128)(2,1)S(1)} %get-tuple-element.11), channel_id=1, source_target_pairs={{0,8},{1,9},{2,10},{3,11},{4,12},{5,13},{6,14},{7,15},{8,0},{9,1},... | collective-permute-start | bytes 393224 | tf_op jit(solution)/shard_map/ppermute | solution.py:43
  4.8 3.7 %collective-permute-done = bf16[2,32,1024]{2,1,0:T(8,128)(2,1)S(1)} collective-permute-done((bf16[2,32,1024]{2,1,0:T(8,128)(2,1)S(1)}, bf16[2,32,1024]{2,1,0:T(8,128)(2,1)S(1)}, u32[]{:S(2)}, u32[]{:S(2)}) %collective-permute-start) | collective-permute-done | bytes 131104 | tf_op jit(solution)/shard_map/ppermute | solution.py:43
  8.7 2.0 collective-permute-start.1
  10.9 2.8 %collective-permute-done.1 = bf16[2,32,1024]{2,1,0:T(8,128)(2,1)S(1)} collective-permute-done((bf16[2,32,1024]{2,1,0:T(8,128)(2,1)S(1)}, bf16[2,32,1024]{2,1,0:T(8,128)(2,1)S(1)}, u32[]{:S(2)}, u32[]{:S(2)}) %collective-permute-start.1) | collective-permute-done | bytes 131104 | tf_op jit(solution)/shard_map/ppermute | solution.py:53
  13.7 1.9 collective-permute-start.2
  15.7 2.0 collective-permute-start.9
  17.7 2.9 %collective-permute-done.2 = bf16[2,32,1024]{2,1,0:T(8,128)(2,1)S(1)} collective-permute-done((bf16[2,32,1024]{2,1,0:T(8,128)(2,1)S(1)}, bf16[2,32,1024]{2,1,0:T(8,128)(2,1)S(1)}, u32[]{:S(2)}, u32[]{:S(2)}) %collective-permute-start.2) | collective-permute-done | bytes 131104 | tf_op jit(solution)/shard_map/ppermute | solution.py:53
  21.6 2.2 %collective-permute-start.10 = (bf16[2,32,1024]{2,1,0:T(8,128)(2,1)S(1)}, bf16[2,32,1024]{2,1,0:T(8,128)(2,1)S(1)}, u32[]{:S(2)}, u32[]{:S(2)}) collective-permute-start(bf16[2,32,1024]{2,1,0:T(8,128)(2,1)S(1)} %collective-permute-done.9), channel_id=1, source_target_pairs={{0,7},{1,0},{2,1},{3,2},{4,3},{5,4},{6,5},{7,6},{8,15},{9,8},{10,9... | collective-permute-start | bytes 393224 | tf_op jit(solution)/shard_map/ppermute | solution.py:54
  23.9 3.0 %collective-permute-done.3 = bf16[2,32,1024]{2,1,0:T(8,128)(2,1)S(1)} collective-permute-done((bf16[2,32,1024]{2,1,0:T(8,128)(2,1)S(1)}, bf16[2,32,1024]{2,1,0:T(8,128)(2,1)S(1)}, u32[]{:S(2)}, u32[]{:S(2)}) %collective-permute-start.3) | collective-permute-done | bytes 131104 | tf_op jit(solution)/shard_map/ppermute | solution.py:53
  28.2 2.2 %collective-permute-start.11 = (bf16[2,32,1024]{2,1,0:T(8,128)(2,1)S(1)}, bf16[2,32,1024]{2,1,0:T(8,128)(2,1)S(1)}, u32[]{:S(2)}, u32[]{:S(2)}) collective-permute-start(bf16[2,32,1024]{2,1,0:T(8,128)(2,1)S(1)} %collective-permute-done.10), channel_id=1, source_target_pairs={{0,7},{1,0},{2,1},{3,2},{4,3},{5,4},{6,5},{7,6},{8,15},{9,8},{10,9... | collective-permute-start | bytes 393224 | tf_op jit(solution)/shard_map/ppermute | solution.py:54
  30.5 4.2 %collective-permute-done.4 = bf16[2,32,1024]{2,1,0:T(8,128)(2,1)S(1)} collective-permute-done((bf16[2,32,1024]{2,1,0:T(8,128)(2,1)S(1)}, bf16[2,32,1024]{2,1,0:T(8,128)(2,1)S(1)}, u32[]{:S(2)}, u32[]{:S(2)}) %collective-permute-start.4) | collective-permute-done | bytes 131104 | tf_op jit(solution)/shard_map/ppermute | solution.py:53
  36.0 1.9 collective-permute-start.12
  37.9 3.6 %collective-permute-done.5 = bf16[2,32,1024]{2,1,0:T(8,128)(2,1)S(1)} collective-permute-done((bf16[2,32,1024]{2,1,0:T(8,128)(2,1)S(1)}, bf16[2,32,1024]{2,1,0:T(8,128)(2,1)S(1)}, u32[]{:S(2)}, u32[]{:S(2)}) %collective-permute-start.5) | collective-permute-done | bytes 131104 | tf_op jit(solution)/shard_map/ppermute | solution.py:53
  42.5 2.0 collective-permute-start.13
  44.5 2.9 %collective-permute-done.6 = bf16[2,32,1024]{2,1,0:T(8,128)(2,1)S(1)} collective-permute-done((bf16[2,32,1024]{2,1,0:T(8,128)(2,1)S(1)}, bf16[2,32,1024]{2,1,0:T(8,128)(2,1)S(1)}, u32[]{:S(2)}, u32[]{:S(2)}) %collective-permute-start.6) | collective-permute-done | bytes 131104 | tf_op jit(solution)/shard_map/ppermute | solution.py:53
  48.2 2.5 %collective-permute-start.14 = (bf16[2,32,1024]{2,1,0:T(8,128)(2,1)S(1)}, bf16[2,32,1024]{2,1,0:T(8,128)(2,1)S(1)}, u32[]{:S(2)}, u32[]{:S(2)}) collective-permute-start(bf16[2,32,1024]{2,1,0:T(8,128)(2,1)S(1)} %collective-permute-done.13), channel_id=1, source_target_pairs={{0,7},{1,0},{2,1},{3,2},{4,3},{5,4},{6,5},{7,6},{8,15},{9,8},{10,9... | collective-permute-start | bytes 393224 | tf_op jit(solution)/shard_map/ppermute | solution.py:54
  50.7 2.9 %collective-permute-done.7 = bf16[2,32,1024]{2,1,0:T(8,128)(2,1)S(1)} collective-permute-done((bf16[2,32,1024]{2,1,0:T(8,128)(2,1)S(1)}, bf16[2,32,1024]{2,1,0:T(8,128)(2,1)S(1)}, u32[]{:S(2)}, u32[]{:S(2)}) %collective-permute-start.7) | collective-permute-done | bytes 131104 | tf_op jit(solution)/shard_map/ppermute | solution.py:53
  56.6 1.3 fusion.17
  58.3 61.0 %all_to_all.15 = f32[8,64,2688]{2,1,0:T(8,128)} all-to-all(f32[8,64,2688]{2,1,0:T(8,128)S(1)} %bitcast.79), channel_id=1, replica_groups=mesh['dp'=2,'pipe'=8,'tensor'=16] {'pipe'}, dimensions={0} | all-to-all | bytes 11010048 | tf_op jit(solution)/shard_map/all_to_all | solution.py:30
  119.2 3.0 %reduce_sum.21 = f32[64,2688]{1,0:T(8,128)S(1)} reduce(f32[8,64,2688]{2,1,0:T(8,128)} %all_to_all.15, f32[]{:T(128)} %constant.124.clone.1), dimensions={0}, to_apply=%region_0.1 | reduce | flops 1204224 | bytes 6193156 | tf_op jit(solution)/shard_map/reduce_sum | solution.py:31
  122.7 27.8 %all_to_all.16 = bf16[8,64,2688]{2,1,0:T(8,128)(2,1)S(1)} all-to-all(bf16[8,64,2688]{2,1,0:T(8,128)(2,1)S(1)} %broadcast_in_dim.62), channel_id=1, replica_groups=mesh['dp'=2,'pipe'=8,'tensor'=16] {'pipe'}, dimensions={0} | all-to-all | bytes 5505024 | tf_op jit(solution)/shard_map/all_to_all | solution.py:23
  153.5 1.3 add_convert_fusion
  155.0 50.1 %all_to_all.17 = bf16[16,32,2048]{2,1,0:T(8,128)(2,1)} all-to-all(bf16[16,32,2048]{2,1,0:T(8,128)(2,1)S(1)} %bitcast.80), channel_id=1, replica_groups=mesh['dp'=2,'pipe'=8,'tensor'=16] {'tensor'}, dimensions={0} | all-to-all | bytes 4194304 | tf_op jit(solution)/shard_map/all_to_all | solution.py:30
  205.1 2.0 reduce_sum.22
  (57 shorter events, 14.6 us)
Async XLA Ops:
  0.6 53.0 %copy-start = (bf16[1024,896]{1,0:T(8,128)(2,1)S(1)}, bf16[1024,896]{1,0:T(8,128)(2,1)}, u32[]{:S(2)}) copy-start(bf16[1024,896]{1,0:T(8,128)(2,1)} %param.11) | copy-start | bytes 5505028
  1.7 6.8 %collective-permute-start = (bf16[2,32,1024]{2,1,0:T(8,128)(2,1)S(1)}, bf16[2,32,1024]{2,1,0:T(8,128)(2,1)S(1)}, u32[]{:S(2)}, u32[]{:S(2)}) collective-permute-start(bf16[2,32,1024]{2,1,0:T(8,128)(2,1)S(1)} %get-tuple-element.11), channel_id=1, source_target_pairs={{0,8},{1,9},{2,10},{3,11},{4,12},{5,13},{6,14},{7,15},{8,0},{9,1},... | collective-permute-start | bytes 393224 | tf_op jit(solution)/shard_map/ppermute | solution.py:43
  8.7 5.0 %collective-permute-start.1 = (bf16[2,32,1024]{2,1,0:T(8,128)(2,1)S(1)}, bf16[2,32,1024]{2,1,0:T(8,128)(2,1)S(1)}, u32[]{:S(2)}, u32[]{:S(2)}) collective-permute-start(bf16[2,32,1024]{2,1,0:T(8,128)(2,1)S(1)} %get-tuple-element.5), channel_id=1, source_target_pairs={{0,1},{1,2},{2,3},{3,4},{4,5},{5,6},{6,7},{7,0},{8,9},{9,10},{10,1... | collective-permute-start | bytes 393224 | tf_op jit(solution)/shard_map/ppermute | solution.py:53
  10.7 5.0 %collective-permute-start.8 = (bf16[2,32,1024]{2,1,0:T(8,128)(2,1)S(1)}, bf16[2,32,1024]{2,1,0:T(8,128)(2,1)S(1)}, u32[]{:S(2)}, u32[]{:S(2)}) collective-permute-start(bf16[2,32,1024]{2,1,0:T(8,128)(2,1)S(1)} %get-tuple-element.6), channel_id=1, source_target_pairs={{0,7},{1,0},{2,1},{3,2},{4,3},{5,4},{6,5},{7,6},{8,15},{9,8},{10,9... | collective-permute-start | bytes 393224 | tf_op jit(solution)/shard_map/ppermute | solution.py:54
  13.7 6.9 %collective-permute-start.2 = (bf16[2,32,1024]{2,1,0:T(8,128)(2,1)S(1)}, bf16[2,32,1024]{2,1,0:T(8,128)(2,1)S(1)}, u32[]{:S(2)}, u32[]{:S(2)}) collective-permute-start(bf16[2,32,1024]{2,1,0:T(8,128)(2,1)S(1)} %collective-permute-done.1), channel_id=1, source_target_pairs={{0,1},{1,2},{2,3},{3,4},{4,5},{5,6},{6,7},{7,0},{8,9},{9,10},{10,1... | collective-permute-start | bytes 393224 | tf_op jit(solution)/shard_map/ppermute | solution.py:53
  15.7 6.0 %collective-permute-start.9 = (bf16[2,32,1024]{2,1,0:T(8,128)(2,1)S(1)}, bf16[2,32,1024]{2,1,0:T(8,128)(2,1)S(1)}, u32[]{:S(2)}, u32[]{:S(2)}) collective-permute-start(bf16[2,32,1024]{2,1,0:T(8,128)(2,1)S(1)} %collective-permute-done.8), channel_id=1, source_target_pairs={{0,7},{1,0},{2,1},{3,2},{4,3},{5,4},{6,5},{7,6},{8,15},{9,8},{10,9... | collective-permute-start | bytes 393224 | tf_op jit(solution)/shard_map/ppermute | solution.py:54
  20.6 6.3 %collective-permute-start.3 = (bf16[2,32,1024]{2,1,0:T(8,128)(2,1)S(1)}, bf16[2,32,1024]{2,1,0:T(8,128)(2,1)S(1)}, u32[]{:S(2)}, u32[]{:S(2)}) collective-permute-start(bf16[2,32,1024]{2,1,0:T(8,128)(2,1)S(1)} %collective-permute-done.2), channel_id=1, source_target_pairs={{0,1},{1,2},{2,3},{3,4},{4,5},{5,6},{6,7},{7,0},{8,9},{9,10},{10,1... | collective-permute-start | bytes 393224 | tf_op jit(solution)/shard_map/ppermute | solution.py:53
  21.6 6.6 %collective-permute-start.10 = (bf16[2,32,1024]{2,1,0:T(8,128)(2,1)S(1)}, bf16[2,32,1024]{2,1,0:T(8,128)(2,1)S(1)}, u32[]{:S(2)}, u32[]{:S(2)}) collective-permute-start(bf16[2,32,1024]{2,1,0:T(8,128)(2,1)S(1)} %collective-permute-done.9), channel_id=1, source_target_pairs={{0,7},{1,0},{2,1},{3,2},{4,3},{5,4},{6,5},{7,6},{8,15},{9,8},{10,9... | collective-permute-start | bytes 393224 | tf_op jit(solution)/shard_map/ppermute | solution.py:54
  26.9 7.8 %collective-permute-start.4 = (bf16[2,32,1024]{2,1,0:T(8,128)(2,1)S(1)}, bf16[2,32,1024]{2,1,0:T(8,128)(2,1)S(1)}, u32[]{:S(2)}, u32[]{:S(2)}) collective-permute-start(bf16[2,32,1024]{2,1,0:T(8,128)(2,1)S(1)} %collective-permute-done.3), channel_id=1, source_target_pairs={{0,1},{1,2},{2,3},{3,4},{4,5},{5,6},{6,7},{7,0},{8,9},{9,10},{10,1... | collective-permute-start | bytes 393224 | tf_op jit(solution)/shard_map/ppermute | solution.py:53
  28.2 7.8 %collective-permute-start.11 = (bf16[2,32,1024]{2,1,0:T(8,128)(2,1)S(1)}, bf16[2,32,1024]{2,1,0:T(8,128)(2,1)S(1)}, u32[]{:S(2)}, u32[]{:S(2)}) collective-permute-start(bf16[2,32,1024]{2,1,0:T(8,128)(2,1)S(1)} %collective-permute-done.10), channel_id=1, source_target_pairs={{0,7},{1,0},{2,1},{3,2},{4,3},{5,4},{6,5},{7,6},{8,15},{9,8},{10,9... | collective-permute-start | bytes 393224 | tf_op jit(solution)/shard_map/ppermute | solution.py:54
  34.7 6.9 %collective-permute-start.5 = (bf16[2,32,1024]{2,1,0:T(8,128)(2,1)S(1)}, bf16[2,32,1024]{2,1,0:T(8,128)(2,1)S(1)}, u32[]{:S(2)}, u32[]{:S(2)}) collective-permute-start(bf16[2,32,1024]{2,1,0:T(8,128)(2,1)S(1)} %collective-permute-done.4), channel_id=1, source_target_pairs={{0,1},{1,2},{2,3},{3,4},{4,5},{5,6},{6,7},{7,0},{8,9},{9,10},{10,1... | collective-permute-start | bytes 393224 | tf_op jit(solution)/shard_map/ppermute | solution.py:53
  36.0 6.5 %collective-permute-start.12 = (bf16[2,32,1024]{2,1,0:T(8,128)(2,1)S(1)}, bf16[2,32,1024]{2,1,0:T(8,128)(2,1)S(1)}, u32[]{:S(2)}, u32[]{:S(2)}) collective-permute-start(bf16[2,32,1024]{2,1,0:T(8,128)(2,1)S(1)} %collective-permute-done.11), channel_id=1, source_target_pairs={{0,7},{1,0},{2,1},{3,2},{4,3},{5,4},{6,5},{7,6},{8,15},{9,8},{10,9... | collective-permute-start | bytes 393224 | tf_op jit(solution)/shard_map/ppermute | solution.py:54
  41.5 5.9 %collective-permute-start.6 = (bf16[2,32,1024]{2,1,0:T(8,128)(2,1)S(1)}, bf16[2,32,1024]{2,1,0:T(8,128)(2,1)S(1)}, u32[]{:S(2)}, u32[]{:S(2)}) collective-permute-start(bf16[2,32,1024]{2,1,0:T(8,128)(2,1)S(1)} %collective-permute-done.5), channel_id=1, source_target_pairs={{0,1},{1,2},{2,3},{3,4},{4,5},{5,6},{6,7},{7,0},{8,9},{9,10},{10,1... | collective-permute-start | bytes 393224 | tf_op jit(solution)/shard_map/ppermute | solution.py:53
  42.5 5.7 %collective-permute-start.13 = (bf16[2,32,1024]{2,1,0:T(8,128)(2,1)S(1)}, bf16[2,32,1024]{2,1,0:T(8,128)(2,1)S(1)}, u32[]{:S(2)}, u32[]{:S(2)}) collective-permute-start(bf16[2,32,1024]{2,1,0:T(8,128)(2,1)S(1)} %collective-permute-done.12), channel_id=1, source_target_pairs={{0,7},{1,0},{2,1},{3,2},{4,3},{5,4},{6,5},{7,6},{8,15},{9,8},{10,9... | collective-permute-start | bytes 393224 | tf_op jit(solution)/shard_map/ppermute | solution.py:54
  47.4 6.2 %collective-permute-start.7 = (bf16[2,32,1024]{2,1,0:T(8,128)(2,1)S(1)}, bf16[2,32,1024]{2,1,0:T(8,128)(2,1)S(1)}, u32[]{:S(2)}, u32[]{:S(2)}) collective-permute-start(bf16[2,32,1024]{2,1,0:T(8,128)(2,1)S(1)} %collective-permute-done.6), channel_id=1, source_target_pairs={{0,1},{1,2},{2,3},{3,4},{4,5},{5,6},{6,7},{7,0},{8,9},{9,10},{10,1... | collective-permute-start | bytes 393224 | tf_op jit(solution)/shard_map/ppermute | solution.py:53
  48.2 8.2 %collective-permute-start.14 = (bf16[2,32,1024]{2,1,0:T(8,128)(2,1)S(1)}, bf16[2,32,1024]{2,1,0:T(8,128)(2,1)S(1)}, u32[]{:S(2)}, u32[]{:S(2)}) collective-permute-start(bf16[2,32,1024]{2,1,0:T(8,128)(2,1)S(1)} %collective-permute-done.13), channel_id=1, source_target_pairs={{0,7},{1,0},{2,1},{3,2},{4,3},{5,4},{6,5},{7,6},{8,15},{9,8},{10,9... | collective-permute-start | bytes 393224 | tf_op jit(solution)/shard_map/ppermute | solution.py:54
  53.6 1.5 copy-start.5
  55.1 1.5 copy-start.3
  119.2 3.0 %copy-start.1 = (bf16[64,896]{1,0:T(8,128)(2,1)S(1)}, bf16[64,896]{1,0:T(8,128)(2,1)}, u32[]{:S(2)}) copy-start(bf16[64,896]{1,0:T(8,128)(2,1)} %param.9) | copy-start | bytes 344068
  119.2 3.0 %copy-start.2 = (bf16[64,896]{1,0:T(8,128)(2,1)S(1)}, bf16[64,896]{1,0:T(8,128)(2,1)}, u32[]{:S(2)}) copy-start(bf16[64,896]{1,0:T(8,128)(2,1)} %param.10) | copy-start | bytes 344068
  150.5 1.5 copy-start.4
  152.0 1.5 copy-start.6

commit v4 on v2

--- a/solution.py
+++ b/solution.py
@@ -1,10 +1,15 @@
+import functools
+
 import jax
 import jax.numpy as jnp
 from jax import lax
+from jax.experimental import pallas as pl
+from jax.experimental.pallas import tpu as pltpu
 from jax.sharding import PartitionSpec as P
 
 PIPE_LINK = jnp.float32
 TENSOR_LINK = jnp.bfloat16
+MESH = pl.DeviceIdType.MESH
 
 
 def make_slopes(hidden_grad, gate_vals, up_vals):
@@ -31,6 +36,84 @@
     return got.astype(jnp.float32).sum(axis=0)
 
 
+def _ring_gather_kernel(axis, outer, inner, ring_on_inner, x_ref, first_ref, second_ref, send_sems, recv_sems, local_sems):
+    me = lax.axis_index(axis)
+    o = me // inner
+    i = me % inner
+    if ring_on_inner:
+        ring = inner
+        pos, other = i, o
+        def at(p, q):
+            return q * inner + p
+    else:
+        ring = outer
+        pos, other = o, i
+        def at(p, q):
+            return p * inner + q
+    partner = at(pos, 1 - other)
+    up = at(lax.rem(pos + 1, ring), other)
+    down = at(lax.rem(pos + ring - 1, ring), other)
+
+    barrier = pltpu.get_barrier_semaphore()
+    for peer in (partner, up, down):
+        pl.semaphore_signal(barrier, inc=1, device_id={axis: peer}, device_id_type=MESH)
+    pl.semaphore_wait(barrier, 3)
+
+    own_first = pltpu.make_async_copy(x_ref.at[0], first_ref.at[other, pos], local_sems.at[0])
+    own_second = pltpu.make_async_copy(x_ref.at[1], second_ref.at[other, pos], local_sems.at[1])
+    own_first.start()
+    own_second.start()
+    swap_first = pltpu.make_async_remote_copy(
+        src_ref=x_ref.at[0], dst_ref=first_ref.at[other, pos],
+        send_sem=send_sems.at[0], recv_sem=recv_sems.at[0],
+        device_id={axis: partner}, device_id_type=MESH)
+    swap_second = pltpu.make_async_remote_copy(
+        src_ref=x_ref.at[1], dst_ref=second_ref.at[other, pos],
+        send_sem=send_sems.at[1], recv_sem=recv_sems.at[1],
+        device_id={axis: partner}, device_id_type=MESH)
+    swap_first.start()
+    swap_second.start()
+    own_first.wait()
+    own_second.wait()
+    swap_first.wait()
+    swap_second.wait()
+
+    for step in range(1, ring):
+        src_up = lax.rem(pos - step + 1 + ring, ring)
+        src_down = lax.rem(pos + step - 1, ring)
+        go_up = pltpu.make_async_remote_copy(
+            src_ref=first_ref.at[:, src_up], dst_ref=first_ref.at[:, src_up],
+            send_sem=send_sems.at[2 * step], recv_sem=recv_sems.at[2 * step],
+            device_id={axis: up}, device_id_type=MESH)
+        go_down = pltpu.make_async_remote_copy(
+            src_ref=second_ref.at[:, src_down], dst_ref=second_ref.at[:, src_down],
+            send_sem=send_sems.at[2 * step + 1], recv_sem=recv_sems.at[2 * step + 1],
+            device_id={axis: down}, device_id_type=MESH)
+        go_up.start()
+        go_down.start()
+        go_up.wait()
+        go_down.wait()
+
+
+def ring_gather(first, second, axis, outer, inner, ring_on_inner, cid):
+    rows, width = first.shape
+    ring = inner if ring_on_inner else outer
+    shape = (2, ring, rows, width)
+    x = jnp.stack([first, second])
+    f, s = pl.pallas_call(
+        functools.partial(_ring_gather_kernel, axis, outer, inner, ring_on_inner),
+        out_shape=(jax.ShapeDtypeStruct(shape, first.dtype), jax.ShapeDtypeStruct(shape, second.dtype)),
+        in_specs=[pl.BlockSpec(memory_space=pltpu.VMEM)],
+        out_specs=(pl.BlockSpec(memory_space=pltpu.VMEM), pl.BlockSpec(memory_space=pltpu.VMEM)),
+        scratch_shapes=[pltpu.SemaphoreType.DMA((2 * ring,)), pltpu.SemaphoreType.DMA((2 * ring,)), pltpu.SemaphoreType.DMA((2,))],
+        compiler_params=pltpu.CompilerParams(collective_id=cid, has_side_effects=True),
+    )(x)
+    if ring_on_inner:
+        return f.reshape(2 * ring * rows, width), s.reshape(2 * ring * rows, width)
+    return (f.transpose(1, 0, 2, 3).reshape(2 * ring * rows, width),
+            s.transpose(1, 0, 2, 3).reshape(2 * ring * rows, width))
+
+
 def per_device(
     forward_acts, backward_grad, stored_gate, stored_up, gate_weight, up_weight, down_weight
 ):
@@ -40,9 +123,9 @@
     model_width = forward_acts.shape[1]
     contract_last = (((1,), (1,)), ((), ()))
 
-    both = gather_rows(jnp.concatenate([forward_acts, backward_grad], axis=1), "tensor", n_tensor)
-    whole_acts = both[:, :model_width]
-    whole_grad = both[:, model_width:]
+    whole_acts, whole_grad = ring_gather(
+        forward_acts, backward_grad, "tensor", 2, n_tensor // 2, True, 0
+    )
 
     gate_part = jnp.dot(whole_acts, gate_weight, preferred_element_type=jnp.float32)
     up_part = jnp.dot(whole_acts, up_weight, preferred_element_type=jnp.float32)

time: 235 us -> 208 us (0.89)
  blocking collectives: 218 us -> 141 us
  Pallas kernels: 0 us -> 47.6 us
    all_to_all x2 -> x1, blocking collectives: 95.2 us -> 28.7 us  [gather_rows(): got = lax.all_to_all(sent, axis, 0, 0, tiled=False)]
    pallas_call x0 -> x1, Pallas kernels: none -> 47.6 us  [ring_gather(): pl.pallas_call(functools.partial(_ring_gather_kernel, axis, outer, inner,...]
    all_to_all x2, blocking collectives: 122 us -> 112 us  [scatter_sum_rows(): got = lax.all_to_all(sent, axis, 0, 0, tiled=False)]
where the time goes in v4:
time: 208 us; the launch traced here: 207 us
  blocking collectives  141 us (68%)
  Pallas kernels  47.6 us (23%)
  matrix products  9.63 us (5%)
  other arithmetic  7.35 us (4%)
    all_to_all x2, blocking collectives, scatter_sum_rows(): got = lax.all_to_all(sent, axis, 0, 0, tiled=False)  112 us
    pallas_call x1, Pallas kernels, ring_gather(): pl.pallas_call(functools.partial(_ring_gather_kernel, axis, outer, inner,...  47.6 us
    all_to_all x1, blocking collectives, gather_rows(): got = lax.all_to_all(sent, axis, 0, 0, tiled=False)  28.7 us
    reduce_sum x2, other arithmetic, scatter_sum_rows(): return got.astype(jnp.float32).sum(axis=0)  4.94 us

profile of v4, /device:TPU:32, one launch (start us, length us, event | category | flops | bytes accessed | tf_op | source)
XLA Modules:
  0.0 207.4 jit_solution(278691205103348623)
XLA Ops:
  0.6 0.0 copy-start
  0.6 1.7 pad_maximum_fusion.3.x_ref
  2.3 47.6 %shard_map.86 = (bf16[2,8,32,1024]{3,2,1,0:T(8,128)(2,1)}, bf16[2,8,32,1024]{3,2,1,0:T(8,128)(2,1)}) custom-call(bf16[2,32,1024]{2,1,0:T(8,128)(2,1)} %pad_maximum_fusion.3.x_ref), custom_call_target="tpu_custom_call" | custom-call | tf_op jit(solution)/shard_map/pallas_call | solution.py:103
  50.0 0.0 copy-start.3
  50.0 3.2 %fusion.15 = f32[512,896]{1,0:T(8,128)S(1)} fusion(bf16[512,1024]{1,0:T(8,128)(2,1)} %bitcast.24, bf16[1024,896]{1,0:T(8,128)(2,1)} %param.12), kind=kOutput, calls=%fused_computation.25 | convolution fusion | flops 939524096 | bytes 4718592 | tf_op jit(solution)/shard_map/dot_general | solution.py:131
  53.2 0.0 copy-done.3
  53.2 0.0 copy-done.7
  53.2 1.2 fusion.14
  54.5 1.3 fusion.16
  55.8 0.4 pad_maximum_fusion
  56.2 62.2 %all_to_all.15 = f32[8,64,2688]{2,1,0:T(8,128)} all-to-all(f32[8,64,2688]{2,1,0:T(8,128)S(1)} %bitcast.16), channel_id=1, replica_groups=mesh['dp'=2,'pipe'=8,'tensor'=16] {'pipe'}, dimensions={0} | all-to-all | bytes 11010048 | tf_op jit(solution)/shard_map/all_to_all | solution.py:35
  118.4 3.0 %reduce_sum.21 = f32[64,2688]{1,0:T(8,128)S(1)} reduce(f32[8,64,2688]{2,1,0:T(8,128)} %all_to_all.15, f32[]{:T(128)} %constant.2.clone.1), dimensions={0}, to_apply=%region_0.0 | reduce | flops 1204224 | bytes 6193156 | tf_op jit(solution)/shard_map/reduce_sum | solution.py:36
  121.4 0.2 fusion.9
  121.6 0.2 broadcast_in_dim.2
  121.8 28.7 %all_to_all.16 = bf16[8,64,2688]{2,1,0:T(8,128)(2,1)S(1)} all-to-all(bf16[8,64,2688]{2,1,0:T(8,128)(2,1)S(1)} %broadcast_in_dim.2), channel_id=1, replica_groups=mesh['dp'=2,'pipe'=8,'tensor'=16] {'pipe'}, dimensions={0} | all-to-all | bytes 5505024 | tf_op jit(solution)/shard_map/all_to_all | solution.py:28
  150.5 1.3 convolution_convert_fusion
  151.8 0.2 copy-done.4
  152.0 1.3 fusion.1
  153.3 0.2 copy-done.5
  153.5 1.3 add_convert_fusion
  154.9 0.2 pad_maximum_fusion.1
  155.0 49.7 %all_to_all.17 = bf16[16,32,2048]{2,1,0:T(8,128)(2,1)} all-to-all(bf16[16,32,2048]{2,1,0:T(8,128)(2,1)S(1)} %bitcast.17), channel_id=1, replica_groups=mesh['dp'=2,'pipe'=8,'tensor'=16] {'tensor'}, dimensions={0} | all-to-all | bytes 4194304 | tf_op jit(solution)/shard_map/all_to_all | solution.py:35
  204.8 2.0 reduce_sum.22
  206.7 0.7 fusion.13
  (11 shorter events, 0.0 us)
Async XLA Ops:
  0.6 53.9 %copy-start = (bf16[896,1024]{1,0:T(8,128)(2,1)S(1)}, bf16[896,1024]{1,0:T(8,128)(2,1)}, u32[]{:S(2)}) copy-start(bf16[896,1024]{1,0:T(8,128)(2,1)} %param.13) | copy-start | bytes 5505028
  50.0 3.2 %copy-start.3 = (bf16[1024,896]{1,0:T(8,128)(2,1)S(1)}, bf16[1024,896]{1,0:T(8,128)(2,1)}, u32[]{:S(2)}) copy-start(bf16[1024,896]{1,0:T(8,128)(2,1)} %param.11) | copy-start | bytes 5505028
  50.0 3.2 %copy-start.7 = (bf16[2,8,32,1024]{3,2,1,0:T(8,128)(2,1)S(1)}, bf16[2,8,32,1024]{3,2,1,0:T(8,128)(2,1)}, u32[]{:S(2)}) copy-start(bf16[2,8,32,1024]{3,2,1,0:T(8,128)(2,1)} %get-tuple-element.4) | copy-start | bytes 3145732
  53.2 1.3 copy-start.6
  118.4 3.0 %copy-start.1 = (bf16[64,896]{1,0:T(8,128)(2,1)S(1)}, bf16[64,896]{1,0:T(8,128)(2,1)}, u32[]{:S(2)}) copy-start(bf16[64,896]{1,0:T(8,128)(2,1)} %param.9) | copy-start | bytes 344068
  118.4 3.0 %copy-start.2 = (bf16[64,896]{1,0:T(8,128)(2,1)S(1)}, bf16[64,896]{1,0:T(8,128)(2,1)}, u32[]{:S(2)}) copy-start(bf16[64,896]{1,0:T(8,128)(2,1)} %param.10) | copy-start | bytes 344068
  150.5 1.5 copy-start.4
  152.0 1.5 copy-start.5

commit v5 on v4

--- a/solution.py
+++ b/solution.py
@@ -36,7 +36,7 @@
     return got.astype(jnp.float32).sum(axis=0)
 
 
-def _ring_gather_kernel(axis, outer, inner, ring_on_inner, x_ref, first_ref, second_ref, send_sems, recv_sems, local_sems):
+def _ring_gather_kernel(axis, outer, inner, ring_on_inner, halves, x_ref, first_ref, second_ref, send_sems, recv_sems, swap_sems, local_sems):
     me = lax.axis_index(axis)
     o = me // inner
     i = me % inner
@@ -53,59 +53,86 @@
     partner = at(pos, 1 - other)
     up = at(lax.rem(pos + 1, ring), other)
     down = at(lax.rem(pos + ring - 1, ring), other)
+    rows = x_ref.shape[1]
+    part = rows // halves
 
     barrier = pltpu.get_barrier_semaphore()
     for peer in (partner, up, down):
         pl.semaphore_signal(barrier, inc=1, device_id={axis: peer}, device_id_type=MESH)
     pl.semaphore_wait(barrier, 3)
 
-    own_first = pltpu.make_async_copy(x_ref.at[0], first_ref.at[other, pos], local_sems.at[0])
-    own_second = pltpu.make_async_copy(x_ref.at[1], second_ref.at[other, pos], local_sems.at[1])
-    own_first.start()
-    own_second.start()
-    swap_first = pltpu.make_async_remote_copy(
-        src_ref=x_ref.at[0], dst_ref=first_ref.at[other, pos],
-        send_sem=send_sems.at[0], recv_sem=recv_sems.at[0],
-        device_id={axis: partner}, device_id_type=MESH)
-    swap_second = pltpu.make_async_remote_copy(
-        src_ref=x_ref.at[1], dst_ref=second_ref.at[other, pos],
-        send_sem=send_sems.at[1], recv_sem=recv_sems.at[1],
-        device_id={axis: partner}, device_id_type=MESH)
-    swap_first.start()
-    swap_second.start()
-    own_first.wait()
-    own_second.wait()
-    swap_first.wait()
-    swap_second.wait()
+    outs = (first_ref, second_ref)
+    locals_ = []
+    swaps = []
+    for d in range(2):
+        c = pltpu.make_async_copy(x_ref.at[d], outs[d].at[other, pos], local_sems.at[d])
+        c.start()
+        locals_.append(c)
+        s = pltpu.make_async_remote_copy(
+            src_ref=x_ref.at[d], dst_ref=outs[d].at[other, pos],
+            send_sem=swap_sems.at[0, d], recv_sem=swap_sems.at[1, d],
+            device_id={axis: partner}, device_id_type=MESH)
+        s.start()
+        swaps.append(s)
+
+    targets = (up, down)
+    copies = {}
+
+    def chunk_copy(d, step, which, r):
+        slot = lax.rem(pos - step + 1 + ring, ring) if d == 0 else lax.rem(pos + step - 1, ring)
+        half = other if which == 0 else 1 - other
+        rs = pl.ds(r * part, part)
+        if step == 1 and which == 0:
+            src = x_ref.at[d, rs]
+        else:
+            src = outs[d].at[half, slot, rs]
+        k = ((d * (ring - 1) + step - 1) * 2 + which) * halves + r
+        return pltpu.make_async_remote_copy(
+            src_ref=src, dst_ref=outs[d].at[half, slot, rs],
+            send_sem=send_sems.at[k], recv_sem=recv_sems.at[k],
+            device_id={axis: targets[d]}, device_id_type=MESH)
 
     for step in range(1, ring):
-        src_up = lax.rem(pos - step + 1 + ring, ring)
-        src_down = lax.rem(pos + step - 1, ring)
-        go_up = pltpu.make_async_remote_copy(
-            src_ref=first_ref.at[:, src_up], dst_ref=first_ref.at[:, src_up],
-            send_sem=send_sems.at[2 * step], recv_sem=recv_sems.at[2 * step],
-            device_id={axis: up}, device_id_type=MESH)
-        go_down = pltpu.make_async_remote_copy(
-            src_ref=second_ref.at[:, src_down], dst_ref=second_ref.at[:, src_down],
-            send_sem=send_sems.at[2 * step + 1], recv_sem=recv_sems.at[2 * step + 1],
-            device_id={axis: down}, device_id_type=MESH)
-        go_up.start()
-        go_down.start()
-        go_up.wait()
-        go_down.wait()
+        for which in range(2):
+            if step == 1 and which == 1:
+                for s in swaps:
+                    s.wait_recv()
+            for r in range(halves):
+                for d in range(2):
+                    if step > 1:
+                        copies[(d, step - 1, which, r)].wait_recv()
+                    c = chunk_copy(d, step, which, r)
+                    c.start()
+                    copies[(d, step, which, r)] = c
+    for which in range(2):
+        for r in range(halves):
+            for d in range(2):
+                copies[(d, ring - 1, which, r)].wait_recv()
+    for c in locals_:
+        c.wait()
+    for s in swaps:
+        s.wait_send()
+    for c in copies.values():
+        c.wait_send()
 
 
-def ring_gather(first, second, axis, outer, inner, ring_on_inner, cid):
+def ring_gather(first, second, axis, outer, inner, ring_on_inner, cid, halves=2):
     rows, width = first.shape
     ring = inner if ring_on_inner else outer
     shape = (2, ring, rows, width)
     x = jnp.stack([first, second])
+    n_copies = 2 * (ring - 1) * 2 * halves
     f, s = pl.pallas_call(
-        functools.partial(_ring_gather_kernel, axis, outer, inner, ring_on_inner),
+        functools.partial(_ring_gather_kernel, axis, outer, inner, ring_on_inner, halves),
         out_shape=(jax.ShapeDtypeStruct(shape, first.dtype), jax.ShapeDtypeStruct(shape, second.dtype)),
         in_specs=[pl.BlockSpec(memory_space=pltpu.VMEM)],
         out_specs=(pl.BlockSpec(memory_space=pltpu.VMEM), pl.BlockSpec(memory_space=pltpu.VMEM)),
-        scratch_shapes=[pltpu.SemaphoreType.DMA((2 * ring,)), pltpu.SemaphoreType.DMA((2 * ring,)), pltpu.SemaphoreType.DMA((2,))],
+        scratch_shapes=[
+            pltpu.SemaphoreType.DMA((n_copies,)),
+            pltpu.SemaphoreType.DMA((n_copies,)),
+            pltpu.SemaphoreType.DMA((2, 2)),
+            pltpu.SemaphoreType.DMA((2,)),
+        ],
         compiler_params=pltpu.CompilerParams(collective_id=cid, has_side_effects=True),
     )(x)
     if ring_on_inner:

time: 208 us -> 202 us (0.971)
  Pallas kernels: 47.6 us -> 37.9 us
  blocking collectives: 141 us -> 145 us
    pallas_call x1, Pallas kernels: 47.6 us -> 37.9 us  [ring_gather(): pl.pallas_call(functools.partial(_ring_gather_kernel, axis, outer, inner,...]
    all_to_all x1, blocking collectives: 28.7 us -> 31.4 us  [gather_rows(): got = lax.all_to_all(sent, axis, 0, 0, tiled=False)]
where the time goes in v5:
time: 202 us
  blocking collectives  145 us (72%)
  Pallas kernels  37.9 us (19%)
  matrix products  9.61 us (5%)
  other arithmetic  7.35 us (4%)
    all_to_all x2, blocking collectives, scatter_sum_rows(): got = lax.all_to_all(sent, axis, 0, 0, tiled=False)  113 us
    pallas_call x1, Pallas kernels, ring_gather(): pl.pallas_call(functools.partial(_ring_gather_kernel, axis, outer, inner,...  37.9 us
    all_to_all x1, blocking collectives, gather_rows(): got = lax.all_to_all(sent, axis, 0, 0, tiled=False)  31.4 us
    reduce_sum x2, other arithmetic, scatter_sum_rows(): return got.astype(jnp.float32).sum(axis=0)  4.94 us

profile of v5, /device:TPU:32, one launch (start us, length us, event | category | flops | bytes accessed | tf_op | source)
XLA Modules:
  0.0 201.8 jit_solution(7131449191809896773)
XLA Ops:
  0.6 0.0 copy-start
  0.6 1.7 pad_maximum_fusion.3.x_ref
  2.3 37.9 %shard_map.86 = (bf16[2,8,32,1024]{3,2,1,0:T(8,128)(2,1)}, bf16[2,8,32,1024]{3,2,1,0:T(8,128)(2,1)}) custom-call(bf16[2,32,1024]{2,1,0:T(8,128)(2,1)} %pad_maximum_fusion.3.x_ref), custom_call_target="tpu_custom_call" | custom-call | tf_op jit(solution)/shard_map/pallas_call | solution.py:125
  40.3 0.0 copy-start.3
  40.3 0.0 copy-start.7
  40.3 3.2 %fusion.15 = f32[512,896]{1,0:T(8,128)S(1)} fusion(bf16[512,1024]{1,0:T(8,128)(2,1)} %bitcast.24, bf16[1024,896]{1,0:T(8,128)(2,1)} %param.12), kind=kOutput, calls=%fused_computation.25 | convolution fusion | flops 939524096 | bytes 4718592 | tf_op jit(solution)/shard_map/dot_general | solution.py:158
  43.5 0.0 copy-done.3
  43.5 1.2 fusion.14
  44.8 1.3 fusion.16
  46.1 0.4 pad_maximum_fusion
  46.4 63.4 %all_to_all.15 = f32[8,64,2688]{2,1,0:T(8,128)} all-to-all(f32[8,64,2688]{2,1,0:T(8,128)S(1)} %bitcast.16), channel_id=1, replica_groups=mesh['dp'=2,'pipe'=8,'tensor'=16] {'pipe'}, dimensions={0} | all-to-all | bytes 11010048 | tf_op jit(solution)/shard_map/all_to_all | solution.py:35
  109.9 3.0 %reduce_sum.21 = f32[64,2688]{1,0:T(8,128)S(1)} reduce(f32[8,64,2688]{2,1,0:T(8,128)} %all_to_all.15, f32[]{:T(128)} %constant.2.clone.1), dimensions={0}, to_apply=%region_0.0 | reduce | flops 1204224 | bytes 6193156 | tf_op jit(solution)/shard_map/reduce_sum | solution.py:36
  112.9 0.2 fusion.9
  113.1 0.2 broadcast_in_dim.2
  113.3 31.4 %all_to_all.16 = bf16[8,64,2688]{2,1,0:T(8,128)(2,1)S(1)} all-to-all(bf16[8,64,2688]{2,1,0:T(8,128)(2,1)S(1)} %broadcast_in_dim.2), channel_id=1, replica_groups=mesh['dp'=2,'pipe'=8,'tensor'=16] {'pipe'}, dimensions={0} | all-to-all | bytes 5505024 | tf_op jit(solution)/shard_map/all_to_all | solution.py:28
  144.7 1.3 convolution_convert_fusion
  146.0 0.2 copy-done.4
  146.2 1.3 fusion.1
  147.5 0.2 copy-done.5
  147.7 1.3 add_convert_fusion
  149.0 0.2 pad_maximum_fusion.1
  149.2 50.0 %all_to_all.17 = bf16[16,32,2048]{2,1,0:T(8,128)(2,1)} all-to-all(bf16[16,32,2048]{2,1,0:T(8,128)(2,1)S(1)} %bitcast.17), channel_id=1, replica_groups=mesh['dp'=2,'pipe'=8,'tensor'=16] {'tensor'}, dimensions={0} | all-to-all | bytes 4194304 | tf_op jit(solution)/shard_map/all_to_all | solution.py:35
  199.2 2.0 reduce_sum.22
  201.2 0.7 fusion.13
  (11 shorter events, 0.0 us)
Async XLA Ops:
  0.6 44.1 %copy-start = (bf16[896,1024]{1,0:T(8,128)(2,1)S(1)}, bf16[896,1024]{1,0:T(8,128)(2,1)}, u32[]{:S(2)}) copy-start(bf16[896,1024]{1,0:T(8,128)(2,1)} %param.13) | copy-start | bytes 5505028
  40.3 3.2 %copy-start.3 = (bf16[1024,896]{1,0:T(8,128)(2,1)S(1)}, bf16[1024,896]{1,0:T(8,128)(2,1)}, u32[]{:S(2)}) copy-start(bf16[1024,896]{1,0:T(8,128)(2,1)} %param.11) | copy-start | bytes 5505028
  40.3 3.2 %copy-start.7 = (bf16[2,8,32,1024]{3,2,1,0:T(8,128)(2,1)S(1)}, bf16[2,8,32,1024]{3,2,1,0:T(8,128)(2,1)}, u32[]{:S(2)}) copy-start(bf16[2,8,32,1024]{3,2,1,0:T(8,128)(2,1)} %get-tuple-element.4) | copy-start | bytes 3145732
  43.5 1.3 copy-start.6
  109.9 3.0 %copy-start.1 = (bf16[64,896]{1,0:T(8,128)(2,1)S(1)}, bf16[64,896]{1,0:T(8,128)(2,1)}, u32[]{:S(2)}) copy-start(bf16[64,896]{1,0:T(8,128)(2,1)} %param.9) | copy-start | bytes 344068
  109.9 3.0 %copy-start.2 = (bf16[64,896]{1,0:T(8,128)(2,1)S(1)}, bf16[64,896]{1,0:T(8,128)(2,1)}, u32[]{:S(2)}) copy-start(bf16[64,896]{1,0:T(8,128)(2,1)} %param.10) | copy-start | bytes 344068
  144.7 1.5 copy-start.4
  146.2 1.5 copy-start.5

commit v6 on v5

--- a/solution.py
+++ b/solution.py
@@ -21,19 +21,6 @@
     )
     up_slope = (hidden_grad * gate_wide * sigma).astype(jnp.bfloat16)
     return jnp.concatenate([gate_slope, up_slope], axis=1)
-
-
-def gather_rows(block, axis, count):
-    sent = jnp.broadcast_to(block[None], (count,) + block.shape)
-    got = lax.all_to_all(sent, axis, 0, 0, tiled=False)
-    return got.reshape((count * block.shape[0],) + block.shape[1:])
-
-
-def scatter_sum_rows(partial, axis, count, link_dtype):
-    rows = partial.shape[0] // count
-    sent = partial.reshape((count, rows) + partial.shape[1:]).astype(link_dtype)
-    got = lax.all_to_all(sent, axis, 0, 0, tiled=False)
-    return got.astype(jnp.float32).sum(axis=0)
 
 
 def _ring_gather_kernel(axis, outer, inner, ring_on_inner, halves, x_ref, first_ref, second_ref, send_sems, recv_sems, swap_sems, local_sems):
@@ -141,6 +128,71 @@
             s.transpose(1, 0, 2, 3).reshape(2 * ring * rows, width))
 
 
+def _exchange_kernel(plan, *refs):
+    k = len(plan)
+    ins, outs = refs[:k], refs[k:2 * k]
+    send_sems, recv_sems, local_sems = refs[2 * k:]
+    axes = {}
+    for axis, count, _ in plan:
+        axes[axis] = count
+    barrier = pltpu.get_barrier_semaphore()
+    total = 0
+    for axis, count in axes.items():
+        me = lax.axis_index(axis)
+        for d in range(1, count):
+            pl.semaphore_signal(barrier, inc=1, device_id={axis: lax.rem(me + d, count)}, device_id_type=MESH)
+        total += count - 1
+    pl.semaphore_wait(barrier, total)
+    started = []
+    for e, (axis, count, spread) in enumerate(plan):
+        me = lax.axis_index(axis)
+        src = ins[e] if spread else ins[e].at[me]
+        own = pltpu.make_async_copy(src, outs[e].at[me], local_sems.at[e])
+        own.start()
+        started.append(own)
+    remote = []
+    for d in range(1, max(c for _, c, _ in plan)):
+        for e, (axis, count, spread) in enumerate(plan):
+            if d >= count:
+                continue
+            me = lax.axis_index(axis)
+            peer = lax.rem(me + d, count)
+            src = ins[e] if spread else ins[e].at[peer]
+            c = pltpu.make_async_remote_copy(
+                src_ref=src, dst_ref=outs[e].at[me],
+                send_sem=send_sems.at[e, d - 1], recv_sem=recv_sems.at[e, d - 1],
+                device_id={axis: peer}, device_id_type=MESH)
+            c.start()
+            remote.append(c)
+    for c in started:
+        c.wait()
+    for c in remote:
+        c.wait_recv()
+    for c in remote:
+        c.wait_send()
+
+
+def exchange(items, cid):
+    plan = tuple((axis, count, spread) for _, axis, count, spread in items)
+    shapes = []
+    for x, axis, count, spread in items:
+        shape = (count,) + x.shape if spread else x.shape
+        shapes.append(jax.ShapeDtypeStruct(shape, x.dtype))
+    widest = max(count for _, _, count, _ in items)
+    return pl.pallas_call(
+        functools.partial(_exchange_kernel, plan),
+        out_shape=tuple(shapes),
+        in_specs=[pl.BlockSpec(memory_space=pl.ANY)] * len(items),
+        out_specs=tuple(pl.BlockSpec(memory_space=pl.ANY) for _ in items),
+        scratch_shapes=[
+            pltpu.SemaphoreType.DMA((len(items), widest - 1)),
+            pltpu.SemaphoreType.DMA((len(items), widest - 1)),
+            pltpu.SemaphoreType.DMA((len(items),)),
+        ],
+        compiler_params=pltpu.CompilerParams(collective_id=cid, has_side_effects=True),
+    )(*[x for x, _, _, _ in items])
+
+
 def per_device(
     forward_acts, backward_grad, stored_gate, stored_up, gate_weight, up_weight, down_weight
 ):
@@ -148,39 +200,65 @@
     n_tensor = lax.axis_size("tensor")
     hidden_width = gate_weight.shape[1]
     model_width = forward_acts.shape[1]
+    half = model_width // 2
     contract_last = (((1,), (1,)), ((), ()))
 
-    whole_acts, whole_grad = ring_gather(
-        forward_acts, backward_grad, "tensor", 2, n_tensor // 2, True, 0
-    )
-
+    def blocks(partial, count, dtype):
+        return partial.reshape((count, partial.shape[0] // count) + partial.shape[1:]).astype(dtype)
+
+    acts_low, acts_high = ring_gather(
+        forward_acts[:, :half], forward_acts[:, half:], "tensor", 2, n_tensor // 2, True, 0
+    )
+    whole_acts = jnp.concatenate([acts_low, acts_high], axis=1)
     gate_part = jnp.dot(whole_acts, gate_weight, preferred_element_type=jnp.float32)
     up_part = jnp.dot(whole_acts, up_weight, preferred_element_type=jnp.float32)
+
+    got_proj, got_grad = exchange(
+        [
+            (blocks(jnp.concatenate([gate_part, up_part], axis=1), n_pipe, PIPE_LINK), "pipe", n_pipe, False),
+            (backward_grad, "tensor", n_tensor, True),
+        ],
+        1,
+    )
+    summed = got_proj.astype(jnp.float32).sum(axis=0)
+    hidden_part = (jax.nn.silu(summed[:, :hidden_width]) * summed[:, hidden_width:]).astype(
+        jnp.bfloat16
+    )
+    whole_grad = got_grad.reshape(n_tensor * backward_grad.shape[0], model_width)
     grad_part = lax.dot_general(
         whole_grad, down_weight, contract_last, preferred_element_type=jnp.float32
     )
-    summed = scatter_sum_rows(
-        jnp.concatenate([gate_part, up_part, grad_part], axis=1), "pipe", n_pipe, PIPE_LINK
-    )
-    gate_pre = summed[:, :hidden_width]
-    up_pre = summed[:, hidden_width : 2 * hidden_width]
-    hidden_grad = summed[:, 2 * hidden_width :]
-    hidden_part = (jax.nn.silu(gate_pre) * up_pre).astype(jnp.bfloat16)
+
+    got_hidden, got_hgrad = exchange(
+        [
+            (hidden_part, "pipe", n_pipe, True),
+            (blocks(grad_part, n_pipe, PIPE_LINK), "pipe", n_pipe, False),
+        ],
+        2,
+    )
+    hidden = got_hidden.reshape(n_pipe * hidden_part.shape[0], hidden_width)
+    hidden_grad = got_hgrad.astype(jnp.float32).sum(axis=0)
     local_slopes = make_slopes(hidden_grad, stored_gate, stored_up)
-
-    rows = gather_rows(jnp.concatenate([hidden_part, local_slopes], axis=1), "pipe", n_pipe)
-    hidden = rows[:, :hidden_width]
-    gate_slopes = rows[:, hidden_width : 2 * hidden_width]
-    up_slopes = rows[:, 2 * hidden_width :]
-
     out_part = jnp.dot(hidden, down_weight, preferred_element_type=jnp.float32)
+
+    got_out, got_slopes = exchange(
+        [
+            (blocks(out_part, n_tensor, TENSOR_LINK), "tensor", n_tensor, False),
+            (local_slopes, "pipe", n_pipe, True),
+        ],
+        3,
+    )
+    layer_output = got_out.astype(jnp.float32).sum(axis=0).astype(jnp.bfloat16)
+    all_slopes = got_slopes.reshape(n_pipe * local_slopes.shape[0], 2 * hidden_width)
     in_part = lax.dot_general(
-        gate_slopes, gate_weight, contract_last, preferred_element_type=jnp.float32
-    ) + lax.dot_general(up_slopes, up_weight, contract_last, preferred_element_type=jnp.float32)
-    finished = scatter_sum_rows(
-        jnp.concatenate([out_part, in_part], axis=1), "tensor", n_tensor, TENSOR_LINK
-    ).astype(jnp.bfloat16)
-    return (finished[:, :model_width], finished[:, model_width:])
+        all_slopes[:, :hidden_width], gate_weight, contract_last, preferred_element_type=jnp.float32
+    ) + lax.dot_general(
+        all_slopes[:, hidden_width:], up_weight, contract_last, preferred_element_type=jnp.float32
+    )
+
+    (got_in,) = exchange([(blocks(in_part, n_tensor, TENSOR_LINK), "tensor", n_tensor, False)], 4)
+    input_grad = got_in.astype(jnp.float32).sum(axis=0).astype(jnp.bfloat16)
+    return (layer_output, input_grad)
 
 
 def solution(mesh):

time: 202 us -> 217 us (1.074)
  Pallas kernels: 37.9 us -> 186 us
  blocking collectives: 145 us -> 0 us
  matrix products: 9.61 us -> 15.8 us
  other arithmetic: 7.35 us -> 12.4 us
    pallas_call x0 -> x4, Pallas kernels: none -> 152 us  [exchange(): pl.pallas_call(functools.partial(_exchange_kernel, plan), out_shape=tuple...]
    all_to_all x3 -> x0, blocking collectives: 145 us -> none  [the longest x2 113 us: scatter_sum_rows(): got = lax.all_to_all(sent, axis, 0, 0, tiled=False)]
    pallas_call x1, Pallas kernels: 37.9 us -> 34.4 us  [ring_gather(): pl.pallas_call(functools.partial(_ring_gather_kernel, axis, outer, inner,...]
    reduce_sum x2 -> x4, other arithmetic: 4.94 us -> 8.12 us  [the longest x1 2.35 us: per_device(): summed = got_proj.astype(jnp.float32).sum(axis=0)]
    dot_general x2, matrix products: 2.59 us -> 5.45 us  [the longest x1 3.2 us: per_device(): lax.dot_general(all_slopes[:, :hidden_width], gate_weight, contract_last,...]
    concatenate x3 -> x2, other arithmetic: 0.57 us -> 2.76 us  [the longest x1 2.06 us: per_device(): jnp.concatenate([gate_part, up_part], axis=1)]
where the time goes in v6:
time: 217 us; the launch traced here: 216 us
  Pallas kernels  186 us (86%)
  matrix products  15.8 us (7%)
  other arithmetic  12.4 us (6%)
    pallas_call x4, Pallas kernels, exchange(): pl.pallas_call(functools.partial(_exchange_kernel, plan), out_shape=tuple...  152 us
    pallas_call x1, Pallas kernels, ring_gather(): pl.pallas_call(functools.partial(_ring_gather_kernel, axis, outer, inner,...  34.4 us

profile of v6, /device:TPU:32, one launch (start us, length us, event | category | flops | bytes accessed | tf_op | source)
XLA Modules:
  0.0 215.9 jit_solution(17278580106514632182)
XLA Ops:
  0.6 0.0 copy-start
  0.6 0.9 slice_bitcast_fusion.1
  1.6 0.6 pad_maximum_fusion.5.x_ref
  2.2 34.4 %shard_map.86 = (bf16[2,8,32,512]{3,2,1,0:T(8,128)(2,1)}, bf16[2,8,32,512]{3,2,1,0:T(8,128)(2,1)}) custom-call(bf16[2,32,512]{2,1,0:T(8,128)(2,1)} %pad_maximum_fusion.5.x_ref), custom_call_target="tpu_custom_call" | custom-call | tf_op jit(solution)/shard_map/pallas_call | solution.py:112
  36.6 0.0 copy-start.3
  36.6 3.2 %fusion.10 = f32[512,896]{1,0:T(8,128)S(1)} fusion(bf16[1024,896]{1,0:T(8,128)(2,1)} %param.12, bf16[512,512]{1,0:T(8,128)(2,1)} %bitcast.32, bf16[512,512]{1,0:T(8,128)(2,1)} %bitcast.30), kind=kOutput, calls=%fused_computation.11 | convolution fusion | flops 941621248 | bytes 4718592 | tf_op jit(solution)/shard_map/dot_general | solution.py:214
  39.8 1.2 fusion.11
  41.1 2.1 pad_maximum_fusion
  43.2 53.1 %shard_map.87 = (f32[8,64,1792]{2,1,0:T(8,128)}, bf16[16,32,1024]{2,1,0:T(8,128)(2,1)}) custom-call(f32[8,64,1792]{2,1,0:T(8,128)} %bitcast.24, bf16[32,1024]{1,0:T(8,128)(2,1)} %refs_1_.1), custom_call_target="tpu_custom_call" | custom-call | tf_op jit(solution)/shard_map/pallas_call | solution.py:182
  96.3 2.3 %reduce_sum.42 = f32[64,1792]{1,0:T(8,128)S(1)} reduce(f32[8,64,1792]{2,1,0:T(8,128)} %get-tuple-element.12, f32[]{:T(128)} %constant.6.clone.1), dimensions={0}, to_apply=%region_0.0 | reduce | flops 802816 | bytes 4128772 | tf_op jit(solution)/shard_map/reduce_sum | solution.py:223
  98.6 0.7 fusion.20.refs_0_
  99.3 0.0 copy-done.6
  99.3 2.5 %fusion.2.refs_1_ = f32[8,64,896]{2,1,0:T(8,128)} fusion(bf16[8,64,1024]{2,1,0:T(8,128)(2,1)S(1)} %bitcast.28, bf16[896,1024]{1,0:T(8,128)(2,1)S(1)} %copy-done), kind=kOutput, calls=%fused_computation.4 | convolution fusion | flops 939524096 | bytes 4718592 | tf_op jit(solution)/shard_map/dot_general | solution.py:228
  101.9 32.3 %shard_map.88 = (bf16[8,64,896]{2,1,0:T(8,128)(2,1)}, f32[8,64,896]{2,1,0:T(8,128)}) custom-call(bf16[64,896]{1,0:T(8,128)(2,1)} %fusion.20.refs_0_, f32[8,64,896]{2,1,0:T(8,128)} %fusion.2.refs_1_), custom_call_target="tpu_custom_call" | custom-call | tf_op jit(solution)/shard_map/pallas_call | solution.py:182
  134.2 3.4 %fusion.4.refs_0_ = bf16[16,32,1024]{2,1,0:T(8,128)(2,1)} fusion(bf16[16,32,896]{2,1,0:T(8,128)(2,1)} %bitcast.29, bf16[896,1024]{1,0:T(8,128)(2,1)S(1)} %copy-done), kind=kOutput, calls=%fused_computation.6 | convolution fusion | flops 940048384 | bytes 3801088 | tf_op jit(solution)/shard_map/dot_general | solution.py:242
  137.6 1.6 reduce_sum.43
  139.3 0.1 fusion.17
  139.4 0.7 pad_maximum_fusion.4.refs_1_
  140.1 37.3 %shard_map.89 = (bf16[16,32,1024]{2,1,0:T(8,128)(2,1)}, bf16[8,64,1792]{2,1,0:T(8,128)(2,1)}) custom-call(bf16[16,32,1024]{2,1,0:T(8,128)(2,1)} %fusion.4.refs_0_, bf16[64,1792]{1,0:T(8,128)(2,1)} %pad_maximum_fusion.4.refs_1_), custom_call_target="tpu_custom_call" | custom-call | tf_op jit(solution)/shard_map/pallas_call | solution.py:182
  177.4 2.1 reduce_sum.44
  179.5 3.2 %fusion.8 = f32[512,1024]{1,0:T(8,128)S(1)} fusion(bf16[1024,896]{1,0:T(8,128)(2,1)} %param.11, bf16[512,1792]{1,0:T(8,128)(2,1)} %bitcast.26), kind=kOutput, calls=%fused_computation.9 | convolution fusion | flops 939524096 | bytes 4849664 | tf_op jit(solution)/shard_map/dot_general | solution.py:253
  182.7 2.3 %add_convert_fusion = bf16[512,1024]{1,0:T(8,128)(2,1)} fusion(f32[512,1024]{1,0:T(8,128)S(1)} %fusion.8, bf16[1024,896]{1,0:T(8,128)(2,1)S(1)} %copy-done.4, bf16[512,1792]{1,0:T(8,128)(2,1)S(1)} %bitcast.27), kind=kOutput, calls=%fused_computation.1 | convolution fusion | flops 940572672 | bytes 5898240 | tf_op jit(solution)/shard_map/dot_general | solution.py:255
  184.9 28.9 %shard_map.90 = bf16[16,32,1024]{2,1,0:T(8,128)(2,1)} custom-call(bf16[16,32,1024]{2,1,0:T(8,128)(2,1)} %bitcast.25), custom_call_target="tpu_custom_call" | custom-call | tf_op jit(solution)/shard_map/pallas_call | solution.py:182
  213.9 2.1 reduce_sum.45
  (15 shorter events, 0.0 us)
Async XLA Ops:
  0.6 98.7 %copy-start = (bf16[896,1024]{1,0:T(8,128)(2,1)S(1)}, bf16[896,1024]{1,0:T(8,128)(2,1)}, u32[]{:S(2)}) copy-start(bf16[896,1024]{1,0:T(8,128)(2,1)} %param.13) | copy-start | bytes 5505028
  36.6 3.2 %copy-start.3 = (bf16[1024,896]{1,0:T(8,128)(2,1)S(1)}, bf16[1024,896]{1,0:T(8,128)(2,1)}, u32[]{:S(2)}) copy-start(bf16[1024,896]{1,0:T(8,128)(2,1)} %param.11) | copy-start | bytes 5505028
  36.6 3.2 %copy-start.7 = (bf16[2,8,32,512]{3,2,1,0:T(8,128)(2,1)S(1)}, bf16[2,8,32,512]{3,2,1,0:T(8,128)(2,1)}, u32[]{:S(2)}) copy-start(bf16[2,8,32,512]{3,2,1,0:T(8,128)(2,1)} %get-tuple-element.10) | copy-start | bytes 1572868
  36.6 3.2 %copy-start.8 = (bf16[2,8,32,512]{3,2,1,0:T(8,128)(2,1)S(1)}, bf16[2,8,32,512]{3,2,1,0:T(8,128)(2,1)}, u32[]{:S(2)}) copy-start(bf16[2,8,32,512]{3,2,1,0:T(8,128)(2,1)} %get-tuple-element.11) | copy-start | bytes 1572868
  96.2 3.1 %copy-start.6 = (bf16[16,32,1024]{2,1,0:T(8,128)(2,1)S(1)}, bf16[16,32,1024]{2,1,0:T(8,128)(2,1)}, u32[]{:S(2)}) copy-start(bf16[16,32,1024]{2,1,0:T(8,128)(2,1)} %get-tuple-element.13) | copy-start | bytes 3145732
  137.6 1.7 copy-start.1
  137.6 1.7 copy-start.2
  179.5 3.2 %copy-start.4 = (bf16[1024,896]{1,0:T(8,128)(2,1)S(1)}, bf16[1024,896]{1,0:T(8,128)(2,1)}, u32[]{:S(2)}) copy-start(bf16[1024,896]{1,0:T(8,128)(2,1)} %param.12) | copy-start | bytes 5505028
  179.5 3.2 %copy-start.5 = (bf16[8,64,1792]{2,1,0:T(8,128)(2,1)S(1)}, bf16[8,64,1792]{2,1,0:T(8,128)(2,1)}, u32[]{:S(2)}) copy-start(bf16[8,64,1792]{2,1,0:T(8,128)(2,1)} %get-tuple-element.17) | copy-start | bytes 5505028

commit v7 on v5

--- a/solution.py
+++ b/solution.py
@@ -55,6 +55,7 @@
     down = at(lax.rem(pos + ring - 1, ring), other)
     rows = x_ref.shape[1]
     part = rows // halves
+    steps = (ring // 2, (ring - 1) // 2)
 
     barrier = pltpu.get_barrier_semaphore()
     for peer in (partner, up, down):
@@ -64,13 +65,13 @@
     outs = (first_ref, second_ref)
     locals_ = []
     swaps = []
-    for d in range(2):
-        c = pltpu.make_async_copy(x_ref.at[d], outs[d].at[other, pos], local_sems.at[d])
+    for a in range(2):
+        c = pltpu.make_async_copy(x_ref.at[a], outs[a].at[other, pos], local_sems.at[a])
         c.start()
         locals_.append(c)
         s = pltpu.make_async_remote_copy(
-            src_ref=x_ref.at[d], dst_ref=outs[d].at[other, pos],
-            send_sem=swap_sems.at[0, d], recv_sem=swap_sems.at[1, d],
+            src_ref=x_ref.at[a], dst_ref=outs[a].at[other, pos],
+            send_sem=swap_sems.at[0, a], recv_sem=swap_sems.at[1, a],
             device_id={axis: partner}, device_id_type=MESH)
         s.start()
         swaps.append(s)
@@ -78,36 +79,42 @@
     targets = (up, down)
     copies = {}
 
-    def chunk_copy(d, step, which, r):
+    def chunk_copy(d, step, which, r, a):
         slot = lax.rem(pos - step + 1 + ring, ring) if d == 0 else lax.rem(pos + step - 1, ring)
         half = other if which == 0 else 1 - other
         rs = pl.ds(r * part, part)
         if step == 1 and which == 0:
-            src = x_ref.at[d, rs]
+            src = x_ref.at[a, rs]
         else:
-            src = outs[d].at[half, slot, rs]
-        k = ((d * (ring - 1) + step - 1) * 2 + which) * halves + r
+            src = outs[a].at[half, slot, rs]
+        k = (((d * ring + step - 1) * 2 + which) * halves + r) * 2 + a
         return pltpu.make_async_remote_copy(
-            src_ref=src, dst_ref=outs[d].at[half, slot, rs],
+            src_ref=src, dst_ref=outs[a].at[half, slot, rs],
             send_sem=send_sems.at[k], recv_sem=recv_sems.at[k],
             device_id={axis: targets[d]}, device_id_type=MESH)
 
-    for step in range(1, ring):
+    for step in range(1, steps[0] + 1):
         for which in range(2):
             if step == 1 and which == 1:
                 for s in swaps:
                     s.wait_recv()
             for r in range(halves):
-                for d in range(2):
-                    if step > 1:
-                        copies[(d, step - 1, which, r)].wait_recv()
-                    c = chunk_copy(d, step, which, r)
-                    c.start()
-                    copies[(d, step, which, r)] = c
-    for which in range(2):
-        for r in range(halves):
-            for d in range(2):
-                copies[(d, ring - 1, which, r)].wait_recv()
+                for a in range(2):
+                    for d in range(2):
+                        if step > steps[d]:
+                            continue
+                        if step > 1:
+                            copies[(d, step - 1, which, r, a)].wait_recv()
+                        c = chunk_copy(d, step, which, r, a)
+                        c.start()
+                        copies[(d, step, which, r, a)] = c
+    for d in range(2):
+        if steps[d] == 0:
+            continue
+        for which in range(2):
+            for r in range(halves):
+                for a in range(2):
+                    copies[(d, steps[d], which, r, a)].wait_recv()
     for c in locals_:
         c.wait()
     for s in swaps:
@@ -121,7 +128,7 @@
     ring = inner if ring_on_inner else outer
     shape = (2, ring, rows, width)
     x = jnp.stack([first, second])
-    n_copies = 2 * (ring - 1) * 2 * halves
+    n_copies = 2 * ring * 2 * halves * 2
     f, s = pl.pallas_call(
         functools.partial(_ring_gather_kernel, axis, outer, inner, ring_on_inner, halves),
         out_shape=(jax.ShapeDtypeStruct(shape, first.dtype), jax.ShapeDtypeStruct(shape, second.dtype)),

time: 202 us -> 211 us (1.045)
  blocking collectives: 145 us -> 155 us
    all_to_all x2, blocking collectives: 113 us -> 121 us  [scatter_sum_rows(): got = lax.all_to_all(sent, axis, 0, 0, tiled=False)]
    all_to_all x1, blocking collectives: 31.4 us -> 34.1 us  [gather_rows(): got = lax.all_to_all(sent, axis, 0, 0, tiled=False)]
where the time goes in v7:
time: 211 us; the launch traced here: 210 us
  blocking collectives  155 us (73%)
  Pallas kernels  36.4 us (17%)
  matrix products  9.63 us (5%)
  other arithmetic  7.35 us (3%)
    all_to_all x2, blocking collectives, scatter_sum_rows(): got = lax.all_to_all(sent, axis, 0, 0, tiled=False)  121 us
    pallas_call x1, Pallas kernels, ring_gather(): pl.pallas_call(functools.partial(_ring_gather_kernel, axis, outer, inner,...  36.4 us
    all_to_all x1, blocking collectives, gather_rows(): got = lax.all_to_all(sent, axis, 0, 0, tiled=False)  34.1 us
    reduce_sum x2, other arithmetic, scatter_sum_rows(): return got.astype(jnp.float32).sum(axis=0)  4.94 us

profile of v7, /device:TPU:32, one launch (start us, length us, event | category | flops | bytes accessed | tf_op | source)
XLA Modules:
  0.0 210.3 jit_solution(15576016107910345867)
XLA Ops:
  0.6 0.0 copy-start
  0.6 1.7 pad_maximum_fusion.3.x_ref
  2.3 36.4 %shard_map.86 = (bf16[2,8,32,1024]{3,2,1,0:T(8,128)(2,1)}, bf16[2,8,32,1024]{3,2,1,0:T(8,128)(2,1)}) custom-call(bf16[2,32,1024]{2,1,0:T(8,128)(2,1)} %pad_maximum_fusion.3.x_ref), custom_call_target="tpu_custom_call" | custom-call | tf_op jit(solution)/shard_map/pallas_call | solution.py:132
  38.7 0.0 copy-start.3
  38.8 3.2 %fusion.15 = f32[512,896]{1,0:T(8,128)S(1)} fusion(bf16[512,1024]{1,0:T(8,128)(2,1)} %bitcast.24, bf16[1024,896]{1,0:T(8,128)(2,1)} %param.12), kind=kOutput, calls=%fused_computation.25 | convolution fusion | flops 939524096 | bytes 4718592 | tf_op jit(solution)/shard_map/dot_general | solution.py:165
  42.0 1.2 fusion.14
  43.3 1.3 fusion.16
  44.6 0.4 pad_maximum_fusion
  44.9 67.2 %all_to_all.15 = f32[8,64,2688]{2,1,0:T(8,128)} all-to-all(f32[8,64,2688]{2,1,0:T(8,128)S(1)} %bitcast.16), channel_id=1, replica_groups=mesh['dp'=2,'pipe'=8,'tensor'=16] {'pipe'}, dimensions={0} | all-to-all | bytes 11010048 | tf_op jit(solution)/shard_map/all_to_all | solution.py:35
  112.1 3.0 %reduce_sum.21 = f32[64,2688]{1,0:T(8,128)S(1)} reduce(f32[8,64,2688]{2,1,0:T(8,128)} %all_to_all.15, f32[]{:T(128)} %constant.2.clone.1), dimensions={0}, to_apply=%region_0.0 | reduce | flops 1204224 | bytes 6193156 | tf_op jit(solution)/shard_map/reduce_sum | solution.py:36
  115.1 0.0 copy-done.1
  115.1 0.0 copy-done.2
  115.1 0.2 fusion.9
  115.3 0.2 broadcast_in_dim.2
  115.5 34.1 %all_to_all.16 = bf16[8,64,2688]{2,1,0:T(8,128)(2,1)S(1)} all-to-all(bf16[8,64,2688]{2,1,0:T(8,128)(2,1)S(1)} %broadcast_in_dim.2), channel_id=1, replica_groups=mesh['dp'=2,'pipe'=8,'tensor'=16] {'pipe'}, dimensions={0} | all-to-all | bytes 5505024 | tf_op jit(solution)/shard_map/all_to_all | solution.py:28
  149.6 1.3 convolution_convert_fusion
  150.9 0.2 copy-done.4
  151.1 1.3 fusion.1
  152.4 0.2 copy-done.5
  152.6 1.3 add_convert_fusion
  153.9 0.2 pad_maximum_fusion.1
  154.1 53.6 %all_to_all.17 = bf16[16,32,2048]{2,1,0:T(8,128)(2,1)} all-to-all(bf16[16,32,2048]{2,1,0:T(8,128)(2,1)S(1)} %bitcast.17), channel_id=1, replica_groups=mesh['dp'=2,'pipe'=8,'tensor'=16] {'tensor'}, dimensions={0} | all-to-all | bytes 4194304 | tf_op jit(solution)/shard_map/all_to_all | solution.py:35
  207.7 2.0 reduce_sum.22
  209.6 0.7 fusion.13
  (11 shorter events, 0.0 us)
Async XLA Ops:
  0.6 42.6 %copy-start = (bf16[896,1024]{1,0:T(8,128)(2,1)S(1)}, bf16[896,1024]{1,0:T(8,128)(2,1)}, u32[]{:S(2)}) copy-start(bf16[896,1024]{1,0:T(8,128)(2,1)} %param.13) | copy-start | bytes 5505028
  38.7 3.2 %copy-start.3 = (bf16[1024,896]{1,0:T(8,128)(2,1)S(1)}, bf16[1024,896]{1,0:T(8,128)(2,1)}, u32[]{:S(2)}) copy-start(bf16[1024,896]{1,0:T(8,128)(2,1)} %param.11) | copy-start | bytes 5505028
  38.7 3.2 %copy-start.7 = (bf16[2,8,32,1024]{3,2,1,0:T(8,128)(2,1)S(1)}, bf16[2,8,32,1024]{3,2,1,0:T(8,128)(2,1)}, u32[]{:S(2)}) copy-start(bf16[2,8,32,1024]{3,2,1,0:T(8,128)(2,1)} %get-tuple-element.4) | copy-start | bytes 3145732
  42.0 1.3 copy-start.6
  112.1 3.0 %copy-start.1 = (bf16[64,896]{1,0:T(8,128)(2,1)S(1)}, bf16[64,896]{1,0:T(8,128)(2,1)}, u32[]{:S(2)}) copy-start(bf16[64,896]{1,0:T(8,128)(2,1)} %param.9) | copy-start | bytes 344068
  112.1 3.0 %copy-start.2 = (bf16[64,896]{1,0:T(8,128)(2,1)S(1)}, bf16[64,896]{1,0:T(8,128)(2,1)}, u32[]{:S(2)}) copy-start(bf16[64,896]{1,0:T(8,128)(2,1)} %param.10) | copy-start | bytes 344068
  149.6 1.5 copy-start.4
  151.1 1.5 copy-start.5

commit v8 on v7

--- a/solution.py
+++ b/solution.py
@@ -148,6 +148,92 @@
             s.transpose(1, 0, 2, 3).reshape(2 * ring * rows, width))
 
 
+def _ring_sum_kernel(axis, outer, chunks, x_ref, out_ref, send_buf, recv_buf, swap_buf, send_sems, recv_sems, swap_sems):
+    me = lax.axis_index(axis)
+    y = me // 2
+    x = me % 2
+    ring = outer
+    up = lax.rem(y + 1, ring) * 2 + x
+    down = lax.rem(y + ring - 1, ring) * 2 + x
+    partner = y * 2 + 1 - x
+    rows = x_ref.shape[1]
+    half = rows // 2
+    part = half // chunks
+
+    barrier = pltpu.get_barrier_semaphore()
+    for peer in (partner, up, down):
+        pl.semaphore_signal(barrier, inc=1, device_id={axis: peer}, device_id_type=MESH)
+    pl.semaphore_wait(barrier, 3)
+
+    targets = (up, down)
+    copies = {}
+
+    def dest(d, step):
+        return lax.rem(y - step + ring, ring) if d == 0 else lax.rem(y + step, ring)
+
+    for step in range(1, ring):
+        for c in range(chunks):
+            for d in range(2):
+                rs = pl.ds(d * half + c * part, part)
+                blocks = pl.ds(dest(d, step) * 2, 2)
+                if step == 1:
+                    src = x_ref.at[blocks, rs]
+                else:
+                    copies[(d, step - 1, c)].wait_recv()
+                    send_buf[d, step, :, pl.ds(c * part, part)] = (
+                        recv_buf[d, step - 1, :, pl.ds(c * part, part)] + x_ref[blocks, rs]
+                    )
+                    src = send_buf.at[d, step, :, pl.ds(c * part, part)]
+                cp = pltpu.make_async_remote_copy(
+                    src_ref=src, dst_ref=recv_buf.at[d, step, :, pl.ds(c * part, part)],
+                    send_sem=send_sems.at[d, step, c], recv_sem=recv_sems.at[d, step, c],
+                    device_id={axis: targets[d]}, device_id_type=MESH)
+                cp.start()
+                copies[(d, step, c)] = cp
+    swaps = []
+    for c in range(chunks):
+        for d in range(2):
+            rs = pl.ds(d * half + c * part, part)
+            local = pl.ds(c * part, part)
+            copies[(d, ring - 1, c)].wait_recv()
+            swap_buf[0, d, local] = recv_buf[d, ring - 1, 1 - x, local] + x_ref[y * 2 + 1 - x, rs]
+            out_ref[rs] = recv_buf[d, ring - 1, x, local] + x_ref[y * 2 + x, rs]
+            sw = pltpu.make_async_remote_copy(
+                src_ref=swap_buf.at[0, d, local], dst_ref=swap_buf.at[1, d, local],
+                send_sem=swap_sems.at[0, d, c], recv_sem=swap_sems.at[1, d, c],
+                device_id={axis: partner}, device_id_type=MESH)
+            sw.start()
+            swaps.append((d, c, sw))
+    for d, c, sw in swaps:
+        rs = pl.ds(d * half + c * part, part)
+        sw.wait_recv()
+        out_ref[rs] = out_ref[rs] + swap_buf[1, d, pl.ds(c * part, part)]
+    for d, c, sw in swaps:
+        sw.wait_send()
+    for cp in copies.values():
+        cp.wait_send()
+
+
+def ring_sum(partial, axis, outer, cid, chunks=2):
+    count, rows, width = partial.shape
+    half = rows // 2
+    return pl.pallas_call(
+        functools.partial(_ring_sum_kernel, axis, outer, chunks),
+        out_shape=jax.ShapeDtypeStruct((rows, width), jnp.float32),
+        in_specs=[pl.BlockSpec(memory_space=pltpu.VMEM)],
+        out_specs=pl.BlockSpec(memory_space=pltpu.VMEM),
+        scratch_shapes=[
+            pltpu.VMEM((2, outer, 2, half, width), jnp.float32),
+            pltpu.VMEM((2, outer, 2, half, width), jnp.float32),
+            pltpu.VMEM((2, 2, half, width), jnp.float32),
+            pltpu.SemaphoreType.DMA((2, outer, chunks)),
+            pltpu.SemaphoreType.DMA((2, outer, chunks)),
+            pltpu.SemaphoreType.DMA((2, 2, chunks)),
+        ],
+        compiler_params=pltpu.CompilerParams(collective_id=cid, has_side_effects=True, vmem_limit_bytes=60 * 1024 * 1024),
+    )(partial)
+
+
 def per_device(
     forward_acts, backward_grad, stored_gate, stored_up, gate_weight, up_weight, down_weight
 ):
@@ -166,8 +252,12 @@
     grad_part = lax.dot_general(
         whole_grad, down_weight, contract_last, preferred_element_type=jnp.float32
     )
-    summed = scatter_sum_rows(
-        jnp.concatenate([gate_part, up_part, grad_part], axis=1), "pipe", n_pipe, PIPE_LINK
+    partials = jnp.concatenate([gate_part, up_part, grad_part], axis=1)
+    summed = ring_sum(
+        partials.reshape((n_pipe, partials.shape[0] // n_pipe, partials.shape[1])),
+        "pipe",
+        n_pipe // 2,
+        1,
     )
     gate_pre = summed[:, :hidden_width]
     up_pre = summed[:, hidden_width : 2 * hidden_width]

time: 211 us -> 204 us (0.967)
  blocking collectives: 155 us -> 88 us
  Pallas kernels: 36.4 us -> 96.4 us
    all_to_all x2 -> x1, blocking collectives: 121 us -> 53.2 us  [scatter_sum_rows(): got = lax.all_to_all(sent, axis, 0, 0, tiled=False)]
    pallas_call x0 -> x1, Pallas kernels: none -> 60 us  [ring_sum(): pl.pallas_call(functools.partial(_ring_sum_kernel, axis, outer, chunks),...]
    reduce_sum x2 -> x1, other arithmetic: 4.94 us -> 1.98 us  [scatter_sum_rows(): return got.astype(jnp.float32).sum(axis=0)]
    concatenate x1, other arithmetic: 0.36 us -> 2.76 us  [per_device(): partials = jnp.concatenate([gate_part, up_part, grad_part], axis=1)]
where the time goes in v8:
time: 204 us
  Pallas kernels  96.4 us (47%)
  blocking collectives  88 us (43%)
  matrix products  9.62 us (5%)
  other arithmetic  7.94 us (4%)
    pallas_call x1, Pallas kernels, ring_sum(): pl.pallas_call(functools.partial(_ring_sum_kernel, axis, outer, chunks),...  60 us
    all_to_all x1, blocking collectives, scatter_sum_rows(): got = lax.all_to_all(sent, axis, 0, 0, tiled=False)  53.2 us
    pallas_call x1, Pallas kernels, ring_gather(): pl.pallas_call(functools.partial(_ring_gather_kernel, axis, outer, inner,...  36.4 us
    all_to_all x1, blocking collectives, gather_rows(): got = lax.all_to_all(sent, axis, 0, 0, tiled=False)  34.8 us

profile of v8, /device:TPU:32, one launch (start us, length us, event | category | flops | bytes accessed | tf_op | source)
XLA Modules:
  0.0 203.9 jit_solution(16555391327221301313)
XLA Ops:
  0.6 0.0 copy-start
  0.6 1.7 pad_maximum_fusion.3.x_ref
  2.3 36.4 %shard_map.86 = (bf16[2,8,32,1024]{3,2,1,0:T(8,128)(2,1)}, bf16[2,8,32,1024]{3,2,1,0:T(8,128)(2,1)}) custom-call(bf16[2,32,1024]{2,1,0:T(8,128)(2,1)} %pad_maximum_fusion.3.x_ref), custom_call_target="tpu_custom_call" | custom-call | tf_op jit(solution)/shard_map/pallas_call | solution.py:132
  38.7 0.0 copy-start.3
  38.8 3.2 %fusion.14 = f32[512,896]{1,0:T(8,128)S(1)} fusion(bf16[512,1024]{1,0:T(8,128)(2,1)} %bitcast.24, bf16[1024,896]{1,0:T(8,128)(2,1)} %param.12), kind=kOutput, calls=%fused_computation.24 | convolution fusion | flops 939524096 | bytes 4718592 | tf_op jit(solution)/shard_map/dot_general | solution.py:251
  42.0 0.0 copy-done.3
  42.0 0.0 copy-done.6
  42.0 0.0 copy-start.5
  42.0 1.3 fusion.13
  43.3 1.3 fusion.15
  44.6 2.8 %pad_maximum_fusion = f32[512,2688]{1,0:T(8,128)} fusion(f32[512,896]{1,0:T(8,128)S(1)} %fusion.15, f32[512,896]{1,0:T(8,128)S(1)} %fusion.14, f32[512,896]{1,0:T(8,128)S(1)} %fusion.13), kind=kLoop, calls=%fused_computation | loop fusion | flops 2752512 | bytes 11010048 | tf_op jit(solution)/shard_map/concatenate | solution.py:255
  47.3 60.0 %shard_map.87 = f32[64,2688]{1,0:T(8,128)} custom-call(f32[8,64,2688]{2,1,0:T(8,128)} %bitcast.16), custom_call_target="tpu_custom_call" | custom-call | tf_op jit(solution)/shard_map/pallas_call | solution.py:220
  107.4 1.3 fusion.9
  108.7 0.2 broadcast_in_dim.2
  108.9 34.8 %all_to_all.10 = bf16[8,64,2688]{2,1,0:T(8,128)(2,1)S(1)} all-to-all(bf16[8,64,2688]{2,1,0:T(8,128)(2,1)S(1)} %broadcast_in_dim.2), channel_id=1, replica_groups=mesh['dp'=2,'pipe'=8,'tensor'=16] {'pipe'}, dimensions={0} | all-to-all | bytes 5505024 | tf_op jit(solution)/shard_map/all_to_all | solution.py:28
  143.8 1.3 convolution_convert_fusion
  145.0 0.0 copy-start.4
  145.1 1.3 fusion.1
  146.3 0.2 copy-done.4
  146.5 1.3 add_convert_fusion
  147.9 0.2 pad_maximum_fusion.1
  148.0 53.2 %all_to_all.11 = bf16[16,32,2048]{2,1,0:T(8,128)(2,1)} all-to-all(bf16[16,32,2048]{2,1,0:T(8,128)(2,1)S(1)} %bitcast.17), channel_id=1, replica_groups=mesh['dp'=2,'pipe'=8,'tensor'=16] {'tensor'}, dimensions={0} | all-to-all | bytes 4194304 | tf_op jit(solution)/shard_map/all_to_all | solution.py:35
  201.2 2.0 reduce_sum.12
  203.2 0.7 fusion.12
  (8 shorter events, 0.0 us)
Async XLA Ops:
  0.6 42.6 %copy-start = (bf16[896,1024]{1,0:T(8,128)(2,1)S(1)}, bf16[896,1024]{1,0:T(8,128)(2,1)}, u32[]{:S(2)}) copy-start(bf16[896,1024]{1,0:T(8,128)(2,1)} %param.13) | copy-start | bytes 5505028
  38.7 3.2 %copy-start.3 = (bf16[1024,896]{1,0:T(8,128)(2,1)S(1)}, bf16[1024,896]{1,0:T(8,128)(2,1)}, u32[]{:S(2)}) copy-start(bf16[1024,896]{1,0:T(8,128)(2,1)} %param.11) | copy-start | bytes 5505028
  38.8 3.2 %copy-start.6 = (bf16[2,8,32,1024]{3,2,1,0:T(8,128)(2,1)S(1)}, bf16[2,8,32,1024]{3,2,1,0:T(8,128)(2,1)}, u32[]{:S(2)}) copy-start(bf16[2,8,32,1024]{3,2,1,0:T(8,128)(2,1)} %get-tuple-element.4) | copy-start | bytes 3145732
  42.0 1.3 copy-start.5
  47.3 60.0 %copy-start.1 = (bf16[64,896]{1,0:T(8,128)(2,1)S(1)}, bf16[64,896]{1,0:T(8,128)(2,1)}, u32[]{:S(2)}) copy-start(bf16[64,896]{1,0:T(8,128)(2,1)} %param.9) | copy-start | bytes 344068
  47.3 60.0 %copy-start.2 = (bf16[64,896]{1,0:T(8,128)(2,1)S(1)}, bf16[64,896]{1,0:T(8,128)(2,1)}, u32[]{:S(2)}) copy-start(bf16[64,896]{1,0:T(8,128)(2,1)} %param.10) | copy-start | bytes 344068
  145.0 1.5 copy-start.4

commit v9 on v8

--- a/solution.py
+++ b/solution.py
@@ -214,7 +214,7 @@
         cp.wait_send()
 
 
-def ring_sum(partial, axis, outer, cid, chunks=2):
+def ring_sum(partial, axis, outer, cid, chunks=4):
     count, rows, width = partial.shape
     half = rows // 2
     return pl.pallas_call(

time: 204 us -> 200 us (0.980)
  Pallas kernels: 96.4 us -> 93.1 us
    pallas_call x1, Pallas kernels: 60 us -> 56.7 us  [ring_sum(): pl.pallas_call(functools.partial(_ring_sum_kernel, axis, outer, chunks),...]
where the time goes in v9:
time: 200 us
  Pallas kernels  93.1 us (47%)
  blocking collectives  87.4 us (44%)
  matrix products  9.62 us (5%)
  other arithmetic  7.94 us (4%)
    pallas_call x1, Pallas kernels, ring_sum(): pl.pallas_call(functools.partial(_ring_sum_kernel, axis, outer, chunks),...  56.7 us
    all_to_all x1, blocking collectives, scatter_sum_rows(): got = lax.all_to_all(sent, axis, 0, 0, tiled=False)  52.7 us
    pallas_call x1, Pallas kernels, ring_gather(): pl.pallas_call(functools.partial(_ring_gather_kernel, axis, outer, inner,...  36.4 us
    all_to_all x1, blocking collectives, gather_rows(): got = lax.all_to_all(sent, axis, 0, 0, tiled=False)  34.6 us

profile of v9, /device:TPU:32, one launch (start us, length us, event | category | flops | bytes accessed | tf_op | source)
XLA Modules:
  0.0 199.9 jit_solution(6218272185521874854)
XLA Ops:
  0.6 0.0 copy-start
  0.6 1.7 pad_maximum_fusion.3.x_ref
  2.3 36.4 %shard_map.86 = (bf16[2,8,32,1024]{3,2,1,0:T(8,128)(2,1)}, bf16[2,8,32,1024]{3,2,1,0:T(8,128)(2,1)}) custom-call(bf16[2,32,1024]{2,1,0:T(8,128)(2,1)} %pad_maximum_fusion.3.x_ref), custom_call_target="tpu_custom_call" | custom-call | tf_op jit(solution)/shard_map/pallas_call | solution.py:132
  38.7 0.0 copy-start.3
  38.8 3.2 %fusion.14 = f32[512,896]{1,0:T(8,128)S(1)} fusion(bf16[512,1024]{1,0:T(8,128)(2,1)} %bitcast.24, bf16[1024,896]{1,0:T(8,128)(2,1)} %param.12), kind=kOutput, calls=%fused_computation.24 | convolution fusion | flops 939524096 | bytes 4718592 | tf_op jit(solution)/shard_map/dot_general | solution.py:251
  42.0 0.0 copy-done.3
  42.0 0.0 copy-done.6
  42.0 0.0 copy-start.5
  42.0 1.3 fusion.13
  43.3 1.3 fusion.15
  44.6 2.8 %pad_maximum_fusion = f32[512,2688]{1,0:T(8,128)} fusion(f32[512,896]{1,0:T(8,128)S(1)} %fusion.15, f32[512,896]{1,0:T(8,128)S(1)} %fusion.14, f32[512,896]{1,0:T(8,128)S(1)} %fusion.13), kind=kLoop, calls=%fused_computation | loop fusion | flops 2752512 | bytes 11010048 | tf_op jit(solution)/shard_map/concatenate | solution.py:255
  47.3 56.7 %shard_map.87 = f32[64,2688]{1,0:T(8,128)} custom-call(f32[8,64,2688]{2,1,0:T(8,128)} %bitcast.16), custom_call_target="tpu_custom_call" | custom-call | tf_op jit(solution)/shard_map/pallas_call | solution.py:220
  104.0 1.3 fusion.9
  105.4 0.2 broadcast_in_dim.2
  105.6 34.6 %all_to_all.10 = bf16[8,64,2688]{2,1,0:T(8,128)(2,1)S(1)} all-to-all(bf16[8,64,2688]{2,1,0:T(8,128)(2,1)S(1)} %broadcast_in_dim.2), channel_id=1, replica_groups=mesh['dp'=2,'pipe'=8,'tensor'=16] {'pipe'}, dimensions={0} | all-to-all | bytes 5505024 | tf_op jit(solution)/shard_map/all_to_all | solution.py:28
  140.2 1.3 convolution_convert_fusion
  141.5 0.0 copy-start.4
  141.5 1.3 fusion.1
  142.8 0.2 copy-done.4
  143.0 1.3 add_convert_fusion
  144.3 0.2 pad_maximum_fusion.1
  144.5 52.7 %all_to_all.11 = bf16[16,32,2048]{2,1,0:T(8,128)(2,1)} all-to-all(bf16[16,32,2048]{2,1,0:T(8,128)(2,1)S(1)} %bitcast.17), channel_id=1, replica_groups=mesh['dp'=2,'pipe'=8,'tensor'=16] {'tensor'}, dimensions={0} | all-to-all | bytes 4194304 | tf_op jit(solution)/shard_map/all_to_all | solution.py:35
  197.3 2.0 reduce_sum.12
  199.2 0.7 fusion.12
  (8 shorter events, 0.0 us)
Async XLA Ops:
  0.6 42.6 %copy-start = (bf16[896,1024]{1,0:T(8,128)(2,1)S(1)}, bf16[896,1024]{1,0:T(8,128)(2,1)}, u32[]{:S(2)}) copy-start(bf16[896,1024]{1,0:T(8,128)(2,1)} %param.13) | copy-start | bytes 5505028
  38.7 3.2 %copy-start.3 = (bf16[1024,896]{1,0:T(8,128)(2,1)S(1)}, bf16[1024,896]{1,0:T(8,128)(2,1)}, u32[]{:S(2)}) copy-start(bf16[1024,896]{1,0:T(8,128)(2,1)} %param.11) | copy-start | bytes 5505028
  38.8 3.2 %copy-start.6 = (bf16[2,8,32,1024]{3,2,1,0:T(8,128)(2,1)S(1)}, bf16[2,8,32,1024]{3,2,1,0:T(8,128)(2,1)}, u32[]{:S(2)}) copy-start(bf16[2,8,32,1024]{3,2,1,0:T(8,128)(2,1)} %get-tuple-element.4) | copy-start | bytes 3145732
  42.0 1.3 copy-start.5
  47.3 56.7 %copy-start.1 = (bf16[64,896]{1,0:T(8,128)(2,1)S(1)}, bf16[64,896]{1,0:T(8,128)(2,1)}, u32[]{:S(2)}) copy-start(bf16[64,896]{1,0:T(8,128)(2,1)} %param.9) | copy-start | bytes 344068
  47.3 56.7 %copy-start.2 = (bf16[64,896]{1,0:T(8,128)(2,1)S(1)}, bf16[64,896]{1,0:T(8,128)(2,1)}, u32[]{:S(2)}) copy-start(bf16[64,896]{1,0:T(8,128)(2,1)} %param.10) | copy-start | bytes 344068
  141.5 1.5 copy-start.4

commit v10 on v9

--- a/solution.py
+++ b/solution.py
@@ -36,7 +36,7 @@
     return got.astype(jnp.float32).sum(axis=0)
 
 
-def _ring_gather_kernel(axis, outer, inner, ring_on_inner, halves, x_ref, first_ref, second_ref, send_sems, recv_sems, swap_sems, local_sems):
+def _ring_gather_kernel(axis, outer, inner, ring_on_inner, halves, first_in, second_in, first_ref, second_ref, send_sems, recv_sems, swap_sems, local_sems):
     me = lax.axis_index(axis)
     o = me // inner
     i = me % inner
@@ -53,7 +53,8 @@
     partner = at(pos, 1 - other)
     up = at(lax.rem(pos + 1, ring), other)
     down = at(lax.rem(pos + ring - 1, ring), other)
-    rows = x_ref.shape[1]
+    ins = (first_in, second_in)
+    rows = first_in.shape[0]
     part = rows // halves
     steps = (ring // 2, (ring - 1) // 2)
 
@@ -66,11 +67,11 @@
     locals_ = []
     swaps = []
     for a in range(2):
-        c = pltpu.make_async_copy(x_ref.at[a], outs[a].at[other, pos], local_sems.at[a])
+        c = pltpu.make_async_copy(ins[a], outs[a].at[other, pos], local_sems.at[a])
         c.start()
         locals_.append(c)
         s = pltpu.make_async_remote_copy(
-            src_ref=x_ref.at[a], dst_ref=outs[a].at[other, pos],
+            src_ref=ins[a], dst_ref=outs[a].at[other, pos],
             send_sem=swap_sems.at[0, a], recv_sem=swap_sems.at[1, a],
             device_id={axis: partner}, device_id_type=MESH)
         s.start()
@@ -84,7 +85,7 @@
         half = other if which == 0 else 1 - other
         rs = pl.ds(r * part, part)
         if step == 1 and which == 0:
-            src = x_ref.at[a, rs]
+            src = ins[a].at[rs]
         else:
             src = outs[a].at[half, slot, rs]
         k = (((d * ring + step - 1) * 2 + which) * halves + r) * 2 + a
@@ -127,12 +128,11 @@
     rows, width = first.shape
     ring = inner if ring_on_inner else outer
     shape = (2, ring, rows, width)
-    x = jnp.stack([first, second])
     n_copies = 2 * ring * 2 * halves * 2
     f, s = pl.pallas_call(
         functools.partial(_ring_gather_kernel, axis, outer, inner, ring_on_inner, halves),
         out_shape=(jax.ShapeDtypeStruct(shape, first.dtype), jax.ShapeDtypeStruct(shape, second.dtype)),
-        in_specs=[pl.BlockSpec(memory_space=pltpu.VMEM)],
+        in_specs=[pl.BlockSpec(memory_space=pltpu.VMEM)] * 2,
         out_specs=(pl.BlockSpec(memory_space=pltpu.VMEM), pl.BlockSpec(memory_space=pltpu.VMEM)),
         scratch_shapes=[
             pltpu.SemaphoreType.DMA((n_copies,)),
@@ -141,7 +141,7 @@
             pltpu.SemaphoreType.DMA((2,)),
         ],
         compiler_params=pltpu.CompilerParams(collective_id=cid, has_side_effects=True),
-    )(x)
+    )(first, second)
     if ring_on_inner:
         return f.reshape(2 * ring * rows, width), s.reshape(2 * ring * rows, width)
     return (f.transpose(1, 0, 2, 3).reshape(2 * ring * rows, width),
@@ -234,6 +234,71 @@
     )(partial)
 
 
+def _exchange_kernel(plan, *refs):
+    k = len(plan)
+    ins, outs = refs[:k], refs[k:2 * k]
+    send_sems, recv_sems, local_sems = refs[2 * k:]
+    axes = {}
+    for axis, count, _ in plan:
+        axes[axis] = count
+    barrier = pltpu.get_barrier_semaphore()
+    total = 0
+    for axis, count in axes.items():
+        me = lax.axis_index(axis)
+        for d in range(1, count):
+            pl.semaphore_signal(barrier, inc=1, device_id={axis: lax.rem(me + d, count)}, device_id_type=MESH)
+        total += count - 1
+    pl.semaphore_wait(barrier, total)
+    started = []
+    for e, (axis, count, spread) in enumerate(plan):
+        me = lax.axis_index(axis)
+        src = ins[e] if spread else ins[e].at[me]
+        own = pltpu.make_async_copy(src, outs[e].at[me], local_sems.at[e])
+        own.start()
+        started.append(own)
+    remote = []
+    for d in range(1, max(c for _, c, _ in plan)):
+        for e, (axis, count, spread) in enumerate(plan):
+            if d >= count:
+                continue
+            me = lax.axis_index(axis)
+            peer = lax.rem(me + d, count)
+            src = ins[e] if spread else ins[e].at[peer]
+            c = pltpu.make_async_remote_copy(
+                src_ref=src, dst_ref=outs[e].at[me],
+                send_sem=send_sems.at[e, d - 1], recv_sem=recv_sems.at[e, d - 1],
+                device_id={axis: peer}, device_id_type=MESH)
+            c.start()
+            remote.append(c)
+    for c in started:
+        c.wait()
+    for c in remote:
+        c.wait_recv()
+    for c in remote:
+        c.wait_send()
+
+
+def exchange(items, cid):
+    plan = tuple((axis, count, spread) for _, axis, count, spread in items)
+    shapes = []
+    for x, axis, count, spread in items:
+        shape = (count,) + x.shape if spread else x.shape
+        shapes.append(jax.ShapeDtypeStruct(shape, x.dtype))
+    widest = max(count for _, _, count, _ in items)
+    return pl.pallas_call(
+        functools.partial(_exchange_kernel, plan),
+        out_shape=tuple(shapes),
+        in_specs=[pl.BlockSpec(memory_space=pl.ANY)] * len(items),
+        out_specs=tuple(pl.BlockSpec(memory_space=pl.ANY) for _ in items),
+        scratch_shapes=[
+            pltpu.SemaphoreType.DMA((len(items), widest - 1)),
+            pltpu.SemaphoreType.DMA((len(items), widest - 1)),
+            pltpu.SemaphoreType.DMA((len(items),)),
+        ],
+        compiler_params=pltpu.CompilerParams(collective_id=cid, has_side_effects=True),
+    )(*[x for x, _, _, _ in items])
+
+
 def per_device(
     forward_acts, backward_grad, stored_gate, stored_up, gate_weight, up_weight, down_weight
 ):
@@ -265,7 +330,9 @@
     hidden_part = (jax.nn.silu(gate_pre) * up_pre).astype(jnp.bfloat16)
     local_slopes = make_slopes(hidden_grad, stored_gate, stored_up)
 
-    rows = gather_rows(jnp.concatenate([hidden_part, local_slopes], axis=1), "pipe", n_pipe)
+    local_rows = jnp.concatenate([hidden_part, local_slopes], axis=1)
+    (rows,) = exchange([(local_rows, "pipe", n_pipe, True)], 2)
+    rows = rows.reshape(n_pipe * local_rows.shape[0], local_rows.shape[1])
     hidden = rows[:, :hidden_width]
     gate_slopes = rows[:, hidden_width : 2 * hidden_width]
     up_slopes = rows[:, 2 * hidden_width :]
@@ -274,9 +341,21 @@
     in_part = lax.dot_general(
         gate_slopes, gate_weight, contract_last, preferred_element_type=jnp.float32
     ) + lax.dot_general(up_slopes, up_weight, contract_last, preferred_element_type=jnp.float32)
-    finished = scatter_sum_rows(
-        jnp.concatenate([out_part, in_part], axis=1), "tensor", n_tensor, TENSOR_LINK
-    ).astype(jnp.bfloat16)
+    finishing = jnp.concatenate([out_part, in_part], axis=1)
+    (got,) = exchange(
+        [
+            (
+                finishing.reshape((n_tensor, finishing.shape[0] // n_tensor, finishing.shape[1])).astype(
+                    TENSOR_LINK
+                ),
+                "tensor",
+                n_tensor,
+                False,
+            )
+        ],
+        3,
+    )
+    finished = got.astype(jnp.float32).sum(axis=0).astype(jnp.bfloat16)
     return (finished[:, :model_width], finished[:, model_width:])
 
 

time: 200 us -> 201 us (level); the launches traced: 200 us -> 198 us
  blocking collectives: 87.4 us -> 0 us
  Pallas kernels: 93.1 us -> 177 us
    all_to_all x2 -> x0, blocking collectives: 87.4 us -> none  [the longest x1 52.7 us: scatter_sum_rows(): got = lax.all_to_all(sent, axis, 0, 0, tiled=False)]
    pallas_call x0 -> x2, Pallas kernels: none -> 83.6 us  [exchange(): pl.pallas_call(functools.partial(_exchange_kernel, plan), out_shape=tuple...]
    concatenate x2, other arithmetic: 0.21 us -> 2.3 us  [the longest x1 1.53 us: per_device(): finishing = jnp.concatenate([out_part, in_part], axis=1)]
where the time goes in v10:
time: 201 us; the launch traced here: 198 us
  Pallas kernels  177 us (88%)
  matrix products  10.3 us (5%)
  other arithmetic  8.4 us (4%)
    pallas_call x2, Pallas kernels, exchange(): pl.pallas_call(functools.partial(_exchange_kernel, plan), out_shape=tuple...  83.6 us
    pallas_call x1, Pallas kernels, ring_sum(): pl.pallas_call(functools.partial(_ring_sum_kernel, axis, outer, chunks),...  56.7 us
    pallas_call x1, Pallas kernels, ring_gather(): pl.pallas_call(functools.partial(_ring_gather_kernel, axis, outer, inner,...  36.6 us

profile of v10, /device:TPU:32, one launch (start us, length us, event | category | flops | bytes accessed | tf_op | source)
XLA Modules:
  0.0 197.5 jit_solution(9805729917519700698)
XLA Ops:
  0.6 0.0 copy-start
  0.6 36.6 %shard_map.86 = (bf16[2,8,32,1024]{3,2,1,0:T(8,128)(2,1)}, bf16[2,8,32,1024]{3,2,1,0:T(8,128)(2,1)}) custom-call(bf16[32,1024]{1,0:T(8,128)(2,1)} %first_in.1, bf16[32,1024]{1,0:T(8,128)(2,1)} %second_in.1), custom_call_target="tpu_custom_call" | custom-call | tf_op jit(solution)/shard_map/pallas_call | solution.py:132
  37.3 0.0 copy-start.6
  37.3 0.0 copy-start.8
  37.3 2.7 %fusion.15 = f32[512,896]{1,0:T(8,128)S(1)} fusion(bf16[512,1024]{1,0:T(8,128)(2,1)} %bitcast.21, bf16[896,1024]{1,0:T(8,128)(2,1)S(1)} %copy-done), kind=kOutput, calls=%fused_computation.24 | convolution fusion | flops 939524096 | bytes 4718592 | tf_op jit(solution)/shard_map/dot_general | solution.py:317
  40.0 0.0 copy-start.4
  40.0 1.2 fusion.14
  41.3 0.2 copy-done.4
  41.5 1.3 fusion.13
  42.8 2.8 %pad_maximum_fusion = f32[512,2688]{1,0:T(8,128)} fusion(f32[512,896]{1,0:T(8,128)S(1)} %fusion.15, f32[512,896]{1,0:T(8,128)S(1)} %fusion.14, f32[512,896]{1,0:T(8,128)S(1)} %fusion.13), kind=kLoop, calls=%fused_computation | loop fusion | flops 2752512 | bytes 11010048 | tf_op jit(solution)/shard_map/concatenate | solution.py:320
  45.5 56.7 %shard_map.87 = f32[64,2688]{1,0:T(8,128)} custom-call(f32[8,64,2688]{2,1,0:T(8,128)} %bitcast.14), custom_call_target="tpu_custom_call" | custom-call | tf_op jit(solution)/shard_map/pallas_call | solution.py:220
  102.2 1.3 fusion.9
  103.6 0.8 pad_maximum_fusion.2.refs_0_
  104.3 31.9 %shard_map.88 = bf16[8,64,2688]{2,1,0:T(8,128)(2,1)} custom-call(bf16[64,2688]{1,0:T(8,128)(2,1)} %pad_maximum_fusion.2.refs_0_), custom_call_target="tpu_custom_call" | custom-call | tf_op jit(solution)/shard_map/pallas_call | solution.py:288
  136.3 0.0 copy-start.5
  136.3 2.6 %convolution_convert_fusion = bf16[512,1024]{1,0:T(8,128)(2,1)S(1)} fusion(bf16[896,1024]{1,0:T(8,128)(2,1)S(1)} %copy-done, bf16[512,2688]{1,0:T(8,128)(2,1)} %bitcast.16), kind=kOutput, calls=%fused_computation.3 | convolution fusion | flops 940048384 | bytes 3801088 | tf_op jit(solution)/shard_map/dot_general | solution.py:340
  138.9 0.0 copy-start.7
  138.9 1.3 fusion.1
  140.2 0.2 copy-done.7
  140.4 1.3 add_convert_fusion
  141.7 1.5 pad_maximum_fusion.1
  143.2 51.6 %shard_map.89 = bf16[16,32,2048]{2,1,0:T(8,128)(2,1)} custom-call(bf16[16,32,2048]{2,1,0:T(8,128)(2,1)} %bitcast.15), custom_call_target="tpu_custom_call" | custom-call | tf_op jit(solution)/shard_map/pallas_call | solution.py:288
  194.9 2.0 %reduce_sum.12 = bf16[32,2048]{1,0:T(8,128)(2,1)S(1)} reduce(bf16[16,32,2048]{2,1,0:T(8,128)(2,1)} %shard_map.89, bf16[]{:T(256)} %constant.6.clone.1), dimensions={0}, to_apply=%region_0.1 | reduce | flops 983040 | bytes 2228226 | tf_op jit(solution)/shard_map/reduce_sum | solution.py:358
  196.9 0.7 fusion.12
  (10 shorter events, 0.0 us)
Async XLA Ops:
  0.6 36.6 %copy-start = (bf16[896,1024]{1,0:T(8,128)(2,1)S(1)}, bf16[896,1024]{1,0:T(8,128)(2,1)}, u32[]{:S(2)}) copy-start(bf16[896,1024]{1,0:T(8,128)(2,1)} %param.13) | copy-start | bytes 5505028
  37.3 2.7 %copy-start.6 = (bf16[1024,896]{1,0:T(8,128)(2,1)S(1)}, bf16[1024,896]{1,0:T(8,128)(2,1)}, u32[]{:S(2)}) copy-start(bf16[1024,896]{1,0:T(8,128)(2,1)} %param.12) | copy-start | bytes 5505028
  37.3 2.7 %copy-start.8 = (bf16[2,8,32,1024]{3,2,1,0:T(8,128)(2,1)S(1)}, bf16[2,8,32,1024]{3,2,1,0:T(8,128)(2,1)}, u32[]{:S(2)}) copy-start(bf16[2,8,32,1024]{3,2,1,0:T(8,128)(2,1)} %get-tuple-element.4) | copy-start | bytes 3145732
  40.0 1.5 copy-start.4
  45.5 56.7 %copy-start.2 = (bf16[64,896]{1,0:T(8,128)(2,1)S(1)}, bf16[64,896]{1,0:T(8,128)(2,1)}, u32[]{:S(2)}) copy-start(bf16[64,896]{1,0:T(8,128)(2,1)} %param.9) | copy-start | bytes 344068
  45.5 56.7 %copy-start.3 = (bf16[64,896]{1,0:T(8,128)(2,1)S(1)}, bf16[64,896]{1,0:T(8,128)(2,1)}, u32[]{:S(2)}) copy-start(bf16[64,896]{1,0:T(8,128)(2,1)} %param.10) | copy-start | bytes 344068
  136.3 2.6 %copy-start.1 = (bf16[8,64,2688]{2,1,0:T(8,128)(2,1)S(1)}, bf16[8,64,2688]{2,1,0:T(8,128)(2,1)}, u32[]{:S(2)}) copy-start(bf16[8,64,2688]{2,1,0:T(8,128)(2,1)} %shard_map.88) | copy-start | bytes 8257540
  136.3 2.6 %copy-start.5 = (bf16[1024,896]{1,0:T(8,128)(2,1)S(1)}, bf16[1024,896]{1,0:T(8,128)(2,1)}, u32[]{:S(2)}) copy-start(bf16[1024,896]{1,0:T(8,128)(2,1)} %param.11) | copy-start | bytes 5505028
  138.9 1.5 copy-start.7

commit v11 on v10

--- a/solution.py
+++ b/solution.py
@@ -7,7 +7,6 @@
 from jax.experimental.pallas import tpu as pltpu
 from jax.sharding import PartitionSpec as P
 
-PIPE_LINK = jnp.float32
 TENSOR_LINK = jnp.bfloat16
 MESH = pl.DeviceIdType.MESH
 
@@ -21,19 +20,6 @@
     )
     up_slope = (hidden_grad * gate_wide * sigma).astype(jnp.bfloat16)
     return jnp.concatenate([gate_slope, up_slope], axis=1)
-
-
-def gather_rows(block, axis, count):
-    sent = jnp.broadcast_to(block[None], (count,) + block.shape)
-    got = lax.all_to_all(sent, axis, 0, 0, tiled=False)
-    return got.reshape((count * block.shape[0],) + block.shape[1:])
-
-
-def scatter_sum_rows(partial, axis, count, link_dtype):
-    rows = partial.shape[0] // count
-    sent = partial.reshape((count, rows) + partial.shape[1:]).astype(link_dtype)
-    got = lax.all_to_all(sent, axis, 0, 0, tiled=False)
-    return got.astype(jnp.float32).sum(axis=0)
 
 
 def _ring_gather_kernel(axis, outer, inner, ring_on_inner, halves, first_in, second_in, first_ref, second_ref, send_sems, recv_sems, swap_sems, local_sems):
@@ -148,7 +134,13 @@
             s.transpose(1, 0, 2, 3).reshape(2 * ring * rows, width))
 
 
-def _ring_sum_kernel(axis, outer, chunks, x_ref, out_ref, send_buf, recv_buf, swap_buf, send_sems, recv_sems, swap_sems):
+def _ring_sum_kernel(axis, outer, chunks, count, *refs):
+    xs = refs[:count]
+    outs = refs[count:2 * count]
+    send_bufs = refs[2 * count:3 * count]
+    recv_bufs = refs[3 * count:4 * count]
+    swap_bufs = refs[4 * count:5 * count]
+    send_sems, recv_sems, swap_sems = refs[5 * count:]
     me = lax.axis_index(axis)
     y = me // 2
     x = me % 2
@@ -156,7 +148,7 @@
     up = lax.rem(y + 1, ring) * 2 + x
     down = lax.rem(y + ring - 1, ring) * 2 + x
     partner = y * 2 + 1 - x
-    rows = x_ref.shape[1]
+    rows = xs[0].shape[1]
     half = rows // 2
     part = half // chunks
 
@@ -174,64 +166,74 @@
     for step in range(1, ring):
         for c in range(chunks):
             for d in range(2):
-                rs = pl.ds(d * half + c * part, part)
-                blocks = pl.ds(dest(d, step) * 2, 2)
-                if step == 1:
-                    src = x_ref.at[blocks, rs]
-                else:
-                    copies[(d, step - 1, c)].wait_recv()
-                    send_buf[d, step, :, pl.ds(c * part, part)] = (
-                        recv_buf[d, step - 1, :, pl.ds(c * part, part)] + x_ref[blocks, rs]
-                    )
-                    src = send_buf.at[d, step, :, pl.ds(c * part, part)]
-                cp = pltpu.make_async_remote_copy(
-                    src_ref=src, dst_ref=recv_buf.at[d, step, :, pl.ds(c * part, part)],
-                    send_sem=send_sems.at[d, step, c], recv_sem=recv_sems.at[d, step, c],
-                    device_id={axis: targets[d]}, device_id_type=MESH)
-                cp.start()
-                copies[(d, step, c)] = cp
+                for t in range(count):
+                    rs = pl.ds(d * half + c * part, part)
+                    local = pl.ds(c * part, part)
+                    blocks = pl.ds(dest(d, step) * 2, 2)
+                    if step == 1:
+                        src = xs[t].at[blocks, rs]
+                    else:
+                        copies[(d, step - 1, c, t)].wait_recv()
+                        send_bufs[t][d, step, :, local] = (
+                            recv_bufs[t][d, step - 1, :, local] + xs[t][blocks, rs]
+                        )
+                        src = send_bufs[t].at[d, step, :, local]
+                    cp = pltpu.make_async_remote_copy(
+                        src_ref=src, dst_ref=recv_bufs[t].at[d, step, :, local],
+                        send_sem=send_sems.at[t, d, step, c], recv_sem=recv_sems.at[t, d, step, c],
+                        device_id={axis: targets[d]}, device_id_type=MESH)
+                    cp.start()
+                    copies[(d, step, c, t)] = cp
     swaps = []
     for c in range(chunks):
         for d in range(2):
-            rs = pl.ds(d * half + c * part, part)
-            local = pl.ds(c * part, part)
-            copies[(d, ring - 1, c)].wait_recv()
-            swap_buf[0, d, local] = recv_buf[d, ring - 1, 1 - x, local] + x_ref[y * 2 + 1 - x, rs]
-            out_ref[rs] = recv_buf[d, ring - 1, x, local] + x_ref[y * 2 + x, rs]
-            sw = pltpu.make_async_remote_copy(
-                src_ref=swap_buf.at[0, d, local], dst_ref=swap_buf.at[1, d, local],
-                send_sem=swap_sems.at[0, d, c], recv_sem=swap_sems.at[1, d, c],
-                device_id={axis: partner}, device_id_type=MESH)
-            sw.start()
-            swaps.append((d, c, sw))
-    for d, c, sw in swaps:
+            for t in range(count):
+                rs = pl.ds(d * half + c * part, part)
+                local = pl.ds(c * part, part)
+                copies[(d, ring - 1, c, t)].wait_recv()
+                swap_bufs[t][0, d, local] = recv_bufs[t][d, ring - 1, 1 - x, local] + xs[t][y * 2 + 1 - x, rs]
+                outs[t][rs] = recv_bufs[t][d, ring - 1, x, local] + xs[t][y * 2 + x, rs]
+                sw = pltpu.make_async_remote_copy(
+                    src_ref=swap_bufs[t].at[0, d, local], dst_ref=swap_bufs[t].at[1, d, local],
+                    send_sem=swap_sems.at[t, 0, d, c], recv_sem=swap_sems.at[t, 1, d, c],
+                    device_id={axis: partner}, device_id_type=MESH)
+                sw.start()
+                swaps.append((d, c, t, sw))
+    for d, c, t, sw in swaps:
         rs = pl.ds(d * half + c * part, part)
         sw.wait_recv()
-        out_ref[rs] = out_ref[rs] + swap_buf[1, d, pl.ds(c * part, part)]
-    for d, c, sw in swaps:
+        outs[t][rs] = outs[t][rs] + swap_bufs[t][1, d, pl.ds(c * part, part)]
+    for d, c, t, sw in swaps:
         sw.wait_send()
     for cp in copies.values():
         cp.wait_send()
 
 
-def ring_sum(partial, axis, outer, cid, chunks=4):
-    count, rows, width = partial.shape
+def ring_sum(partials, axis, outer, cid, chunks=4):
+    count = len(partials)
+    rows = partials[0].shape[1]
     half = rows // 2
+    scratch = []
+    for kind in range(3):
+        for p in partials:
+            width = p.shape[2]
+            if kind < 2:
+                scratch.append(pltpu.VMEM((2, outer, 2, half, width), jnp.float32))
+            else:
+                scratch.append(pltpu.VMEM((2, 2, half, width), jnp.float32))
+    scratch += [
+        pltpu.SemaphoreType.DMA((count, 2, outer, chunks)),
+        pltpu.SemaphoreType.DMA((count, 2, outer, chunks)),
+        pltpu.SemaphoreType.DMA((count, 2, 2, chunks)),
+    ]
     return pl.pallas_call(
-        functools.partial(_ring_sum_kernel, axis, outer, chunks),
-        out_shape=jax.ShapeDtypeStruct((rows, width), jnp.float32),
-        in_specs=[pl.BlockSpec(memory_space=pltpu.VMEM)],
-        out_specs=pl.BlockSpec(memory_space=pltpu.VMEM),
-        scratch_shapes=[
-            pltpu.VMEM((2, outer, 2, half, width), jnp.float32),
-            pltpu.VMEM((2, outer, 2, half, width), jnp.float32),
-            pltpu.VMEM((2, 2, half, width), jnp.float32),
-            pltpu.SemaphoreType.DMA((2, outer, chunks)),
-            pltpu.SemaphoreType.DMA((2, outer, chunks)),
-            pltpu.SemaphoreType.DMA((2, 2, chunks)),
-        ],
+        functools.partial(_ring_sum_kernel, axis, outer, chunks, count),
+        out_shape=tuple(jax.ShapeDtypeStruct((rows, p.shape[2]), jnp.float32) for p in partials),
+        in_specs=[pl.BlockSpec(memory_space=pltpu.VMEM)] * count,
+        out_specs=tuple(pl.BlockSpec(memory_space=pltpu.VMEM) for _ in partials),
+        scratch_shapes=scratch,
         compiler_params=pltpu.CompilerParams(collective_id=cid, has_side_effects=True, vmem_limit_bytes=60 * 1024 * 1024),
-    )(partial)
+    )(*partials)
 
 
 def _exchange_kernel(plan, *refs):
@@ -317,16 +319,12 @@
     grad_part = lax.dot_general(
         whole_grad, down_weight, contract_last, preferred_element_type=jnp.float32
     )
-    partials = jnp.concatenate([gate_part, up_part, grad_part], axis=1)
-    summed = ring_sum(
-        partials.reshape((n_pipe, partials.shape[0] // n_pipe, partials.shape[1])),
+    gate_pre, up_pre, hidden_grad = ring_sum(
+        [p.reshape((n_pipe, p.shape[0] // n_pipe, p.shape[1])) for p in (gate_part, up_part, grad_part)],
         "pipe",
         n_pipe // 2,
         1,
     )
-    gate_pre = summed[:, :hidden_width]
-    up_pre = summed[:, hidden_width : 2 * hidden_width]
-    hidden_grad = summed[:, 2 * hidden_width :]
     hidden_part = (jax.nn.silu(gate_pre) * up_pre).astype(jnp.bfloat16)
     local_slopes = make_slopes(hidden_grad, stored_gate, stored_up)
 

time: 201 us -> 203 us (level)
  matrix products: 10.3 us -> 14.7 us
  other arithmetic: 8.4 us -> 5.61 us
    dot_general x1, matrix products: 1.25 us -> 4.41 us  [per_device(): up_part = jnp.dot(whole_acts, up_weight, preferred_element_type=jnp.float32)]
    concatenate x1 -> x0, other arithmetic: 2.78 us -> none  [per_device(): partials = jnp.concatenate([gate_part, up_part, grad_part], axis=1)]
where the time goes in v11:
time: 203 us; the launch traced here: 200 us
  Pallas kernels  178 us (88%)
  matrix products  14.7 us (7%)
  other arithmetic  5.61 us (3%)
    pallas_call x2, Pallas kernels, exchange(): pl.pallas_call(functools.partial(_exchange_kernel, plan), out_shape=tuple...  83.9 us
    pallas_call x1, Pallas kernels, ring_sum(): pl.pallas_call(functools.partial(_ring_sum_kernel, axis, outer, chunks, c...  57.3 us
    pallas_call x1, Pallas kernels, ring_gather(): pl.pallas_call(functools.partial(_ring_gather_kernel, axis, outer, inner,...  36.6 us
    dot_general x1, matrix products, per_device(): up_part = jnp.dot(whole_acts, up_weight, preferred_element_type=jnp.float32)  4.41 us

profile of v11, /device:TPU:32, one launch (start us, length us, event | category | flops | bytes accessed | tf_op | source)
XLA Modules:
  0.0 199.7 jit_solution(8098577958813970461)
XLA Ops:
  0.6 0.0 copy-start
  0.6 36.6 %shard_map.86 = (bf16[2,8,32,1024]{3,2,1,0:T(8,128)(2,1)}, bf16[2,8,32,1024]{3,2,1,0:T(8,128)(2,1)}) custom-call(bf16[32,1024]{1,0:T(8,128)(2,1)} %first_in.1, bf16[32,1024]{1,0:T(8,128)(2,1)} %second_in.1), custom_call_target="tpu_custom_call" | custom-call | tf_op jit(solution)/shard_map/pallas_call | solution.py:118
  37.3 4.4 %fusion.2.refs_1_ = f32[8,64,896]{2,1,0:T(8,128)} fusion(bf16[8,64,1024]{2,1,0:T(8,128)(2,1)} %bitcast.24, bf16[1024,896]{1,0:T(8,128)(2,1)} %param.12), kind=kOutput, calls=%fused_computation.4 | convolution fusion | flops 939524096 | bytes 4718592 | tf_op jit(solution)/shard_map/dot_general | solution.py:318
  41.7 0.0 copy-done.8
  41.7 2.5 %fusion.4.refs_0_ = f32[8,64,896]{2,1,0:T(8,128)} fusion(bf16[8,64,1024]{2,1,0:T(8,128)(2,1)S(1)} %bitcast.25, bf16[1024,896]{1,0:T(8,128)(2,1)S(1)} %copy-done), kind=kOutput, calls=%fused_computation.6 | convolution fusion | flops 939524096 | bytes 4718592 | tf_op jit(solution)/shard_map/dot_general | solution.py:317
  44.2 2.6 %fusion.refs_2_ = f32[8,64,896]{2,1,0:T(8,128)} fusion(bf16[8,64,1024]{2,1,0:T(8,128)(2,1)S(1)} %bitcast.23, bf16[896,1024]{1,0:T(8,128)(2,1)S(1)} %copy-done.5), kind=kOutput, calls=%fused_computation.2 | convolution fusion | flops 939524096 | bytes 4718592 | tf_op jit(solution)/shard_map/dot_general | solution.py:319
  46.8 57.3 %shard_map.87 = (f32[64,896]{1,0:T(8,128)}, f32[64,896]{1,0:T(8,128)}, f32[64,896]{1,0:T(8,128)}) custom-call(f32[8,64,896]{2,1,0:T(8,128)} %fusion.4.refs_0_, f32[8,64,896]{2,1,0:T(8,128)} %fusion.2.refs_1_, f32[8,64,896]{2,1,0:T(8,128)} %fusion.refs_2_), custom_call_target="tpu_custom_call" | custom-call | tf_op jit(solution)/shard_map/pallas_call | solution.py:229
  104.1 0.0 copy-done.2
  104.1 0.0 copy-done.3
  104.1 1.3 fusion.15
  105.5 0.8 pad_maximum_fusion.1.refs_0_
  106.2 32.2 %shard_map.88 = bf16[8,64,2688]{2,1,0:T(8,128)(2,1)} custom-call(bf16[64,2688]{1,0:T(8,128)(2,1)} %pad_maximum_fusion.1.refs_0_), custom_call_target="tpu_custom_call" | custom-call | tf_op jit(solution)/shard_map/pallas_call | solution.py:290
  138.5 0.0 copy-start.4
  138.5 2.6 %fusion.7 = f32[512,1024]{1,0:T(8,128)S(1)} fusion(bf16[1024,896]{1,0:T(8,128)(2,1)S(1)} %copy-done, bf16[512,2688]{1,0:T(8,128)(2,1)} %bitcast.20), kind=kOutput, calls=%fused_computation.10 | convolution fusion | flops 939524096 | bytes 4849664 | tf_op jit(solution)/shard_map/dot_general | solution.py:339
  141.1 0.0 copy-done.1
  141.1 0.0 copy-done.4
  141.1 0.0 copy-start.6
  141.1 1.3 add_convert_fusion
  142.5 0.2 copy-done.6
  142.6 1.3 convolution_convert_fusion
  143.9 1.5 pad_maximum_fusion
  145.4 51.6 %shard_map.89 = bf16[16,32,2048]{2,1,0:T(8,128)(2,1)} custom-call(bf16[16,32,2048]{2,1,0:T(8,128)(2,1)} %bitcast.19), custom_call_target="tpu_custom_call" | custom-call | tf_op jit(solution)/shard_map/pallas_call | solution.py:290
  197.1 2.0 reduce_sum.12
  199.1 0.7 fusion.18
  (9 shorter events, 0.0 us)
Async XLA Ops:
  0.6 41.0 %copy-start = (bf16[1024,896]{1,0:T(8,128)(2,1)S(1)}, bf16[1024,896]{1,0:T(8,128)(2,1)}, u32[]{:S(2)}) copy-start(bf16[1024,896]{1,0:T(8,128)(2,1)} %param.11) | copy-start | bytes 5505028
  37.2 4.4 %copy-start.8 = (bf16[2,8,32,1024]{3,2,1,0:T(8,128)(2,1)S(1)}, bf16[2,8,32,1024]{3,2,1,0:T(8,128)(2,1)}, u32[]{:S(2)}) copy-start(bf16[2,8,32,1024]{3,2,1,0:T(8,128)(2,1)} %get-tuple-element.7) | copy-start | bytes 3145732
  41.7 2.5 %copy-start.5 = (bf16[896,1024]{1,0:T(8,128)(2,1)S(1)}, bf16[896,1024]{1,0:T(8,128)(2,1)}, u32[]{:S(2)}) copy-start(bf16[896,1024]{1,0:T(8,128)(2,1)} %param.13) | copy-start | bytes 5505028
  41.7 2.5 %copy-start.7 = (bf16[2,8,32,1024]{3,2,1,0:T(8,128)(2,1)S(1)}, bf16[2,8,32,1024]{3,2,1,0:T(8,128)(2,1)}, u32[]{:S(2)}) copy-start(bf16[2,8,32,1024]{3,2,1,0:T(8,128)(2,1)} %get-tuple-element.8) | copy-start | bytes 3145732
  46.8 57.3 %copy-start.2 = (bf16[64,896]{1,0:T(8,128)(2,1)S(1)}, bf16[64,896]{1,0:T(8,128)(2,1)}, u32[]{:S(2)}) copy-start(bf16[64,896]{1,0:T(8,128)(2,1)} %param.9) | copy-start | bytes 344068
  46.8 57.3 %copy-start.3 = (bf16[64,896]{1,0:T(8,128)(2,1)S(1)}, bf16[64,896]{1,0:T(8,128)(2,1)}, u32[]{:S(2)}) copy-start(bf16[64,896]{1,0:T(8,128)(2,1)} %param.10) | copy-start | bytes 344068
  138.5 2.6 %copy-start.1 = (bf16[8,64,2688]{2,1,0:T(8,128)(2,1)S(1)}, bf16[8,64,2688]{2,1,0:T(8,128)(2,1)}, u32[]{:S(2)}) copy-start(bf16[8,64,2688]{2,1,0:T(8,128)(2,1)} %shard_map.88) | copy-start | bytes 8257540
  138.5 2.6 %copy-start.4 = (bf16[1024,896]{1,0:T(8,128)(2,1)S(1)}, bf16[1024,896]{1,0:T(8,128)(2,1)}, u32[]{:S(2)}) copy-start(bf16[1024,896]{1,0:T(8,128)(2,1)} %param.12) | copy-start | bytes 5505028
  141.1 1.5 copy-start.6

commit v12 on v10

--- a/solution.py
+++ b/solution.py
@@ -7,7 +7,6 @@
 from jax.experimental.pallas import tpu as pltpu
 from jax.sharding import PartitionSpec as P
 
-PIPE_LINK = jnp.float32
 TENSOR_LINK = jnp.bfloat16
 MESH = pl.DeviceIdType.MESH
 
@@ -21,19 +20,6 @@
     )
     up_slope = (hidden_grad * gate_wide * sigma).astype(jnp.bfloat16)
     return jnp.concatenate([gate_slope, up_slope], axis=1)
-
-
-def gather_rows(block, axis, count):
-    sent = jnp.broadcast_to(block[None], (count,) + block.shape)
-    got = lax.all_to_all(sent, axis, 0, 0, tiled=False)
-    return got.reshape((count * block.shape[0],) + block.shape[1:])
-
-
-def scatter_sum_rows(partial, axis, count, link_dtype):
-    rows = partial.shape[0] // count
-    sent = partial.reshape((count, rows) + partial.shape[1:]).astype(link_dtype)
-    got = lax.all_to_all(sent, axis, 0, 0, tiled=False)
-    return got.astype(jnp.float32).sum(axis=0)
 
 
 def _ring_gather_kernel(axis, outer, inner, ring_on_inner, halves, first_in, second_in, first_ref, second_ref, send_sems, recv_sems, swap_sems, local_sems):
@@ -330,33 +316,29 @@
     hidden_part = (jax.nn.silu(gate_pre) * up_pre).astype(jnp.bfloat16)
     local_slopes = make_slopes(hidden_grad, stored_gate, stored_up)
 
-    local_rows = jnp.concatenate([hidden_part, local_slopes], axis=1)
-    (rows,) = exchange([(local_rows, "pipe", n_pipe, True)], 2)
-    rows = rows.reshape(n_pipe * local_rows.shape[0], local_rows.shape[1])
-    hidden = rows[:, :hidden_width]
-    gate_slopes = rows[:, hidden_width : 2 * hidden_width]
-    up_slopes = rows[:, 2 * hidden_width :]
+    got_hidden, got_slopes = exchange(
+        [(hidden_part, "pipe", n_pipe, True), (local_slopes, "pipe", n_pipe, True)], 2
+    )
+    hidden = got_hidden.reshape(n_pipe * hidden_part.shape[0], hidden_width)
+    all_slopes = got_slopes.reshape(n_pipe * local_slopes.shape[0], 2 * hidden_width)
+    gate_slopes = all_slopes[:, :hidden_width]
+    up_slopes = all_slopes[:, hidden_width:]
 
     out_part = jnp.dot(hidden, down_weight, preferred_element_type=jnp.float32)
     in_part = lax.dot_general(
         gate_slopes, gate_weight, contract_last, preferred_element_type=jnp.float32
     ) + lax.dot_general(up_slopes, up_weight, contract_last, preferred_element_type=jnp.float32)
-    finishing = jnp.concatenate([out_part, in_part], axis=1)
-    (got,) = exchange(
-        [
-            (
-                finishing.reshape((n_tensor, finishing.shape[0] // n_tensor, finishing.shape[1])).astype(
-                    TENSOR_LINK
-                ),
-                "tensor",
-                n_tensor,
-                False,
-            )
-        ],
-        3,
-    )
-    finished = got.astype(jnp.float32).sum(axis=0).astype(jnp.bfloat16)
-    return (finished[:, :model_width], finished[:, model_width:])
+    def blocks(partial):
+        return partial.reshape((n_tensor, partial.shape[0] // n_tensor, partial.shape[1])).astype(
+            TENSOR_LINK
+        )
+
+    got_out, got_in = exchange(
+        [(blocks(out_part), "tensor", n_tensor, False), (blocks(in_part), "tensor", n_tensor, False)], 3
+    )
+    layer_output = got_out.astype(jnp.float32).sum(axis=0).astype(jnp.bfloat16)
+    input_grad = got_in.astype(jnp.float32).sum(axis=0).astype(jnp.bfloat16)
+    return (layer_output, input_grad)
 
 
 def solution(mesh):

time: 201 us -> 203 us (level)
  no operation moved by 1% of the time
where the time goes in v12:
time: 203 us; the launch traced here: 199 us
  Pallas kernels  177 us (87%)
  matrix products  12.3 us (6%)
  other arithmetic  8.45 us (4%)
    pallas_call x2, Pallas kernels, exchange(): pl.pallas_call(functools.partial(_exchange_kernel, plan), out_shape=tuple...  84.1 us
    pallas_call x1, Pallas kernels, ring_sum(): pl.pallas_call(functools.partial(_ring_sum_kernel, axis, outer, chunks),...  56.7 us
    pallas_call x1, Pallas kernels, ring_gather(): pl.pallas_call(functools.partial(_ring_gather_kernel, axis, outer, inner,...  36.6 us

profile of v12, /device:TPU:32, one launch (start us, length us, event | category | flops | bytes accessed | tf_op | source)
XLA Modules:
  0.0 199.4 jit_solution(8516643604316866242)
XLA Ops:
  0.6 0.0 copy-start
  0.6 36.6 %shard_map.86 = (bf16[2,8,32,1024]{3,2,1,0:T(8,128)(2,1)}, bf16[2,8,32,1024]{3,2,1,0:T(8,128)(2,1)}) custom-call(bf16[32,1024]{1,0:T(8,128)(2,1)} %first_in.1, bf16[32,1024]{1,0:T(8,128)(2,1)} %second_in.1), custom_call_target="tpu_custom_call" | custom-call | tf_op jit(solution)/shard_map/pallas_call | solution.py:118
  37.3 0.0 copy-start.6
  37.3 2.7 %fusion.18 = f32[512,896]{1,0:T(8,128)S(1)} fusion(bf16[512,1024]{1,0:T(8,128)(2,1)} %bitcast.26, bf16[896,1024]{1,0:T(8,128)(2,1)S(1)} %copy-done), kind=kOutput, calls=%fused_computation.23 | convolution fusion | flops 939524096 | bytes 4718592 | tf_op jit(solution)/shard_map/dot_general | solution.py:303
  40.0 0.0 copy-start.4
  40.0 1.2 fusion.17
  41.3 0.2 copy-done.4
  41.5 1.3 fusion.16
  42.8 2.8 %pad_maximum_fusion = f32[512,2688]{1,0:T(8,128)} fusion(f32[512,896]{1,0:T(8,128)S(1)} %fusion.18, f32[512,896]{1,0:T(8,128)S(1)} %fusion.17, f32[512,896]{1,0:T(8,128)S(1)} %fusion.16), kind=kLoop, calls=%fused_computation | loop fusion | flops 2752512 | bytes 11010048 | tf_op jit(solution)/shard_map/concatenate | solution.py:306
  45.5 56.7 %shard_map.87 = f32[64,2688]{1,0:T(8,128)} custom-call(f32[8,64,2688]{2,1,0:T(8,128)} %bitcast.20), custom_call_target="tpu_custom_call" | custom-call | tf_op jit(solution)/shard_map/pallas_call | solution.py:206
  102.2 0.0 copy-done.2
  102.2 0.0 copy-done.3
  102.2 2.0 fusion.13
  104.2 0.7 pad_maximum_fusion.1.refs_1_
  104.9 32.1 %shard_map.88 = (bf16[8,64,896]{2,1,0:T(8,128)(2,1)}, bf16[8,64,1792]{2,1,0:T(8,128)(2,1)}) custom-call(bf16[64,896]{1,0:T(8,128)(2,1)} %get-tuple-element.16.refs_0_, bf16[64,1792]{1,0:T(8,128)(2,1)} %pad_maximum_fusion.1.refs_1_), custom_call_target="tpu_custom_call" | custom-call | tf_op jit(solution)/shard_map/pallas_call | solution.py:274
  137.0 0.0 copy-start.5
  137.0 3.6 %fusion.2.refs_0_ = bf16[16,32,1024]{2,1,0:T(8,128)(2,1)} fusion(bf16[16,32,896]{2,1,0:T(8,128)(2,1)} %bitcast.27, bf16[896,1024]{1,0:T(8,128)(2,1)S(1)} %copy-done), kind=kOutput, calls=%fused_computation.4 | convolution fusion | flops 940048384 | bytes 3801088 | tf_op jit(solution)/shard_map/dot_general | solution.py:327
  140.6 0.0 copy-done.5
  140.6 1.3 fusion.6
  141.9 0.2 copy-done.7
  142.1 2.3 %add_convert_fusion = bf16[512,1024]{1,0:T(8,128)(2,1)} fusion(f32[512,1024]{1,0:T(8,128)S(1)} %fusion.6, bf16[1024,896]{1,0:T(8,128)(2,1)S(1)} %copy-done.7, bf16[512,1792]{1,0:T(8,128)(2,1)S(1)} %bitcast.23), kind=kOutput, calls=%fused_computation.1 | convolution fusion | flops 940572672 | bytes 5898240 | tf_op jit(solution)/shard_map/dot_general | solution.py:330
  144.4 52.0 %shard_map.89 = (bf16[16,32,1024]{2,1,0:T(8,128)(2,1)}, bf16[16,32,1024]{2,1,0:T(8,128)(2,1)}) custom-call(bf16[16,32,1024]{2,1,0:T(8,128)(2,1)} %fusion.2.refs_0_, bf16[16,32,1024]{2,1,0:T(8,128)(2,1)} %bitcast.21), custom_call_target="tpu_custom_call" | custom-call | tf_op jit(solution)/shard_map/pallas_call | solution.py:274
  196.4 2.1 %reduce_sum.24 = bf16[32,1024]{1,0:T(8,128)(2,1)} reduce(bf16[16,32,1024]{2,1,0:T(8,128)(2,1)} %get-tuple-element.12, bf16[]{:T(256)} %constant.7.clone.1), dimensions={0}, to_apply=%region_0.1 | reduce | flops 491520 | bytes 1114114 | tf_op jit(solution)/shard_map/reduce_sum | solution.py:339
  198.6 0.8 reduce_sum.25
  (11 shorter events, 0.0 us)
Async XLA Ops:
  0.6 36.7 %copy-start = (bf16[896,1024]{1,0:T(8,128)(2,1)S(1)}, bf16[896,1024]{1,0:T(8,128)(2,1)}, u32[]{:S(2)}) copy-start(bf16[896,1024]{1,0:T(8,128)(2,1)} %param.13) | copy-start | bytes 5505028
  37.3 2.7 %copy-start.6 = (bf16[1024,896]{1,0:T(8,128)(2,1)S(1)}, bf16[1024,896]{1,0:T(8,128)(2,1)}, u32[]{:S(2)}) copy-start(bf16[1024,896]{1,0:T(8,128)(2,1)} %param.12) | copy-start | bytes 5505028
  37.3 2.7 %copy-start.9 = (bf16[2,8,32,1024]{3,2,1,0:T(8,128)(2,1)S(1)}, bf16[2,8,32,1024]{3,2,1,0:T(8,128)(2,1)}, u32[]{:S(2)}) copy-start(bf16[2,8,32,1024]{3,2,1,0:T(8,128)(2,1)} %get-tuple-element.8) | copy-start | bytes 3145732
  40.0 1.5 copy-start.4
  45.5 56.7 %copy-start.2 = (bf16[64,896]{1,0:T(8,128)(2,1)S(1)}, bf16[64,896]{1,0:T(8,128)(2,1)}, u32[]{:S(2)}) copy-start(bf16[64,896]{1,0:T(8,128)(2,1)} %param.9) | copy-start | bytes 344068
  45.5 56.7 %copy-start.3 = (bf16[64,896]{1,0:T(8,128)(2,1)S(1)}, bf16[64,896]{1,0:T(8,128)(2,1)}, u32[]{:S(2)}) copy-start(bf16[64,896]{1,0:T(8,128)(2,1)} %param.10) | copy-start | bytes 344068
  137.0 3.6 %copy-start.5 = (bf16[1024,896]{1,0:T(8,128)(2,1)S(1)}, bf16[1024,896]{1,0:T(8,128)(2,1)}, u32[]{:S(2)}) copy-start(bf16[1024,896]{1,0:T(8,128)(2,1)} %param.11) | copy-start | bytes 5505028
  137.0 3.6 %copy-start.8 = (bf16[8,64,1792]{2,1,0:T(8,128)(2,1)S(1)}, bf16[8,64,1792]{2,1,0:T(8,128)(2,1)}, u32[]{:S(2)}) copy-start(bf16[8,64,1792]{2,1,0:T(8,128)(2,1)} %get-tuple-element.11) | copy-start | bytes 5505028
  140.6 1.5 copy-start.7
  196.4 2.2 %copy-start.1 = (bf16[16,32,1024]{2,1,0:T(8,128)(2,1)S(1)}, bf16[16,32,1024]{2,1,0:T(8,128)(2,1)}, u32[]{:S(2)}) copy-start(bf16[16,32,1024]{2,1,0:T(8,128)(2,1)} %get-tuple-element.13) | copy-start | bytes 3145732

commit v13 on v9

--- a/solution.py
+++ b/solution.py
@@ -55,7 +55,12 @@
     down = at(lax.rem(pos + ring - 1, ring), other)
     rows = x_ref.shape[1]
     part = rows // halves
-    steps = (ring // 2, (ring - 1) // 2)
+    steps = (ring // 2, ring // 2)
+
+    def carries(d, step, r):
+        if ring % 2 == 1 or step < ring // 2:
+            return True
+        return (r < halves // 2) == (d == 0)
 
     barrier = pltpu.get_barrier_semaphore()
     for peer in (partner, up, down):
@@ -93,6 +98,7 @@
             send_sem=send_sems.at[k], recv_sem=recv_sems.at[k],
             device_id={axis: targets[d]}, device_id_type=MESH)
 
+    last = {}
     for step in range(1, steps[0] + 1):
         for which in range(2):
             if step == 1 and which == 1:
@@ -101,20 +107,16 @@
             for r in range(halves):
                 for a in range(2):
                     for d in range(2):
-                        if step > steps[d]:
+                        if not carries(d, step, r):
                             continue
                         if step > 1:
-                            copies[(d, step - 1, which, r, a)].wait_recv()
+                            last[(d, which, r, a)].wait_recv()
                         c = chunk_copy(d, step, which, r, a)
                         c.start()
                         copies[(d, step, which, r, a)] = c
-    for d in range(2):
-        if steps[d] == 0:
-            continue
-        for which in range(2):
-            for r in range(halves):
-                for a in range(2):
-                    copies[(d, steps[d], which, r, a)].wait_recv()
+                        last[(d, which, r, a)] = c
+    for c in last.values():
+        c.wait_recv()
     for c in locals_:
         c.wait()
     for s in swaps:

time: 200 us -> 197 us (0.985)
  Pallas kernels: 93.1 us -> 90.2 us
where the time goes in v13:
time: 197 us; the launch traced here: 196 us
  Pallas kernels  90.2 us (46%)
  blocking collectives  86.7 us (44%)
  matrix products  9.62 us (5%)
  other arithmetic  7.94 us (4%)
    pallas_call x1, Pallas kernels, ring_sum(): pl.pallas_call(functools.partial(_ring_sum_kernel, axis, outer, chunks),...  55.1 us
    all_to_all x1, blocking collectives, scatter_sum_rows(): got = lax.all_to_all(sent, axis, 0, 0, tiled=False)  53.9 us
    pallas_call x1, Pallas kernels, ring_gather(): pl.pallas_call(functools.partial(_ring_gather_kernel, axis, outer, inner,...  35.1 us
    all_to_all x1, blocking collectives, gather_rows(): got = lax.all_to_all(sent, axis, 0, 0, tiled=False)  32.8 us

profile of v13, /device:TPU:32, one launch (start us, length us, event | category | flops | bytes accessed | tf_op | source)
XLA Modules:
  0.0 196.4 jit_solution(17623972569442532113)
XLA Ops:
  0.6 0.0 copy-start
  0.6 1.7 pad_maximum_fusion.3.x_ref
  2.3 35.1 %shard_map.86 = (bf16[2,8,32,1024]{3,2,1,0:T(8,128)(2,1)}, bf16[2,8,32,1024]{3,2,1,0:T(8,128)(2,1)}) custom-call(bf16[2,32,1024]{2,1,0:T(8,128)(2,1)} %pad_maximum_fusion.3.x_ref), custom_call_target="tpu_custom_call" | custom-call | tf_op jit(solution)/shard_map/pallas_call | solution.py:134
  37.4 0.0 copy-start.3
  37.4 0.0 copy-start.6
  37.4 3.2 %fusion.14 = f32[512,896]{1,0:T(8,128)S(1)} fusion(bf16[512,1024]{1,0:T(8,128)(2,1)} %bitcast.24, bf16[1024,896]{1,0:T(8,128)(2,1)} %param.12), kind=kOutput, calls=%fused_computation.24 | convolution fusion | flops 939524096 | bytes 4718592 | tf_op jit(solution)/shard_map/dot_general | solution.py:253
  40.6 0.0 copy-done.3
  40.6 0.0 copy-done.6
  40.7 1.3 fusion.13
  41.9 1.3 fusion.15
  43.2 2.8 %pad_maximum_fusion = f32[512,2688]{1,0:T(8,128)} fusion(f32[512,896]{1,0:T(8,128)S(1)} %fusion.15, f32[512,896]{1,0:T(8,128)S(1)} %fusion.14, f32[512,896]{1,0:T(8,128)S(1)} %fusion.13), kind=kLoop, calls=%fused_computation | loop fusion | flops 2752512 | bytes 11010048 | tf_op jit(solution)/shard_map/concatenate | solution.py:257
  46.0 55.1 %shard_map.87 = f32[64,2688]{1,0:T(8,128)} custom-call(f32[8,64,2688]{2,1,0:T(8,128)} %bitcast.16), custom_call_target="tpu_custom_call" | custom-call | tf_op jit(solution)/shard_map/pallas_call | solution.py:222
  101.1 1.3 fusion.9
  102.5 0.2 broadcast_in_dim.2
  102.7 32.8 %all_to_all.10 = bf16[8,64,2688]{2,1,0:T(8,128)(2,1)S(1)} all-to-all(bf16[8,64,2688]{2,1,0:T(8,128)(2,1)S(1)} %broadcast_in_dim.2), channel_id=1, replica_groups=mesh['dp'=2,'pipe'=8,'tensor'=16] {'pipe'}, dimensions={0} | all-to-all | bytes 5505024 | tf_op jit(solution)/shard_map/all_to_all | solution.py:28
  135.5 1.3 convolution_convert_fusion
  136.8 0.0 copy-start.4
  136.8 1.3 fusion.1
  138.1 0.2 copy-done.4
  138.3 1.3 add_convert_fusion
  139.6 0.2 pad_maximum_fusion.1
  139.8 53.9 %all_to_all.11 = bf16[16,32,2048]{2,1,0:T(8,128)(2,1)} all-to-all(bf16[16,32,2048]{2,1,0:T(8,128)(2,1)S(1)} %bitcast.17), channel_id=1, replica_groups=mesh['dp'=2,'pipe'=8,'tensor'=16] {'tensor'}, dimensions={0} | all-to-all | bytes 4194304 | tf_op jit(solution)/shard_map/all_to_all | solution.py:35
  193.7 2.0 %reduce_sum.12 = bf16[32,2048]{1,0:T(8,128)(2,1)S(1)} reduce(bf16[16,32,2048]{2,1,0:T(8,128)(2,1)} %all_to_all.11, bf16[]{:T(256)} %constant.6.clone.1), dimensions={0}, to_apply=%region_0.1 | reduce | flops 983040 | bytes 2228226 | tf_op jit(solution)/shard_map/reduce_sum | solution.py:36
  195.7 0.7 fusion.12
  (8 shorter events, 0.0 us)
Async XLA Ops:
  0.6 41.3 %copy-start = (bf16[896,1024]{1,0:T(8,128)(2,1)S(1)}, bf16[896,1024]{1,0:T(8,128)(2,1)}, u32[]{:S(2)}) copy-start(bf16[896,1024]{1,0:T(8,128)(2,1)} %param.13) | copy-start | bytes 5505028
  37.4 3.2 %copy-start.3 = (bf16[1024,896]{1,0:T(8,128)(2,1)S(1)}, bf16[1024,896]{1,0:T(8,128)(2,1)}, u32[]{:S(2)}) copy-start(bf16[1024,896]{1,0:T(8,128)(2,1)} %param.11) | copy-start | bytes 5505028
  37.4 3.2 %copy-start.6 = (bf16[2,8,32,1024]{3,2,1,0:T(8,128)(2,1)S(1)}, bf16[2,8,32,1024]{3,2,1,0:T(8,128)(2,1)}, u32[]{:S(2)}) copy-start(bf16[2,8,32,1024]{3,2,1,0:T(8,128)(2,1)} %get-tuple-element.4) | copy-start | bytes 3145732
  40.7 1.3 copy-start.5
  46.0 55.1 %copy-start.1 = (bf16[64,896]{1,0:T(8,128)(2,1)S(1)}, bf16[64,896]{1,0:T(8,128)(2,1)}, u32[]{:S(2)}) copy-start(bf16[64,896]{1,0:T(8,128)(2,1)} %param.9) | copy-start | bytes 344068
  46.0 55.1 %copy-start.2 = (bf16[64,896]{1,0:T(8,128)(2,1)S(1)}, bf16[64,896]{1,0:T(8,128)(2,1)}, u32[]{:S(2)}) copy-start(bf16[64,896]{1,0:T(8,128)(2,1)} %param.10) | copy-start | bytes 344068
  136.8 1.5 copy-start.4

commit v14 on v10

--- a/solution.py
+++ b/solution.py
@@ -7,7 +7,6 @@
 from jax.experimental.pallas import tpu as pltpu
 from jax.sharding import PartitionSpec as P
 
-PIPE_LINK = jnp.float32
 TENSOR_LINK = jnp.bfloat16
 MESH = pl.DeviceIdType.MESH
 
@@ -23,12 +22,6 @@
     return jnp.concatenate([gate_slope, up_slope], axis=1)
 
 
-def gather_rows(block, axis, count):
-    sent = jnp.broadcast_to(block[None], (count,) + block.shape)
-    got = lax.all_to_all(sent, axis, 0, 0, tiled=False)
-    return got.reshape((count * block.shape[0],) + block.shape[1:])
-
-
 def scatter_sum_rows(partial, axis, count, link_dtype):
     rows = partial.shape[0] // count
     sent = partial.reshape((count, rows) + partial.shape[1:]).astype(link_dtype)
@@ -36,7 +29,7 @@
     return got.astype(jnp.float32).sum(axis=0)
 
 
-def _ring_gather_kernel(axis, outer, inner, ring_on_inner, halves, first_in, second_in, first_ref, second_ref, send_sems, recv_sems, swap_sems, local_sems):
+def _ring_gather_kernel(axis, outer, inner, ring_on_inner, halves, x_ref, first_ref, second_ref, send_sems, recv_sems, swap_sems, local_sems):
     me = lax.axis_index(axis)
     o = me // inner
     i = me % inner
@@ -53,10 +46,14 @@
     partner = at(pos, 1 - other)
     up = at(lax.rem(pos + 1, ring), other)
     down = at(lax.rem(pos + ring - 1, ring), other)
-    ins = (first_in, second_in)
-    rows = first_in.shape[0]
+    rows = x_ref.shape[1]
     part = rows // halves
-    steps = (ring // 2, (ring - 1) // 2)
+    steps = (ring // 2, ring // 2)
+
+    def carries(d, step, r):
+        if ring % 2 == 1 or step < ring // 2:
+            return True
+        return (r < halves // 2) == (d == 0)
 
     barrier = pltpu.get_barrier_semaphore()
     for peer in (partner, up, down):
@@ -67,11 +64,11 @@
     locals_ = []
     swaps = []
     for a in range(2):
-        c = pltpu.make_async_copy(ins[a], outs[a].at[other, pos], local_sems.at[a])
+        c = pltpu.make_async_copy(x_ref.at[a], outs[a].at[other, pos], local_sems.at[a])
         c.start()
         locals_.append(c)
         s = pltpu.make_async_remote_copy(
-            src_ref=ins[a], dst_ref=outs[a].at[other, pos],
+            src_ref=x_ref.at[a], dst_ref=outs[a].at[other, pos],
             send_sem=swap_sems.at[0, a], recv_sem=swap_sems.at[1, a],
             device_id={axis: partner}, device_id_type=MESH)
         s.start()
@@ -85,7 +82,7 @@
         half = other if which == 0 else 1 - other
         rs = pl.ds(r * part, part)
         if step == 1 and which == 0:
-            src = ins[a].at[rs]
+            src = x_ref.at[a, rs]
         else:
             src = outs[a].at[half, slot, rs]
         k = (((d * ring + step - 1) * 2 + which) * halves + r) * 2 + a
@@ -94,6 +91,7 @@
             send_sem=send_sems.at[k], recv_sem=recv_sems.at[k],
             device_id={axis: targets[d]}, device_id_type=MESH)
 
+    last = {}
     for step in range(1, steps[0] + 1):
         for which in range(2):
             if step == 1 and which == 1:
@@ -102,20 +100,16 @@
             for r in range(halves):
                 for a in range(2):
                     for d in range(2):
-                        if step > steps[d]:
+                        if not carries(d, step, r):
                             continue
                         if step > 1:
-                            copies[(d, step - 1, which, r, a)].wait_recv()
+                            last[(d, which, r, a)].wait_recv()
                         c = chunk_copy(d, step, which, r, a)
                         c.start()
                         copies[(d, step, which, r, a)] = c
-    for d in range(2):
-        if steps[d] == 0:
-            continue
-        for which in range(2):
-            for r in range(halves):
-                for a in range(2):
-                    copies[(d, steps[d], which, r, a)].wait_recv()
+                        last[(d, which, r, a)] = c
+    for c in last.values():
+        c.wait_recv()
     for c in locals_:
         c.wait()
     for s in swaps:
@@ -128,11 +122,12 @@
     rows, width = first.shape
     ring = inner if ring_on_inner else outer
     shape = (2, ring, rows, width)
+    x = jnp.stack([first, second])
     n_copies = 2 * ring * 2 * halves * 2
     f, s = pl.pallas_call(
         functools.partial(_ring_gather_kernel, axis, outer, inner, ring_on_inner, halves),
         out_shape=(jax.ShapeDtypeStruct(shape, first.dtype), jax.ShapeDtypeStruct(shape, second.dtype)),
-        in_specs=[pl.BlockSpec(memory_space=pltpu.VMEM)] * 2,
+        in_specs=[pl.BlockSpec(memory_space=pltpu.VMEM)],
         out_specs=(pl.BlockSpec(memory_space=pltpu.VMEM), pl.BlockSpec(memory_space=pltpu.VMEM)),
         scratch_shapes=[
             pltpu.SemaphoreType.DMA((n_copies,)),
@@ -141,7 +136,7 @@
             pltpu.SemaphoreType.DMA((2,)),
         ],
         compiler_params=pltpu.CompilerParams(collective_id=cid, has_side_effects=True),
-    )(first, second)
+    )(x)
     if ring_on_inner:
         return f.reshape(2 * ring * rows, width), s.reshape(2 * ring * rows, width)
     return (f.transpose(1, 0, 2, 3).reshape(2 * ring * rows, width),
@@ -341,21 +336,9 @@
     in_part = lax.dot_general(
         gate_slopes, gate_weight, contract_last, preferred_element_type=jnp.float32
     ) + lax.dot_general(up_slopes, up_weight, contract_last, preferred_element_type=jnp.float32)
-    finishing = jnp.concatenate([out_part, in_part], axis=1)
-    (got,) = exchange(
-        [
-            (
-                finishing.reshape((n_tensor, finishing.shape[0] // n_tensor, finishing.shape[1])).astype(
-                    TENSOR_LINK
-                ),
-                "tensor",
-                n_tensor,
-                False,
-            )
-        ],
-        3,
-    )
-    finished = got.astype(jnp.float32).sum(axis=0).astype(jnp.bfloat16)
+    finished = scatter_sum_rows(
+        jnp.concatenate([out_part, in_part], axis=1), "tensor", n_tensor, TENSOR_LINK
+    ).astype(jnp.bfloat16)
     return (finished[:, :model_width], finished[:, model_width:])
 
 

time: 201 us -> 200 us (level); the launches traced: 198 us -> 200 us
  blocking collectives: 0 us -> 58 us
  Pallas kernels: 177 us -> 120 us
    all_to_all x0 -> x1, blocking collectives: none -> 58 us  [scatter_sum_rows(): got = lax.all_to_all(sent, axis, 0, 0, tiled=False)]
    pallas_call x2 -> x1, Pallas kernels: 83.6 us -> 30 us  [exchange(): pl.pallas_call(functools.partial(_exchange_kernel, plan), out_shape=tuple...]
where the time goes in v14:
time: 200 us
  Pallas kernels  120 us (60%)
  blocking collectives  58 us (29%)
  matrix products  10.9 us (5%)
  other arithmetic  8.72 us (4%)
    all_to_all x1, blocking collectives, scatter_sum_rows(): got = lax.all_to_all(sent, axis, 0, 0, tiled=False)  58 us
    pallas_call x1, Pallas kernels, ring_sum(): pl.pallas_call(functools.partial(_ring_sum_kernel, axis, outer, chunks),...  55.1 us
    pallas_call x1, Pallas kernels, ring_gather(): pl.pallas_call(functools.partial(_ring_gather_kernel, axis, outer, inner,...  35.1 us
    pallas_call x1, Pallas kernels, exchange(): pl.pallas_call(functools.partial(_exchange_kernel, plan), out_shape=tuple...  30 us

profile of v14, /device:TPU:32, one launch (start us, length us, event | category | flops | bytes accessed | tf_op | source)
XLA Modules:
  0.0 199.6 jit_solution(5692029818442959123)
XLA Ops:
  0.6 0.0 copy-start
  0.6 1.7 pad_maximum_fusion.3.x_ref
  2.3 35.1 %shard_map.86 = (bf16[2,8,32,1024]{3,2,1,0:T(8,128)(2,1)}, bf16[2,8,32,1024]{3,2,1,0:T(8,128)(2,1)}) custom-call(bf16[2,32,1024]{2,1,0:T(8,128)(2,1)} %pad_maximum_fusion.3.x_ref), custom_call_target="tpu_custom_call" | custom-call | tf_op jit(solution)/shard_map/pallas_call | solution.py:127
  37.4 0.0 copy-start.4
  37.4 3.2 %fusion.14 = f32[512,896]{1,0:T(8,128)S(1)} fusion(bf16[512,1024]{1,0:T(8,128)(2,1)} %bitcast.24, bf16[1024,896]{1,0:T(8,128)(2,1)} %param.12), kind=kOutput, calls=%fused_computation.24 | convolution fusion | flops 939524096 | bytes 4718592 | tf_op jit(solution)/shard_map/dot_general | solution.py:311
  40.7 1.2 fusion.13
  41.9 1.3 fusion.15
  43.2 2.8 %pad_maximum_fusion = f32[512,2688]{1,0:T(8,128)} fusion(f32[512,896]{1,0:T(8,128)S(1)} %fusion.15, f32[512,896]{1,0:T(8,128)S(1)} %fusion.14, f32[512,896]{1,0:T(8,128)S(1)} %fusion.13), kind=kLoop, calls=%fused_computation | loop fusion | flops 2752512 | bytes 11010048 | tf_op jit(solution)/shard_map/concatenate | solution.py:315
  46.0 55.1 %shard_map.87 = f32[64,2688]{1,0:T(8,128)} custom-call(f32[8,64,2688]{2,1,0:T(8,128)} %bitcast.16), custom_call_target="tpu_custom_call" | custom-call | tf_op jit(solution)/shard_map/pallas_call | solution.py:215
  101.1 0.0 copy-done.2
  101.1 0.0 copy-done.3
  101.1 1.3 fusion.9
  102.5 0.8 pad_maximum_fusion.2.refs_0_
  103.2 30.0 %shard_map.88 = bf16[8,64,2688]{2,1,0:T(8,128)(2,1)} custom-call(bf16[64,2688]{1,0:T(8,128)(2,1)} %pad_maximum_fusion.2.refs_0_), custom_call_target="tpu_custom_call" | custom-call | tf_op jit(solution)/shard_map/pallas_call | solution.py:283
  133.3 0.0 copy-start.5
  133.3 2.6 %convolution_convert_fusion = bf16[512,1024]{1,0:T(8,128)(2,1)S(1)} fusion(bf16[896,1024]{1,0:T(8,128)(2,1)S(1)} %copy-done, bf16[512,2688]{1,0:T(8,128)(2,1)} %bitcast.18), kind=kOutput, calls=%fused_computation.3 | convolution fusion | flops 940048384 | bytes 3801088 | tf_op jit(solution)/shard_map/dot_general | solution.py:335
  135.9 0.0 copy-start.6
  135.9 1.3 fusion.1
  137.2 0.2 copy-done.6
  137.4 1.3 add_convert_fusion
  138.7 0.2 pad_maximum_fusion.1
  138.9 58.0 %all_to_all.5 = bf16[16,32,2048]{2,1,0:T(8,128)(2,1)} all-to-all(bf16[16,32,2048]{2,1,0:T(8,128)(2,1)S(1)} %bitcast.17), channel_id=1, replica_groups=mesh['dp'=2,'pipe'=8,'tensor'=16] {'tensor'}, dimensions={0} | all-to-all | bytes 4194304 | tf_op jit(solution)/shard_map/all_to_all | solution.py:28
  197.0 2.0 reduce_sum.12
  198.9 0.7 fusion.12
  (11 shorter events, 0.0 us)
Async XLA Ops:
  0.6 41.3 %copy-start = (bf16[896,1024]{1,0:T(8,128)(2,1)S(1)}, bf16[896,1024]{1,0:T(8,128)(2,1)}, u32[]{:S(2)}) copy-start(bf16[896,1024]{1,0:T(8,128)(2,1)} %param.13) | copy-start | bytes 5505028
  37.4 3.2 %copy-start.4 = (bf16[1024,896]{1,0:T(8,128)(2,1)S(1)}, bf16[1024,896]{1,0:T(8,128)(2,1)}, u32[]{:S(2)}) copy-start(bf16[1024,896]{1,0:T(8,128)(2,1)} %param.11) | copy-start | bytes 5505028
  37.4 3.2 %copy-start.8 = (bf16[2,8,32,1024]{3,2,1,0:T(8,128)(2,1)S(1)}, bf16[2,8,32,1024]{3,2,1,0:T(8,128)(2,1)}, u32[]{:S(2)}) copy-start(bf16[2,8,32,1024]{3,2,1,0:T(8,128)(2,1)} %get-tuple-element.4) | copy-start | bytes 3145732
  40.7 1.3 copy-start.7
  46.0 55.1 %copy-start.2 = (bf16[64,896]{1,0:T(8,128)(2,1)S(1)}, bf16[64,896]{1,0:T(8,128)(2,1)}, u32[]{:S(2)}) copy-start(bf16[64,896]{1,0:T(8,128)(2,1)} %param.9) | copy-start | bytes 344068
  46.0 55.1 %copy-start.3 = (bf16[64,896]{1,0:T(8,128)(2,1)S(1)}, bf16[64,896]{1,0:T(8,128)(2,1)}, u32[]{:S(2)}) copy-start(bf16[64,896]{1,0:T(8,128)(2,1)} %param.10) | copy-start | bytes 344068
  133.3 2.6 %copy-start.1 = (bf16[8,64,2688]{2,1,0:T(8,128)(2,1)S(1)}, bf16[8,64,2688]{2,1,0:T(8,128)(2,1)}, u32[]{:S(2)}) copy-start(bf16[8,64,2688]{2,1,0:T(8,128)(2,1)} %shard_map.88) | copy-start | bytes 8257540
  133.3 2.6 %copy-start.5 = (bf16[1024,896]{1,0:T(8,128)(2,1)S(1)}, bf16[1024,896]{1,0:T(8,128)(2,1)}, u32[]{:S(2)}) copy-start(bf16[1024,896]{1,0:T(8,128)(2,1)} %param.11) | copy-start | bytes 5505028
  135.9 1.5 copy-start.6

commit v15 on v13

--- a/solution.py
+++ b/solution.py
@@ -125,7 +125,7 @@
         c.wait_send()
 
 
-def ring_gather(first, second, axis, outer, inner, ring_on_inner, cid, halves=2):
+def ring_gather(first, second, axis, outer, inner, ring_on_inner, cid, halves=4):
     rows, width = first.shape
     ring = inner if ring_on_inner else outer
     shape = (2, ring, rows, width)

time: 197 us -> 199 us (1.010)
  Pallas kernels: 90.2 us -> 92.7 us
    pallas_call x1, Pallas kernels: 35.1 us -> 37.3 us  [ring_gather(): pl.pallas_call(functools.partial(_ring_gather_kernel, axis, outer, inner,...]
where the time goes in v15:
time: 199 us
  Pallas kernels  92.7 us (47%)
  blocking collectives  86.6 us (44%)
  matrix products  9.62 us (5%)
  other arithmetic  7.94 us (4%)
    pallas_call x1, Pallas kernels, ring_sum(): pl.pallas_call(functools.partial(_ring_sum_kernel, axis, outer, chunks),...  55.4 us
    all_to_all x1, blocking collectives, scatter_sum_rows(): got = lax.all_to_all(sent, axis, 0, 0, tiled=False)  53.5 us
    pallas_call x1, Pallas kernels, ring_gather(): pl.pallas_call(functools.partial(_ring_gather_kernel, axis, outer, inner,...  37.3 us
    all_to_all x1, blocking collectives, gather_rows(): got = lax.all_to_all(sent, axis, 0, 0, tiled=False)  33 us

profile of v15, /device:TPU:32, one launch (start us, length us, event | category | flops | bytes accessed | tf_op | source)
XLA Modules:
  0.0 198.8 jit_solution(3020564020307857127)
XLA Ops:
  0.6 0.0 copy-start
  0.6 1.7 pad_maximum_fusion.3.x_ref
  2.3 37.3 %shard_map.86 = (bf16[2,8,32,1024]{3,2,1,0:T(8,128)(2,1)}, bf16[2,8,32,1024]{3,2,1,0:T(8,128)(2,1)}) custom-call(bf16[2,32,1024]{2,1,0:T(8,128)(2,1)} %pad_maximum_fusion.3.x_ref), custom_call_target="tpu_custom_call" | custom-call | tf_op jit(solution)/shard_map/pallas_call | solution.py:134
  39.6 0.0 copy-start.3
  39.6 0.0 copy-start.6
  39.6 3.2 %fusion.14 = f32[512,896]{1,0:T(8,128)S(1)} fusion(bf16[512,1024]{1,0:T(8,128)(2,1)} %bitcast.24, bf16[1024,896]{1,0:T(8,128)(2,1)} %param.12), kind=kOutput, calls=%fused_computation.24 | convolution fusion | flops 939524096 | bytes 4718592 | tf_op jit(solution)/shard_map/dot_general | solution.py:253
  42.8 0.0 copy-done.3
  42.9 0.0 copy-done.6
  42.9 1.3 fusion.13
  44.2 1.3 fusion.15
  45.4 2.8 %pad_maximum_fusion = f32[512,2688]{1,0:T(8,128)} fusion(f32[512,896]{1,0:T(8,128)S(1)} %fusion.15, f32[512,896]{1,0:T(8,128)S(1)} %fusion.14, f32[512,896]{1,0:T(8,128)S(1)} %fusion.13), kind=kLoop, calls=%fused_computation | loop fusion | flops 2752512 | bytes 11010048 | tf_op jit(solution)/shard_map/concatenate | solution.py:257
  48.2 55.4 %shard_map.87 = f32[64,2688]{1,0:T(8,128)} custom-call(f32[8,64,2688]{2,1,0:T(8,128)} %bitcast.16), custom_call_target="tpu_custom_call" | custom-call | tf_op jit(solution)/shard_map/pallas_call | solution.py:222
  103.7 1.3 fusion.9
  105.1 0.2 broadcast_in_dim.2
  105.3 33.0 %all_to_all.10 = bf16[8,64,2688]{2,1,0:T(8,128)(2,1)S(1)} all-to-all(bf16[8,64,2688]{2,1,0:T(8,128)(2,1)S(1)} %broadcast_in_dim.2), channel_id=1, replica_groups=mesh['dp'=2,'pipe'=8,'tensor'=16] {'pipe'}, dimensions={0} | all-to-all | bytes 5505024 | tf_op jit(solution)/shard_map/all_to_all | solution.py:28
  138.3 1.3 convolution_convert_fusion
  139.6 0.0 copy-start.4
  139.6 1.3 fusion.1
  140.9 0.2 copy-done.4
  141.1 1.3 add_convert_fusion
  142.4 0.2 pad_maximum_fusion.1
  142.6 53.5 %all_to_all.11 = bf16[16,32,2048]{2,1,0:T(8,128)(2,1)} all-to-all(bf16[16,32,2048]{2,1,0:T(8,128)(2,1)S(1)} %bitcast.17), channel_id=1, replica_groups=mesh['dp'=2,'pipe'=8,'tensor'=16] {'tensor'}, dimensions={0} | all-to-all | bytes 4194304 | tf_op jit(solution)/shard_map/all_to_all | solution.py:35
  196.1 2.0 reduce_sum.12
  198.1 0.7 fusion.12
  (8 shorter events, 0.0 us)
Async XLA Ops:
  0.6 43.5 %copy-start = (bf16[896,1024]{1,0:T(8,128)(2,1)S(1)}, bf16[896,1024]{1,0:T(8,128)(2,1)}, u32[]{:S(2)}) copy-start(bf16[896,1024]{1,0:T(8,128)(2,1)} %param.13) | copy-start | bytes 5505028
  39.6 3.2 %copy-start.3 = (bf16[1024,896]{1,0:T(8,128)(2,1)S(1)}, bf16[1024,896]{1,0:T(8,128)(2,1)}, u32[]{:S(2)}) copy-start(bf16[1024,896]{1,0:T(8,128)(2,1)} %param.11) | copy-start | bytes 5505028
  39.6 3.2 %copy-start.6 = (bf16[2,8,32,1024]{3,2,1,0:T(8,128)(2,1)S(1)}, bf16[2,8,32,1024]{3,2,1,0:T(8,128)(2,1)}, u32[]{:S(2)}) copy-start(bf16[2,8,32,1024]{3,2,1,0:T(8,128)(2,1)} %get-tuple-element.4) | copy-start | bytes 3145732
  42.9 1.3 copy-start.5
  48.2 55.5 %copy-start.1 = (bf16[64,896]{1,0:T(8,128)(2,1)S(1)}, bf16[64,896]{1,0:T(8,128)(2,1)}, u32[]{:S(2)}) copy-start(bf16[64,896]{1,0:T(8,128)(2,1)} %param.9) | copy-start | bytes 344068
  48.2 55.5 %copy-start.2 = (bf16[64,896]{1,0:T(8,128)(2,1)S(1)}, bf16[64,896]{1,0:T(8,128)(2,1)}, u32[]{:S(2)}) copy-start(bf16[64,896]{1,0:T(8,128)(2,1)} %param.10) | copy-start | bytes 344068
  139.6 1.5 copy-start.4

commit v16 on v13

--- a/solution.py
+++ b/solution.py
@@ -36,7 +36,7 @@
     return got.astype(jnp.float32).sum(axis=0)
 
 
-def _ring_gather_kernel(axis, outer, inner, ring_on_inner, halves, x_ref, first_ref, second_ref, send_sems, recv_sems, swap_sems, local_sems):
+def _ring_gather_kernel(axis, outer, inner, ring_on_inner, halves, first_in, second_in, first_ref, second_ref, send_sems, recv_sems, swap_sems, local_sems):
     me = lax.axis_index(axis)
     o = me // inner
     i = me % inner
@@ -53,7 +53,8 @@
     partner = at(pos, 1 - other)
     up = at(lax.rem(pos + 1, ring), other)
     down = at(lax.rem(pos + ring - 1, ring), other)
-    rows = x_ref.shape[1]
+    ins = (first_in, second_in)
+    rows = first_in.shape[0]
     part = rows // halves
     steps = (ring // 2, ring // 2)
 
@@ -71,11 +72,11 @@
     locals_ = []
     swaps = []
     for a in range(2):
-        c = pltpu.make_async_copy(x_ref.at[a], outs[a].at[other, pos], local_sems.at[a])
+        c = pltpu.make_async_copy(ins[a], outs[a].at[other, pos], local_sems.at[a])
         c.start()
         locals_.append(c)
         s = pltpu.make_async_remote_copy(
-            src_ref=x_ref.at[a], dst_ref=outs[a].at[other, pos],
+            src_ref=ins[a], dst_ref=outs[a].at[other, pos],
             send_sem=swap_sems.at[0, a], recv_sem=swap_sems.at[1, a],
             device_id={axis: partner}, device_id_type=MESH)
         s.start()
@@ -89,7 +90,7 @@
         half = other if which == 0 else 1 - other
         rs = pl.ds(r * part, part)
         if step == 1 and which == 0:
-            src = x_ref.at[a, rs]
+            src = ins[a].at[rs]
         else:
             src = outs[a].at[half, slot, rs]
         k = (((d * ring + step - 1) * 2 + which) * halves + r) * 2 + a
@@ -129,12 +130,11 @@
     rows, width = first.shape
     ring = inner if ring_on_inner else outer
     shape = (2, ring, rows, width)
-    x = jnp.stack([first, second])
     n_copies = 2 * ring * 2 * halves * 2
     f, s = pl.pallas_call(
         functools.partial(_ring_gather_kernel, axis, outer, inner, ring_on_inner, halves),
         out_shape=(jax.ShapeDtypeStruct(shape, first.dtype), jax.ShapeDtypeStruct(shape, second.dtype)),
-        in_specs=[pl.BlockSpec(memory_space=pltpu.VMEM)],
+        in_specs=[pl.BlockSpec(memory_space=pltpu.VMEM)] * 2,
         out_specs=(pl.BlockSpec(memory_space=pltpu.VMEM), pl.BlockSpec(memory_space=pltpu.VMEM)),
         scratch_shapes=[
             pltpu.SemaphoreType.DMA((n_copies,)),
@@ -143,7 +143,7 @@
             pltpu.SemaphoreType.DMA((2,)),
         ],
         compiler_params=pltpu.CompilerParams(collective_id=cid, has_side_effects=True),
-    )(x)
+    )(first, second)
     if ring_on_inner:
         return f.reshape(2 * ring * rows, width), s.reshape(2 * ring * rows, width)
     return (f.transpose(1, 0, 2, 3).reshape(2 * ring * rows, width),

time: 197 us -> 195 us (0.990)
  no operation moved by 1% of the time
where the time goes in v16:
time: 195 us
  Pallas kernels  90.4 us (46%)
  blocking collectives  86.7 us (44%)
  matrix products  9.6 us (5%)
  other arithmetic  6.28 us (3%)
    pallas_call x1, Pallas kernels, ring_sum(): pl.pallas_call(functools.partial(_ring_sum_kernel, axis, outer, chunks),...  55.1 us
    all_to_all x1, blocking collectives, scatter_sum_rows(): got = lax.all_to_all(sent, axis, 0, 0, tiled=False)  53.9 us
    pallas_call x1, Pallas kernels, ring_gather(): pl.pallas_call(functools.partial(_ring_gather_kernel, axis, outer, inner,...  35.3 us
    all_to_all x1, blocking collectives, gather_rows(): got = lax.all_to_all(sent, axis, 0, 0, tiled=False)  32.8 us

profile of v16, /device:TPU:32, one launch (start us, length us, event | category | flops | bytes accessed | tf_op | source)
XLA Modules:
  0.0 194.9 jit_solution(16322647996487721843)
XLA Ops:
  0.6 0.0 copy-start
  0.6 35.3 %shard_map.86 = (bf16[2,8,32,1024]{3,2,1,0:T(8,128)(2,1)}, bf16[2,8,32,1024]{3,2,1,0:T(8,128)(2,1)}) custom-call(bf16[32,1024]{1,0:T(8,128)(2,1)} %first_in.1, bf16[32,1024]{1,0:T(8,128)(2,1)} %second_in.1), custom_call_target="tpu_custom_call" | custom-call | tf_op jit(solution)/shard_map/pallas_call | solution.py:134
  35.9 0.0 copy-start.3
  36.0 0.0 copy-start.6
  36.0 3.2 %fusion.14 = f32[512,896]{1,0:T(8,128)S(1)} fusion(bf16[512,1024]{1,0:T(8,128)(2,1)} %bitcast.20, bf16[1024,896]{1,0:T(8,128)(2,1)} %param.12), kind=kOutput, calls=%fused_computation.23 | convolution fusion | flops 939524096 | bytes 4718592 | tf_op jit(solution)/shard_map/dot_general | solution.py:253
  39.2 0.0 copy-done.3
  39.2 0.0 copy-done.6
  39.2 0.0 copy-start.5
  39.2 1.3 fusion.13
  40.5 1.3 fusion.15
  41.8 2.8 %pad_maximum_fusion = f32[512,2688]{1,0:T(8,128)} fusion(f32[512,896]{1,0:T(8,128)S(1)} %fusion.15, f32[512,896]{1,0:T(8,128)S(1)} %fusion.14, f32[512,896]{1,0:T(8,128)S(1)} %fusion.13), kind=kLoop, calls=%fused_computation | loop fusion | flops 2752512 | bytes 11010048 | tf_op jit(solution)/shard_map/concatenate | solution.py:257
  44.5 55.1 %shard_map.87 = f32[64,2688]{1,0:T(8,128)} custom-call(f32[8,64,2688]{2,1,0:T(8,128)} %bitcast.14), custom_call_target="tpu_custom_call" | custom-call | tf_op jit(solution)/shard_map/pallas_call | solution.py:222
  99.7 1.3 fusion.9
  101.0 0.2 broadcast_in_dim.2
  101.2 32.8 %all_to_all.10 = bf16[8,64,2688]{2,1,0:T(8,128)(2,1)S(1)} all-to-all(bf16[8,64,2688]{2,1,0:T(8,128)(2,1)S(1)} %broadcast_in_dim.2), channel_id=1, replica_groups=mesh['dp'=2,'pipe'=8,'tensor'=16] {'pipe'}, dimensions={0} | all-to-all | bytes 5505024 | tf_op jit(solution)/shard_map/all_to_all | solution.py:28
  134.1 1.3 convolution_convert_fusion
  135.4 0.0 copy-start.4
  135.4 1.3 fusion.1
  136.7 0.2 copy-done.4
  136.9 1.3 add_convert_fusion
  138.2 0.2 pad_maximum_fusion.1
  138.3 53.9 %all_to_all.11 = bf16[16,32,2048]{2,1,0:T(8,128)(2,1)} all-to-all(bf16[16,32,2048]{2,1,0:T(8,128)(2,1)S(1)} %bitcast.15), channel_id=1, replica_groups=mesh['dp'=2,'pipe'=8,'tensor'=16] {'tensor'}, dimensions={0} | all-to-all | bytes 4194304 | tf_op jit(solution)/shard_map/all_to_all | solution.py:35
  192.3 2.0 %reduce_sum.12 = bf16[32,2048]{1,0:T(8,128)(2,1)S(1)} reduce(bf16[16,32,2048]{2,1,0:T(8,128)(2,1)} %all_to_all.11, bf16[]{:T(256)} %constant.6.clone.1), dimensions={0}, to_apply=%region_0.1 | reduce | flops 983040 | bytes 2228226 | tf_op jit(solution)/shard_map/reduce_sum | solution.py:36
  194.2 0.7 fusion.12
  (7 shorter events, 0.0 us)
Async XLA Ops:
  0.6 39.8 %copy-start = (bf16[896,1024]{1,0:T(8,128)(2,1)S(1)}, bf16[896,1024]{1,0:T(8,128)(2,1)}, u32[]{:S(2)}) copy-start(bf16[896,1024]{1,0:T(8,128)(2,1)} %param.13) | copy-start | bytes 5505028
  35.9 3.2 %copy-start.3 = (bf16[1024,896]{1,0:T(8,128)(2,1)S(1)}, bf16[1024,896]{1,0:T(8,128)(2,1)}, u32[]{:S(2)}) copy-start(bf16[1024,896]{1,0:T(8,128)(2,1)} %param.11) | copy-start | bytes 5505028
  36.0 3.2 %copy-start.6 = (bf16[2,8,32,1024]{3,2,1,0:T(8,128)(2,1)S(1)}, bf16[2,8,32,1024]{3,2,1,0:T(8,128)(2,1)}, u32[]{:S(2)}) copy-start(bf16[2,8,32,1024]{3,2,1,0:T(8,128)(2,1)} %get-tuple-element.4) | copy-start | bytes 3145732
  39.2 1.3 copy-start.5
  44.5 55.1 %copy-start.1 = (bf16[64,896]{1,0:T(8,128)(2,1)S(1)}, bf16[64,896]{1,0:T(8,128)(2,1)}, u32[]{:S(2)}) copy-start(bf16[64,896]{1,0:T(8,128)(2,1)} %param.9) | copy-start | bytes 344068
  44.5 55.1 %copy-start.2 = (bf16[64,896]{1,0:T(8,128)(2,1)S(1)}, bf16[64,896]{1,0:T(8,128)(2,1)}, u32[]{:S(2)}) copy-start(bf16[64,896]{1,0:T(8,128)(2,1)} %param.10) | copy-start | bytes 344068
  135.4 1.5 copy-start.4

commit v17 on v16

--- a/solution.py
+++ b/solution.py
@@ -21,12 +21,6 @@
     )
     up_slope = (hidden_grad * gate_wide * sigma).astype(jnp.bfloat16)
     return jnp.concatenate([gate_slope, up_slope], axis=1)
-
-
-def gather_rows(block, axis, count):
-    sent = jnp.broadcast_to(block[None], (count,) + block.shape)
-    got = lax.all_to_all(sent, axis, 0, 0, tiled=False)
-    return got.reshape((count * block.shape[0],) + block.shape[1:])
 
 
 def scatter_sum_rows(partial, axis, count, link_dtype):
@@ -267,7 +261,12 @@
     hidden_part = (jax.nn.silu(gate_pre) * up_pre).astype(jnp.bfloat16)
     local_slopes = make_slopes(hidden_grad, stored_gate, stored_up)
 
-    rows = gather_rows(jnp.concatenate([hidden_part, local_slopes], axis=1), "pipe", n_pipe)
+    local_rows = jnp.concatenate([hidden_part, local_slopes], axis=1)
+    split = local_rows.shape[1] // 2
+    rows_low, rows_high = ring_gather(
+        local_rows[:, :split], local_rows[:, split:], "pipe", n_pipe // 2, 2, False, 2
+    )
+    rows = jnp.concatenate([rows_low, rows_high], axis=1)
     hidden = rows[:, :hidden_width]
     gate_slopes = rows[:, hidden_width : 2 * hidden_width]
     up_slopes = rows[:, 2 * hidden_width :]

time: 195 us -> 194 us (level)
  blocking collectives: 86.7 us -> 54.3 us
  Pallas kernels: 90.4 us -> 118 us
    all_to_all x1 -> x0, blocking collectives: 32.8 us -> none  [gather_rows(): got = lax.all_to_all(sent, axis, 0, 0, tiled=False)]
    pallas_call x1 -> x2, Pallas kernels: 35.3 us -> 63.1 us  [ring_gather(): pl.pallas_call(functools.partial(_ring_gather_kernel, axis, outer, inner,...]
where the time goes in v17:
time: 194 us; the launch traced here: 193 us
  Pallas kernels  118 us (61%)
  blocking collectives  54.3 us (28%)
  matrix products  9.62 us (5%)
  other arithmetic  7.09 us (4%)
  local copies, waits for them, and re-layouts  3 us (2%)
    pallas_call x2, Pallas kernels, ring_gather(): pl.pallas_call(functools.partial(_ring_gather_kernel, axis, outer, inner,...  63.1 us
    pallas_call x1, Pallas kernels, ring_sum(): pl.pallas_call(functools.partial(_ring_sum_kernel, axis, outer, chunks),...  55.1 us
    all_to_all x1, blocking collectives, scatter_sum_rows(): got = lax.all_to_all(sent, axis, 0, 0, tiled=False)  54.3 us

profile of v17, /device:TPU:32, one launch (start us, length us, event | category | flops | bytes accessed | tf_op | source)
XLA Modules:
  0.0 193.0 jit_solution(3413815154868379757)
XLA Ops:
  0.6 0.0 copy-start
  0.6 35.3 %shard_map.86 = (bf16[2,8,32,1024]{3,2,1,0:T(8,128)(2,1)}, bf16[2,8,32,1024]{3,2,1,0:T(8,128)(2,1)}) custom-call(bf16[32,1024]{1,0:T(8,128)(2,1)} %first_in.1, bf16[32,1024]{1,0:T(8,128)(2,1)} %second_in.1), custom_call_target="tpu_custom_call" | custom-call | tf_op jit(solution)/shard_map/pallas_call | solution.py:128
  35.9 0.0 copy-start.1
  35.9 3.2 %fusion.15 = f32[512,896]{1,0:T(8,128)S(1)} fusion(bf16[512,1024]{1,0:T(8,128)(2,1)} %bitcast.26, bf16[1024,896]{1,0:T(8,128)(2,1)} %param.12), kind=kOutput, calls=%fused_computation.26 | convolution fusion | flops 939524096 | bytes 4718592 | tf_op jit(solution)/shard_map/dot_general | solution.py:247
  39.2 1.2 fusion.14
  40.5 1.3 fusion.16
  41.8 2.8 %pad_maximum_fusion = f32[512,2688]{1,0:T(8,128)} fusion(f32[512,896]{1,0:T(8,128)S(1)} %fusion.16, f32[512,896]{1,0:T(8,128)S(1)} %fusion.15, f32[512,896]{1,0:T(8,128)S(1)} %fusion.14), kind=kLoop, calls=%fused_computation | loop fusion | flops 2752512 | bytes 11010048 | tf_op jit(solution)/shard_map/concatenate | solution.py:251
  44.5 55.1 %shard_map.87 = f32[64,2688]{1,0:T(8,128)} custom-call(f32[8,64,2688]{2,1,0:T(8,128)} %bitcast.17), custom_call_target="tpu_custom_call" | custom-call | tf_op jit(solution)/shard_map/pallas_call | solution.py:216
  99.7 1.3 fusion.11
  101.0 0.8 pad_maximum_fusion.4
  101.8 27.8 %shard_map.88 = (bf16[2,4,64,1344]{3,2,1,0:T(8,128)(2,1)}, bf16[2,4,64,1344]{3,2,1,0:T(8,128)(2,1)}) custom-call(bf16[64,1344]{1,0:T(8,128)(2,1)} %get-tuple-element.16.first_in, bf16[64,1344]{1,0:T(8,128)(2,1)} %get-tuple-element.15.second_in), custom_call_target="tpu_custom_call" | custom-call | tf_op jit(solution)/shard_map/pallas_call | solution.py:128
  129.6 1.6 copy.9
  131.2 0.2 copy-done.3
  131.4 0.1 copy.10
  131.5 0.0 copy-start.2
  131.5 1.3 convolution_convert_fusion
  132.8 0.2 copy-done.2
  133.0 1.3 fusion.1
  134.3 0.2 copy-done.6
  134.5 1.3 add_convert_fusion
  135.8 0.2 pad_maximum_fusion.1
  136.0 54.3 %all_to_all.5 = bf16[16,32,2048]{2,1,0:T(8,128)(2,1)} all-to-all(bf16[16,32,2048]{2,1,0:T(8,128)(2,1)S(1)} %bitcast.18), channel_id=1, replica_groups=mesh['dp'=2,'pipe'=8,'tensor'=16] {'tensor'}, dimensions={0} | all-to-all | bytes 4194304 | tf_op jit(solution)/shard_map/all_to_all | solution.py:29
  190.4 2.0 %reduce_sum.12 = bf16[32,2048]{1,0:T(8,128)(2,1)S(1)} reduce(bf16[16,32,2048]{2,1,0:T(8,128)(2,1)} %all_to_all.5, bf16[]{:T(256)} %constant.6.clone.1), dimensions={0}, to_apply=%region_0.1 | reduce | flops 983040 | bytes 2228226 | tf_op jit(solution)/shard_map/reduce_sum | solution.py:30
  192.4 0.7 fusion.13
  (12 shorter events, 0.0 us)
Async XLA Ops:
  0.6 39.8 %copy-start = (bf16[896,1024]{1,0:T(8,128)(2,1)S(1)}, bf16[896,1024]{1,0:T(8,128)(2,1)}, u32[]{:S(2)}) copy-start(bf16[896,1024]{1,0:T(8,128)(2,1)} %param.13) | copy-start | bytes 5505028
  35.9 3.2 %copy-start.1 = (bf16[1024,896]{1,0:T(8,128)(2,1)S(1)}, bf16[1024,896]{1,0:T(8,128)(2,1)}, u32[]{:S(2)}) copy-start(bf16[1024,896]{1,0:T(8,128)(2,1)} %param.11) | copy-start | bytes 5505028
  35.9 3.2 %copy-start.8 = (bf16[2,8,32,1024]{3,2,1,0:T(8,128)(2,1)S(1)}, bf16[2,8,32,1024]{3,2,1,0:T(8,128)(2,1)}, u32[]{:S(2)}) copy-start(bf16[2,8,32,1024]{3,2,1,0:T(8,128)(2,1)} %get-tuple-element.6) | copy-start | bytes 3145732
  39.2 1.3 copy-start.7
  44.5 55.1 %copy-start.4 = (bf16[64,896]{1,0:T(8,128)(2,1)S(1)}, bf16[64,896]{1,0:T(8,128)(2,1)}, u32[]{:S(2)}) copy-start(bf16[64,896]{1,0:T(8,128)(2,1)} %param.9) | copy-start | bytes 344068
  44.5 55.1 %copy-start.5 = (bf16[64,896]{1,0:T(8,128)(2,1)S(1)}, bf16[64,896]{1,0:T(8,128)(2,1)}, u32[]{:S(2)}) copy-start(bf16[64,896]{1,0:T(8,128)(2,1)} %param.10) | copy-start | bytes 344068
  129.6 1.8 copy-start.3
  131.5 1.5 copy-start.2
  133.0 1.5 copy-start.6

commit v18 on v17

--- a/solution.py
+++ b/solution.py
@@ -63,14 +63,17 @@
     pl.semaphore_wait(barrier, 3)
 
     outs = (first_ref, second_ref)
+
+    def slot_of(a, half, slot):
+        return outs[a].at[half, slot] if ring_on_inner else outs[a].at[slot, half]
     locals_ = []
     swaps = []
     for a in range(2):
-        c = pltpu.make_async_copy(ins[a], outs[a].at[other, pos], local_sems.at[a])
+        c = pltpu.make_async_copy(ins[a], slot_of(a, other, pos), local_sems.at[a])
         c.start()
         locals_.append(c)
         s = pltpu.make_async_remote_copy(
-            src_ref=ins[a], dst_ref=outs[a].at[other, pos],
+            src_ref=ins[a], dst_ref=slot_of(a, other, pos),
             send_sem=swap_sems.at[0, a], recv_sem=swap_sems.at[1, a],
             device_id={axis: partner}, device_id_type=MESH)
         s.start()
@@ -86,10 +89,10 @@
         if step == 1 and which == 0:
             src = ins[a].at[rs]
         else:
-            src = outs[a].at[half, slot, rs]
+            src = slot_of(a, half, slot).at[rs]
         k = (((d * ring + step - 1) * 2 + which) * halves + r) * 2 + a
         return pltpu.make_async_remote_copy(
-            src_ref=src, dst_ref=outs[a].at[half, slot, rs],
+            src_ref=src, dst_ref=slot_of(a, half, slot).at[rs],
             send_sem=send_sems.at[k], recv_sem=recv_sems.at[k],
             device_id={axis: targets[d]}, device_id_type=MESH)
 
@@ -123,7 +126,7 @@
 def ring_gather(first, second, axis, outer, inner, ring_on_inner, cid, halves=2):
     rows, width = first.shape
     ring = inner if ring_on_inner else outer
-    shape = (2, ring, rows, width)
+    shape = (2, ring, rows, width) if ring_on_inner else (ring, 2, rows, width)
     n_copies = 2 * ring * 2 * halves * 2
     f, s = pl.pallas_call(
         functools.partial(_ring_gather_kernel, axis, outer, inner, ring_on_inner, halves),
@@ -138,10 +141,7 @@
         ],
         compiler_params=pltpu.CompilerParams(collective_id=cid, has_side_effects=True),
     )(first, second)
-    if ring_on_inner:
-        return f.reshape(2 * ring * rows, width), s.reshape(2 * ring * rows, width)
-    return (f.transpose(1, 0, 2, 3).reshape(2 * ring * rows, width),
-            s.transpose(1, 0, 2, 3).reshape(2 * ring * rows, width))
+    return f.reshape(2 * ring * rows, width), s.reshape(2 * ring * rows, width)
 
 
 def _ring_sum_kernel(axis, outer, chunks, x_ref, out_ref, send_buf, recv_buf, swap_buf, send_sems, recv_sems, swap_sems):

time: 194 us -> 193 us (level)
  local copies, waits for them, and re-layouts: 3 us -> 0.9 us
where the time goes in v18:
time: 193 us; the launch traced here: 192 us
  Pallas kernels  118 us (61%)
  blocking collectives  54.4 us (28%)
  matrix products  10.9 us (6%)
  other arithmetic  7.08 us (4%)
    pallas_call x2, Pallas kernels, ring_gather(): pl.pallas_call(functools.partial(_ring_gather_kernel, axis, outer, inner,...  63 us
    pallas_call x1, Pallas kernels, ring_sum(): pl.pallas_call(functools.partial(_ring_sum_kernel, axis, outer, chunks),...  55.1 us
    all_to_all x1, blocking collectives, scatter_sum_rows(): got = lax.all_to_all(sent, axis, 0, 0, tiled=False)  54.4 us

profile of v18, /device:TPU:32, one launch (start us, length us, event | category | flops | bytes accessed | tf_op | source)
XLA Modules:
  0.0 192.2 jit_solution(17098354189115070959)
XLA Ops:
  0.6 0.0 copy-start
  0.6 35.3 %shard_map.86 = (bf16[2,8,32,1024]{3,2,1,0:T(8,128)(2,1)}, bf16[2,8,32,1024]{3,2,1,0:T(8,128)(2,1)}) custom-call(bf16[32,1024]{1,0:T(8,128)(2,1)} %first_in.1, bf16[32,1024]{1,0:T(8,128)(2,1)} %second_in.1), custom_call_target="tpu_custom_call" | custom-call | tf_op jit(solution)/shard_map/pallas_call | solution.py:131
  35.9 0.0 copy-start.1
  35.9 0.0 copy-start.9
  36.0 3.2 %fusion.15 = f32[512,896]{1,0:T(8,128)S(1)} fusion(bf16[512,1024]{1,0:T(8,128)(2,1)} %bitcast.22, bf16[1024,896]{1,0:T(8,128)(2,1)} %param.12), kind=kOutput, calls=%fused_computation.26 | convolution fusion | flops 939524096 | bytes 4718592 | tf_op jit(solution)/shard_map/dot_general | solution.py:247
  39.2 1.2 fusion.14
  40.5 1.3 fusion.16
  41.8 2.8 %pad_maximum_fusion = f32[512,2688]{1,0:T(8,128)} fusion(f32[512,896]{1,0:T(8,128)S(1)} %fusion.16, f32[512,896]{1,0:T(8,128)S(1)} %fusion.15, f32[512,896]{1,0:T(8,128)S(1)} %fusion.14), kind=kLoop, calls=%fused_computation | loop fusion | flops 2752512 | bytes 11010048 | tf_op jit(solution)/shard_map/concatenate | solution.py:251
  44.5 55.1 %shard_map.87 = f32[64,2688]{1,0:T(8,128)} custom-call(f32[8,64,2688]{2,1,0:T(8,128)} %bitcast.15), custom_call_target="tpu_custom_call" | custom-call | tf_op jit(solution)/shard_map/pallas_call | solution.py:216
  99.6 1.3 fusion.11
  101.0 0.8 pad_maximum_fusion.4
  101.8 27.8 %shard_map.88 = (bf16[4,2,64,1344]{3,2,1,0:T(8,128)(2,1)}, bf16[4,2,64,1344]{3,2,1,0:T(8,128)(2,1)}) custom-call(bf16[64,1344]{1,0:T(8,128)(2,1)} %get-tuple-element.16.first_in, bf16[64,1344]{1,0:T(8,128)(2,1)} %get-tuple-element.15.second_in), custom_call_target="tpu_custom_call" | custom-call | tf_op jit(solution)/shard_map/pallas_call | solution.py:131
  129.6 0.0 copy-start.2
  129.6 0.0 copy-start.3
  129.6 0.0 copy-start.4
  129.6 2.6 %convolution_convert_fusion = bf16[512,1024]{1,0:T(8,128)(2,1)S(1)} fusion(bf16[896,1024]{1,0:T(8,128)(2,1)S(1)} %copy-done, bf16[512,1344]{1,0:T(8,128)(2,1)} %bitcast.19), kind=kOutput, calls=%fused_computation.3 | convolution fusion | flops 940048384 | bytes 3801088 | tf_op jit(solution)/shard_map/dot_general | solution.py:274
  132.2 0.0 copy-start.7
  132.2 1.3 fusion.1
  133.5 0.2 copy-done.7
  133.7 1.3 add_convert_fusion
  135.0 0.2 pad_maximum_fusion.1
  135.2 54.4 %all_to_all.5 = bf16[16,32,2048]{2,1,0:T(8,128)(2,1)} all-to-all(bf16[16,32,2048]{2,1,0:T(8,128)(2,1)S(1)} %bitcast.16), channel_id=1, replica_groups=mesh['dp'=2,'pipe'=8,'tensor'=16] {'tensor'}, dimensions={0} | all-to-all | bytes 4194304 | tf_op jit(solution)/shard_map/all_to_all | solution.py:29
  189.6 2.0 %reduce_sum.12 = bf16[32,2048]{1,0:T(8,128)(2,1)S(1)} reduce(bf16[16,32,2048]{2,1,0:T(8,128)(2,1)} %all_to_all.5, bf16[]{:T(256)} %constant.6.clone.1), dimensions={0}, to_apply=%region_0.1 | reduce | flops 983040 | bytes 2228226 | tf_op jit(solution)/shard_map/reduce_sum | solution.py:30
  191.6 0.7 fusion.13
  (12 shorter events, 0.0 us)
Async XLA Ops:
  0.6 39.8 %copy-start = (bf16[896,1024]{1,0:T(8,128)(2,1)S(1)}, bf16[896,1024]{1,0:T(8,128)(2,1)}, u32[]{:S(2)}) copy-start(bf16[896,1024]{1,0:T(8,128)(2,1)} %param.13) | copy-start | bytes 5505028
  35.9 3.2 %copy-start.1 = (bf16[1024,896]{1,0:T(8,128)(2,1)S(1)}, bf16[1024,896]{1,0:T(8,128)(2,1)}, u32[]{:S(2)}) copy-start(bf16[1024,896]{1,0:T(8,128)(2,1)} %param.11) | copy-start | bytes 5505028
  35.9 3.2 %copy-start.9 = (bf16[2,8,32,1024]{3,2,1,0:T(8,128)(2,1)S(1)}, bf16[2,8,32,1024]{3,2,1,0:T(8,128)(2,1)}, u32[]{:S(2)}) copy-start(bf16[2,8,32,1024]{3,2,1,0:T(8,128)(2,1)} %get-tuple-element.6) | copy-start | bytes 3145732
  39.2 1.3 copy-start.8
  44.5 55.1 %copy-start.5 = (bf16[64,896]{1,0:T(8,128)(2,1)S(1)}, bf16[64,896]{1,0:T(8,128)(2,1)}, u32[]{:S(2)}) copy-start(bf16[64,896]{1,0:T(8,128)(2,1)} %param.9) | copy-start | bytes 344068
  44.5 55.1 %copy-start.6 = (bf16[64,896]{1,0:T(8,128)(2,1)S(1)}, bf16[64,896]{1,0:T(8,128)(2,1)}, u32[]{:S(2)}) copy-start(bf16[64,896]{1,0:T(8,128)(2,1)} %param.10) | copy-start | bytes 344068
  129.6 2.6 %copy-start.2 = (bf16[1024,896]{1,0:T(8,128)(2,1)S(1)}, bf16[1024,896]{1,0:T(8,128)(2,1)}, u32[]{:S(2)}) copy-start(bf16[1024,896]{1,0:T(8,128)(2,1)} %param.11) | copy-start | bytes 5505028
  129.6 2.6 %copy-start.3 = (bf16[4,2,64,1344]{3,2,1,0:T(8,128)(2,1)S(1)}, bf16[4,2,64,1344]{3,2,1,0:T(8,128)(2,1)}, u32[]{:S(2)}) copy-start(bf16[4,2,64,1344]{3,2,1,0:T(8,128)(2,1)} %get-tuple-element.9) | copy-start | bytes 4128772
  129.6 2.6 %copy-start.4 = (bf16[4,2,64,1344]{3,2,1,0:T(8,128)(2,1)S(1)}, bf16[4,2,64,1344]{3,2,1,0:T(8,128)(2,1)}, u32[]{:S(2)}) copy-start(bf16[4,2,64,1344]{3,2,1,0:T(8,128)(2,1)} %get-tuple-element.8) | copy-start | bytes 4128772
  132.2 1.5 copy-start.7

commit v19 on v18

--- a/solution.py
+++ b/solution.py
@@ -20,7 +20,7 @@
         jnp.bfloat16
     )
     up_slope = (hidden_grad * gate_wide * sigma).astype(jnp.bfloat16)
-    return jnp.concatenate([gate_slope, up_slope], axis=1)
+    return gate_slope, up_slope
 
 
 def scatter_sum_rows(partial, axis, count, link_dtype):
@@ -30,7 +30,7 @@
     return got.astype(jnp.float32).sum(axis=0)
 
 
-def _ring_gather_kernel(axis, outer, inner, ring_on_inner, halves, first_in, second_in, first_ref, second_ref, send_sems, recv_sems, swap_sems, local_sems):
+def _ring_gather_kernel(axis, outer, inner, ring_on_inner, halves, count, *refs):
     me = lax.axis_index(axis)
     o = me // inner
     i = me % inner
@@ -47,8 +47,10 @@
     partner = at(pos, 1 - other)
     up = at(lax.rem(pos + 1, ring), other)
     down = at(lax.rem(pos + ring - 1, ring), other)
-    ins = (first_in, second_in)
-    rows = first_in.shape[0]
+    ins = refs[:count]
+    outs = refs[count:2 * count]
+    send_sems, recv_sems, swap_sems, local_sems = refs[2 * count:]
+    rows = ins[0].shape[0]
     part = rows // halves
     steps = (ring // 2, ring // 2)
 
@@ -62,13 +64,12 @@
         pl.semaphore_signal(barrier, inc=1, device_id={axis: peer}, device_id_type=MESH)
     pl.semaphore_wait(barrier, 3)
 
-    outs = (first_ref, second_ref)
 
     def slot_of(a, half, slot):
         return outs[a].at[half, slot] if ring_on_inner else outs[a].at[slot, half]
     locals_ = []
     swaps = []
-    for a in range(2):
+    for a in range(count):
         c = pltpu.make_async_copy(ins[a], slot_of(a, other, pos), local_sems.at[a])
         c.start()
         locals_.append(c)
@@ -90,7 +91,7 @@
             src = ins[a].at[rs]
         else:
             src = slot_of(a, half, slot).at[rs]
-        k = (((d * ring + step - 1) * 2 + which) * halves + r) * 2 + a
+        k = (((d * ring + step - 1) * 2 + which) * halves + r) * count + a
         return pltpu.make_async_remote_copy(
             src_ref=src, dst_ref=slot_of(a, half, slot).at[rs],
             send_sem=send_sems.at[k], recv_sem=recv_sems.at[k],
@@ -103,7 +104,7 @@
                 for s in swaps:
                     s.wait_recv()
             for r in range(halves):
-                for a in range(2):
+                for a in range(count):
                     for d in range(2):
                         if not carries(d, step, r):
                             continue
@@ -123,25 +124,28 @@
         c.wait_send()
 
 
-def ring_gather(first, second, axis, outer, inner, ring_on_inner, cid, halves=2):
-    rows, width = first.shape
+def ring_gather(arrays, axis, outer, inner, ring_on_inner, cid, halves=2):
+    rows = arrays[0].shape[0]
+    count = len(arrays)
     ring = inner if ring_on_inner else outer
-    shape = (2, ring, rows, width) if ring_on_inner else (ring, 2, rows, width)
-    n_copies = 2 * ring * 2 * halves * 2
-    f, s = pl.pallas_call(
-        functools.partial(_ring_gather_kernel, axis, outer, inner, ring_on_inner, halves),
-        out_shape=(jax.ShapeDtypeStruct(shape, first.dtype), jax.ShapeDtypeStruct(shape, second.dtype)),
-        in_specs=[pl.BlockSpec(memory_space=pltpu.VMEM)] * 2,
-        out_specs=(pl.BlockSpec(memory_space=pltpu.VMEM), pl.BlockSpec(memory_space=pltpu.VMEM)),
+    shapes = [
+        (2, ring, rows, a.shape[1]) if ring_on_inner else (ring, 2, rows, a.shape[1]) for a in arrays
+    ]
+    n_copies = 2 * ring * 2 * halves * count
+    got = pl.pallas_call(
+        functools.partial(_ring_gather_kernel, axis, outer, inner, ring_on_inner, halves, count),
+        out_shape=tuple(jax.ShapeDtypeStruct(s, a.dtype) for s, a in zip(shapes, arrays)),
+        in_specs=[pl.BlockSpec(memory_space=pltpu.VMEM)] * count,
+        out_specs=tuple(pl.BlockSpec(memory_space=pltpu.VMEM) for _ in arrays),
         scratch_shapes=[
             pltpu.SemaphoreType.DMA((n_copies,)),
             pltpu.SemaphoreType.DMA((n_copies,)),
-            pltpu.SemaphoreType.DMA((2, 2)),
-            pltpu.SemaphoreType.DMA((2,)),
+            pltpu.SemaphoreType.DMA((2, count)),
+            pltpu.SemaphoreType.DMA((count,)),
         ],
         compiler_params=pltpu.CompilerParams(collective_id=cid, has_side_effects=True),
-    )(first, second)
-    return f.reshape(2 * ring * rows, width), s.reshape(2 * ring * rows, width)
+    )(*arrays)
+    return [g.reshape(2 * ring * rows, a.shape[1]) for g, a in zip(got, arrays)]
 
 
 def _ring_sum_kernel(axis, outer, chunks, x_ref, out_ref, send_buf, recv_buf, swap_buf, send_sems, recv_sems, swap_sems):
@@ -240,7 +244,7 @@
     contract_last = (((1,), (1,)), ((), ()))
 
     whole_acts, whole_grad = ring_gather(
-        forward_acts, backward_grad, "tensor", 2, n_tensor // 2, True, 0
+        [forward_acts, backward_grad], "tensor", 2, n_tensor // 2, True, 0
     )
 
     gate_part = jnp.dot(whole_acts, gate_weight, preferred_element_type=jnp.float32)
@@ -259,17 +263,11 @@
     up_pre = summed[:, hidden_width : 2 * hidden_width]
     hidden_grad = summed[:, 2 * hidden_width :]
     hidden_part = (jax.nn.silu(gate_pre) * up_pre).astype(jnp.bfloat16)
-    local_slopes = make_slopes(hidden_grad, stored_gate, stored_up)
-
-    local_rows = jnp.concatenate([hidden_part, local_slopes], axis=1)
-    split = local_rows.shape[1] // 2
-    rows_low, rows_high = ring_gather(
-        local_rows[:, :split], local_rows[:, split:], "pipe", n_pipe // 2, 2, False, 2
-    )
-    rows = jnp.concatenate([rows_low, rows_high], axis=1)
-    hidden = rows[:, :hidden_width]
-    gate_slopes = rows[:, hidden_width : 2 * hidden_width]
-    up_slopes = rows[:, 2 * hidden_width :]
+    local_gate_slope, local_up_slope = make_slopes(hidden_grad, stored_gate, stored_up)
+
+    hidden, gate_slopes, up_slopes = ring_gather(
+        [hidden_part, local_gate_slope, local_up_slope], "pipe", n_pipe // 2, 2, False, 2
+    )
 
     out_part = jnp.dot(hidden, down_weight, preferred_element_type=jnp.float32)
     in_part = lax.dot_general(

time: 193 us -> 193 us (level)
  no operation moved by 1% of the time
where the time goes in v19:
time: 193 us; the launch traced here: 192 us
  Pallas kernels  118 us (61%)
  blocking collectives  54.5 us (28%)
  matrix products  10.9 us (6%)
  other arithmetic  6.94 us (4%)
    pallas_call x2, Pallas kernels, ring_gather(): pl.pallas_call(functools.partial(_ring_gather_kernel, axis, outer, inner,...  62.5 us
    pallas_call x1, Pallas kernels, ring_sum(): pl.pallas_call(functools.partial(_ring_sum_kernel, axis, outer, chunks),...  55.1 us
    all_to_all x1, blocking collectives, scatter_sum_rows(): got = lax.all_to_all(sent, axis, 0, 0, tiled=False)  54.5 us

profile of v19, /device:TPU:32, one launch (start us, length us, event | category | flops | bytes accessed | tf_op | source)
XLA Modules:
  0.0 191.9 jit_solution(2656200707015637231)
XLA Ops:
  0.6 0.0 copy-start
  0.6 35.3 %shard_map.86 = (bf16[2,8,32,1024]{3,2,1,0:T(8,128)(2,1)}, bf16[2,8,32,1024]{3,2,1,0:T(8,128)(2,1)}) custom-call(bf16[32,1024]{1,0:T(8,128)(2,1)} %refs_0_.1, bf16[32,1024]{1,0:T(8,128)(2,1)} %refs_1_.1), custom_call_target="tpu_custom_call" | custom-call | tf_op jit(solution)/shard_map/pallas_call | solution.py:135
  35.9 0.0 copy-start.3
  35.9 0.0 copy-start.7
  35.9 3.2 %fusion.10 = f32[512,896]{1,0:T(8,128)S(1)} fusion(bf16[512,1024]{1,0:T(8,128)(2,1)} %bitcast.22, bf16[1024,896]{1,0:T(8,128)(2,1)} %param.12), kind=kOutput, calls=%fused_computation.18 | convolution fusion | flops 939524096 | bytes 4718592 | tf_op jit(solution)/shard_map/dot_general | solution.py:251
  39.2 0.0 copy-done.3
  39.2 0.0 copy-done.7
  39.2 1.2 fusion.9
  40.5 1.3 fusion.11
  41.8 2.8 %pad_maximum_fusion = f32[512,2688]{1,0:T(8,128)} fusion(f32[512,896]{1,0:T(8,128)S(1)} %fusion.11, f32[512,896]{1,0:T(8,128)S(1)} %fusion.10, f32[512,896]{1,0:T(8,128)S(1)} %fusion.9), kind=kLoop, calls=%fused_computation | loop fusion | flops 2752512 | bytes 11010048 | tf_op jit(solution)/shard_map/concatenate | solution.py:255
  44.5 55.1 %shard_map.87 = f32[64,2688]{1,0:T(8,128)} custom-call(f32[8,64,2688]{2,1,0:T(8,128)} %bitcast.19), custom_call_target="tpu_custom_call" | custom-call | tf_op jit(solution)/shard_map/pallas_call | solution.py:220
  99.7 2.0 %fusion.7 = (bf16[64,896]{1,0:T(8,128)(2,1)}, bf16[64,896]{1,0:T(8,128)(2,1)}, bf16[64,896]{1,0:T(8,128)(2,1)}) fusion(bf16[64,896]{1,0:T(8,128)(2,1)S(1)} %copy-done.1, f32[64,2688]{1,0:T(8,128)} %shard_map.87, bf16[64,896]{1,0:T(8,128)(2,1)S(1)} %copy-done.2), kind=kLoop, calls=%fused_computation.14 | loop fusion | flops 1204224 | bytes 1261568 | tf_op jit(solution)/shard_map/convert_element_type | solution.py:22
  101.7 27.2 %shard_map.88 = (bf16[4,2,64,896]{3,2,1,0:T(8,128)(2,1)}, bf16[4,2,64,896]{3,2,1,0:T(8,128)(2,1)}, bf16[4,2,64,896]{3,2,1,0:T(8,128)(2,1)}) custom-call(bf16[64,896]{1,0:T(8,128)(2,1)} %get-tuple-element.14.refs_0_, bf16[64,896]{1,0:T(8,128)(2,1)} %get-tuple-element.13.refs_1_, bf16[64,896]{1,0:T(8,128)(2,1)} %get-tuple-element.12.refs_2_), custom_call_target="tpu_custom_call" | custom-call | tf_op jit(solution)/shard_map/pallas_call | solution.py:135
  128.9 0.0 copy-start.4
  128.9 2.6 %convolution_convert_fusion = bf16[512,1024]{1,0:T(8,128)(2,1)S(1)} fusion(bf16[512,896]{1,0:T(8,128)(2,1)} %bitcast.26, bf16[896,1024]{1,0:T(8,128)(2,1)S(1)} %copy-done), kind=kOutput, calls=%fused_computation.3 | convolution fusion | flops 940048384 | bytes 3801088 | tf_op jit(solution)/shard_map/dot_general | solution.py:272
  131.5 0.0 copy-start.5
  131.6 1.3 fusion.12
  132.8 0.2 copy-done.5
  133.0 0.2 copy-done.8
  133.3 1.3 add_convert_fusion
  134.6 0.2 pad_maximum_fusion.1
  134.8 54.5 %all_to_all.5 = bf16[16,32,2048]{2,1,0:T(8,128)(2,1)} all-to-all(bf16[16,32,2048]{2,1,0:T(8,128)(2,1)S(1)} %bitcast.20), channel_id=1, replica_groups=mesh['dp'=2,'pipe'=8,'tensor'=16] {'tensor'}, dimensions={0} | all-to-all | bytes 4194304 | tf_op jit(solution)/shard_map/all_to_all | solution.py:29
  189.3 2.0 %reduce_sum.12 = bf16[32,2048]{1,0:T(8,128)(2,1)S(1)} reduce(bf16[16,32,2048]{2,1,0:T(8,128)(2,1)} %all_to_all.5, bf16[]{:T(256)} %constant.6.clone.1), dimensions={0}, to_apply=%region_0.1 | reduce | flops 983040 | bytes 2228226 | tf_op jit(solution)/shard_map/reduce_sum | solution.py:30
  191.2 0.7 fusion.8
  (11 shorter events, 0.0 us)
Async XLA Ops:
  0.6 39.8 %copy-start = (bf16[896,1024]{1,0:T(8,128)(2,1)S(1)}, bf16[896,1024]{1,0:T(8,128)(2,1)}, u32[]{:S(2)}) copy-start(bf16[896,1024]{1,0:T(8,128)(2,1)} %param.13) | copy-start | bytes 5505028
  35.9 3.2 %copy-start.3 = (bf16[1024,896]{1,0:T(8,128)(2,1)S(1)}, bf16[1024,896]{1,0:T(8,128)(2,1)}, u32[]{:S(2)}) copy-start(bf16[1024,896]{1,0:T(8,128)(2,1)} %param.11) | copy-start | bytes 5505028
  35.9 3.2 %copy-start.7 = (bf16[2,8,32,1024]{3,2,1,0:T(8,128)(2,1)S(1)}, bf16[2,8,32,1024]{3,2,1,0:T(8,128)(2,1)}, u32[]{:S(2)}) copy-start(bf16[2,8,32,1024]{3,2,1,0:T(8,128)(2,1)} %get-tuple-element.7) | copy-start | bytes 3145732
  39.2 1.3 copy-start.6
  44.5 55.1 %copy-start.1 = (bf16[64,896]{1,0:T(8,128)(2,1)S(1)}, bf16[64,896]{1,0:T(8,128)(2,1)}, u32[]{:S(2)}) copy-start(bf16[64,896]{1,0:T(8,128)(2,1)} %param.9) | copy-start | bytes 344068
  44.5 55.1 %copy-start.2 = (bf16[64,896]{1,0:T(8,128)(2,1)S(1)}, bf16[64,896]{1,0:T(8,128)(2,1)}, u32[]{:S(2)}) copy-start(bf16[64,896]{1,0:T(8,128)(2,1)} %param.10) | copy-start | bytes 344068
  128.9 2.6 %copy-start.4 = (bf16[1024,896]{1,0:T(8,128)(2,1)S(1)}, bf16[1024,896]{1,0:T(8,128)(2,1)}, u32[]{:S(2)}) copy-start(bf16[1024,896]{1,0:T(8,128)(2,1)} %param.11) | copy-start | bytes 5505028
  128.9 2.6 %copy-start.9 = (bf16[4,2,64,896]{3,2,1,0:T(8,128)(2,1)S(1)}, bf16[4,2,64,896]{3,2,1,0:T(8,128)(2,1)}, u32[]{:S(2)}) copy-start(bf16[4,2,64,896]{3,2,1,0:T(8,128)(2,1)} %get-tuple-element.10) | copy-start | bytes 2752516
  131.5 1.5 copy-start.5
  131.5 1.7 copy-start.8

commit v20 on v19

--- a/solution.py
+++ b/solution.py
@@ -148,7 +148,14 @@
     return [g.reshape(2 * ring * rows, a.shape[1]) for g, a in zip(got, arrays)]
 
 
-def _ring_sum_kernel(axis, outer, chunks, x_ref, out_ref, send_buf, recv_buf, swap_buf, send_sems, recv_sems, swap_sems):
+def _ring_sum_kernel(axis, outer, chunks, count, *refs):
+    xs = refs[:count]
+    outs = refs[count:2 * count]
+    send_bufs = refs[2 * count:3 * count]
+    recv_bufs = refs[3 * count:4 * count]
+    swap_bufs = refs[4 * count:5 * count]
+    held = refs[5 * count:6 * count]
+    send_sems, recv_sems, swap_sems, load_sems = refs[6 * count:]
     me = lax.axis_index(axis)
     y = me // 2
     x = me % 2
@@ -156,9 +163,15 @@
     up = lax.rem(y + 1, ring) * 2 + x
     down = lax.rem(y + ring - 1, ring) * 2 + x
     partner = y * 2 + 1 - x
-    rows = x_ref.shape[1]
+    rows = xs[0].shape[1]
     half = rows // 2
     part = half // chunks
+
+    loads = []
+    for t in range(count):
+        ld = pltpu.make_async_copy(xs[t], held[t], load_sems.at[t])
+        ld.start()
+        loads.append(ld)
 
     barrier = pltpu.get_barrier_semaphore()
     for peer in (partner, up, down):
@@ -174,64 +187,83 @@
     for step in range(1, ring):
         for c in range(chunks):
             for d in range(2):
-                rs = pl.ds(d * half + c * part, part)
-                blocks = pl.ds(dest(d, step) * 2, 2)
-                if step == 1:
-                    src = x_ref.at[blocks, rs]
-                else:
-                    copies[(d, step - 1, c)].wait_recv()
-                    send_buf[d, step, :, pl.ds(c * part, part)] = (
-                        recv_buf[d, step - 1, :, pl.ds(c * part, part)] + x_ref[blocks, rs]
-                    )
-                    src = send_buf.at[d, step, :, pl.ds(c * part, part)]
-                cp = pltpu.make_async_remote_copy(
-                    src_ref=src, dst_ref=recv_buf.at[d, step, :, pl.ds(c * part, part)],
-                    send_sem=send_sems.at[d, step, c], recv_sem=recv_sems.at[d, step, c],
-                    device_id={axis: targets[d]}, device_id_type=MESH)
-                cp.start()
-                copies[(d, step, c)] = cp
+                for t in range(count):
+                    rs = pl.ds(d * half + c * part, part)
+                    local = pl.ds(c * part, part)
+                    blocks = pl.ds(dest(d, step) * 2, 2)
+                    if step == 1:
+                        src = xs[t].at[blocks, rs]
+                    else:
+                        if loads:
+                            for ld in loads:
+                                ld.wait()
+                            loads.clear()
+                        copies[(d, step - 1, c, t)].wait_recv()
+                        send_bufs[t][d, step, :, local] = (
+                            recv_bufs[t][d, step - 1, :, local] + held[t][blocks, rs]
+                        )
+                        src = send_bufs[t].at[d, step, :, local]
+                    cp = pltpu.make_async_remote_copy(
+                        src_ref=src, dst_ref=recv_bufs[t].at[d, step, :, local],
+                        send_sem=send_sems.at[t, d, step, c], recv_sem=recv_sems.at[t, d, step, c],
+                        device_id={axis: targets[d]}, device_id_type=MESH)
+                    cp.start()
+                    copies[(d, step, c, t)] = cp
+    for ld in loads:
+        ld.wait()
     swaps = []
     for c in range(chunks):
         for d in range(2):
-            rs = pl.ds(d * half + c * part, part)
-            local = pl.ds(c * part, part)
-            copies[(d, ring - 1, c)].wait_recv()
-            swap_buf[0, d, local] = recv_buf[d, ring - 1, 1 - x, local] + x_ref[y * 2 + 1 - x, rs]
-            out_ref[rs] = recv_buf[d, ring - 1, x, local] + x_ref[y * 2 + x, rs]
-            sw = pltpu.make_async_remote_copy(
-                src_ref=swap_buf.at[0, d, local], dst_ref=swap_buf.at[1, d, local],
-                send_sem=swap_sems.at[0, d, c], recv_sem=swap_sems.at[1, d, c],
-                device_id={axis: partner}, device_id_type=MESH)
-            sw.start()
-            swaps.append((d, c, sw))
-    for d, c, sw in swaps:
+            for t in range(count):
+                rs = pl.ds(d * half + c * part, part)
+                local = pl.ds(c * part, part)
+                copies[(d, ring - 1, c, t)].wait_recv()
+                swap_bufs[t][0, d, local] = recv_bufs[t][d, ring - 1, 1 - x, local] + held[t][y * 2 + 1 - x, rs]
+                outs[t][rs] = recv_bufs[t][d, ring - 1, x, local] + held[t][y * 2 + x, rs]
+                sw = pltpu.make_async_remote_copy(
+                    src_ref=swap_bufs[t].at[0, d, local], dst_ref=swap_bufs[t].at[1, d, local],
+                    send_sem=swap_sems.at[t, 0, d, c], recv_sem=swap_sems.at[t, 1, d, c],
+                    device_id={axis: partner}, device_id_type=MESH)
+                sw.start()
+                swaps.append((d, c, t, sw))
+    for d, c, t, sw in swaps:
         rs = pl.ds(d * half + c * part, part)
         sw.wait_recv()
-        out_ref[rs] = out_ref[rs] + swap_buf[1, d, pl.ds(c * part, part)]
-    for d, c, sw in swaps:
+        outs[t][rs] = outs[t][rs] + swap_bufs[t][1, d, pl.ds(c * part, part)]
+    for d, c, t, sw in swaps:
         sw.wait_send()
     for cp in copies.values():
         cp.wait_send()
 
 
-def ring_sum(partial, axis, outer, cid, chunks=4):
-    count, rows, width = partial.shape
+def ring_sum(partials, axis, outer, cid, chunks=4):
+    count = len(partials)
+    rows = partials[0].shape[1]
     half = rows // 2
+    scratch = []
+    for kind in range(4):
+        for p in partials:
+            width = p.shape[2]
+            if kind < 2:
+                scratch.append(pltpu.VMEM((2, outer, 2, half, width), jnp.float32))
+            elif kind == 2:
+                scratch.append(pltpu.VMEM((2, 2, half, width), jnp.float32))
+            else:
+                scratch.append(pltpu.VMEM(p.shape, jnp.float32))
+    scratch += [
+        pltpu.SemaphoreType.DMA((count, 2, outer, chunks)),
+        pltpu.SemaphoreType.DMA((count, 2, outer, chunks)),
+        pltpu.SemaphoreType.DMA((count, 2, 2, chunks)),
+        pltpu.SemaphoreType.DMA((count,)),
+    ]
     return pl.pallas_call(
-        functools.partial(_ring_sum_kernel, axis, outer, chunks),
-        out_shape=jax.ShapeDtypeStruct((rows, width), jnp.float32),
-        in_specs=[pl.BlockSpec(memory_space=pltpu.VMEM)],
-        out_specs=pl.BlockSpec(memory_space=pltpu.VMEM),
-        scratch_shapes=[
-            pltpu.VMEM((2, outer, 2, half, width), jnp.float32),
-            pltpu.VMEM((2, outer, 2, half, width), jnp.float32),
-            pltpu.VMEM((2, 2, half, width), jnp.float32),
-            pltpu.SemaphoreType.DMA((2, outer, chunks)),
-            pltpu.SemaphoreType.DMA((2, outer, chunks)),
-            pltpu.SemaphoreType.DMA((2, 2, chunks)),
-        ],
+        functools.partial(_ring_sum_kernel, axis, outer, chunks, count),
+        out_shape=tuple(jax.ShapeDtypeStruct((rows, p.shape[2]), jnp.float32) for p in partials),
+        in_specs=[pl.BlockSpec(memory_space=pl.ANY)] * count,
+        out_specs=tuple(pl.BlockSpec(memory_space=pltpu.VMEM) for _ in partials),
+        scratch_shapes=scratch,
         compiler_params=pltpu.CompilerParams(collective_id=cid, has_side_effects=True, vmem_limit_bytes=60 * 1024 * 1024),
-    )(partial)
+    )(*partials)
 
 
 def per_device(
@@ -252,16 +284,12 @@
     grad_part = lax.dot_general(
         whole_grad, down_weight, contract_last, preferred_element_type=jnp.float32
     )
-    partials = jnp.concatenate([gate_part, up_part, grad_part], axis=1)
-    summed = ring_sum(
-        partials.reshape((n_pipe, partials.shape[0] // n_pipe, partials.shape[1])),
+    gate_pre, up_pre, hidden_grad = ring_sum(
+        [p.reshape((n_pipe, p.shape[0] // n_pipe, p.shape[1])) for p in (gate_part, up_part, grad_part)],
         "pipe",
         n_pipe // 2,
         1,
     )
-    gate_pre = summed[:, :hidden_width]
-    up_pre = summed[:, hidden_width : 2 * hidden_width]
-    hidden_grad = summed[:, 2 * hidden_width :]
     hidden_part = (jax.nn.silu(gate_pre) * up_pre).astype(jnp.bfloat16)
     local_gate_slope, local_up_slope = make_slopes(hidden_grad, stored_gate, stored_up)
 

time: 193 us -> 192 us (level)
  matrix products: 10.9 us -> 14.7 us
  other arithmetic: 6.94 us -> 4.17 us
  Pallas kernels: 118 us -> 116 us
    concatenate x1 -> x0, other arithmetic: 2.77 us -> none  [per_device(): partials = jnp.concatenate([gate_part, up_part, grad_part], axis=1)]
where the time goes in v20:
time: 192 us; the launch traced here: 191 us
  Pallas kernels  116 us (60%)
  blocking collectives  53.9 us (28%)
  matrix products  14.7 us (8%)
  other arithmetic  4.17 us (2%)
    pallas_call x2, Pallas kernels, ring_gather(): pl.pallas_call(functools.partial(_ring_gather_kernel, axis, outer, inner,...  62.8 us
    all_to_all x1, blocking collectives, scatter_sum_rows(): got = lax.all_to_all(sent, axis, 0, 0, tiled=False)  53.9 us
    pallas_call x1, Pallas kernels, ring_sum(): pl.pallas_call(functools.partial(_ring_sum_kernel, axis, outer, chunks, c...  53.3 us
    dot_general x1, matrix products, per_device(): up_part = jnp.dot(whole_acts, up_weight, preferred_element_type=jnp.float32)  4.47 us

profile of v20, /device:TPU:32, one launch (start us, length us, event | category | flops | bytes accessed | tf_op | source)
XLA Modules:
  0.0 190.7 jit_solution(4469325592163872530)
XLA Ops:
  0.6 0.0 copy-start
  0.6 35.3 %shard_map.86 = (bf16[2,8,32,1024]{3,2,1,0:T(8,128)(2,1)}, bf16[2,8,32,1024]{3,2,1,0:T(8,128)(2,1)}) custom-call(bf16[32,1024]{1,0:T(8,128)(2,1)} %refs_0_.1, bf16[32,1024]{1,0:T(8,128)(2,1)} %refs_1_.1), custom_call_target="tpu_custom_call" | custom-call | tf_op jit(solution)/shard_map/pallas_call | solution.py:135
  35.9 0.0 copy-start.3
  35.9 4.5 %fusion.2.refs_1_ = f32[8,64,896]{2,1,0:T(8,128)} fusion(bf16[8,64,1024]{2,1,0:T(8,128)(2,1)} %bitcast.26, bf16[1024,896]{1,0:T(8,128)(2,1)} %param.12), kind=kOutput, calls=%fused_computation.4 | convolution fusion | flops 939524096 | bytes 4718592 | tf_op jit(solution)/shard_map/dot_general | solution.py:283
  40.4 0.0 copy-done.3
  40.4 2.5 %fusion.4.refs_0_ = f32[8,64,896]{2,1,0:T(8,128)} fusion(bf16[8,64,1024]{2,1,0:T(8,128)(2,1)S(1)} %bitcast.27, bf16[1024,896]{1,0:T(8,128)(2,1)S(1)} %copy-done.3), kind=kOutput, calls=%fused_computation.6 | convolution fusion | flops 939524096 | bytes 4718592 | tf_op jit(solution)/shard_map/dot_general | solution.py:282
  42.9 2.6 %fusion.refs_2_ = f32[8,64,896]{2,1,0:T(8,128)} fusion(bf16[8,64,1024]{2,1,0:T(8,128)(2,1)S(1)} %bitcast.25, bf16[896,1024]{1,0:T(8,128)(2,1)S(1)} %copy-done), kind=kOutput, calls=%fused_computation.2 | convolution fusion | flops 939524096 | bytes 4718592 | tf_op jit(solution)/shard_map/dot_general | solution.py:284
  45.5 53.3 %shard_map.87 = (f32[64,896]{1,0:T(8,128)}, f32[64,896]{1,0:T(8,128)}, f32[64,896]{1,0:T(8,128)}) custom-call(f32[8,64,896]{2,1,0:T(8,128)} %fusion.4.refs_0_, f32[8,64,896]{2,1,0:T(8,128)} %fusion.2.refs_1_, f32[8,64,896]{2,1,0:T(8,128)} %fusion.refs_2_), custom_call_target="tpu_custom_call" | custom-call | tf_op jit(solution)/shard_map/pallas_call | solution.py:259
  98.8 0.0 copy-done.1
  98.8 0.0 copy-done.2
  98.8 2.0 %fusion.13 = (bf16[64,896]{1,0:T(8,128)(2,1)}, bf16[64,896]{1,0:T(8,128)(2,1)}, bf16[64,896]{1,0:T(8,128)(2,1)}) fusion(f32[64,896]{1,0:T(8,128)} %get-tuple-element.14, bf16[64,896]{1,0:T(8,128)(2,1)S(1)} %copy-done.1, bf16[64,896]{1,0:T(8,128)(2,1)S(1)} %copy-done.2, f32[64,896]{1,0:T(8,128)} %get-tuple-element.13, f32[64,896]{1,0:T(8,128)} %get-tuple-element.12), kind=kLoop, calls=%fused_computation.19 | loop fusion | flops 1204224 | bytes 1261568 | tf_op jit(solution)/shard_map/convert_element_type | solution.py:22
  100.8 27.5 %shard_map.88 = (bf16[4,2,64,896]{3,2,1,0:T(8,128)(2,1)}, bf16[4,2,64,896]{3,2,1,0:T(8,128)(2,1)}, bf16[4,2,64,896]{3,2,1,0:T(8,128)(2,1)}) custom-call(bf16[64,896]{1,0:T(8,128)(2,1)} %get-tuple-element.22.refs_0_, bf16[64,896]{1,0:T(8,128)(2,1)} %get-tuple-element.19.refs_1_, bf16[64,896]{1,0:T(8,128)(2,1)} %get-tuple-element.18.refs_2_), custom_call_target="tpu_custom_call" | custom-call | tf_op jit(solution)/shard_map/pallas_call | solution.py:135
  128.4 0.0 copy-start.4
  128.4 2.6 %convolution_convert_fusion = bf16[512,1024]{1,0:T(8,128)(2,1)S(1)} fusion(bf16[512,896]{1,0:T(8,128)(2,1)} %bitcast.30, bf16[896,1024]{1,0:T(8,128)(2,1)S(1)} %copy-done), kind=kOutput, calls=%fused_computation.8 | convolution fusion | flops 940048384 | bytes 3801088 | tf_op jit(solution)/shard_map/dot_general | solution.py:300
  131.0 0.0 copy-done.4
  131.0 0.0 copy-start.5
  131.0 1.3 fusion.15
  132.3 0.2 copy-done.5
  132.5 0.2 copy-done.8
  132.7 1.3 add_convert_fusion
  134.0 0.2 pad_maximum_fusion
  134.2 53.9 %all_to_all.5 = bf16[16,32,2048]{2,1,0:T(8,128)(2,1)} all-to-all(bf16[16,32,2048]{2,1,0:T(8,128)(2,1)S(1)} %bitcast.24), channel_id=1, replica_groups=mesh['dp'=2,'pipe'=8,'tensor'=16] {'tensor'}, dimensions={0} | all-to-all | bytes 4194304 | tf_op jit(solution)/shard_map/all_to_all | solution.py:29
  188.1 2.0 %reduce_sum.12 = bf16[32,2048]{1,0:T(8,128)(2,1)S(1)} reduce(bf16[16,32,2048]{2,1,0:T(8,128)(2,1)} %all_to_all.5, bf16[]{:T(256)} %constant.6.clone.1), dimensions={0}, to_apply=%region_0.1 | reduce | flops 983040 | bytes 2228226 | tf_op jit(solution)/shard_map/reduce_sum | solution.py:30
  190.1 0.7 fusion.14
  (10 shorter events, 0.0 us)
Async XLA Ops:
  0.6 42.3 %copy-start = (bf16[896,1024]{1,0:T(8,128)(2,1)S(1)}, bf16[896,1024]{1,0:T(8,128)(2,1)}, u32[]{:S(2)}) copy-start(bf16[896,1024]{1,0:T(8,128)(2,1)} %param.13) | copy-start | bytes 5505028
  35.9 4.5 %copy-start.3 = (bf16[1024,896]{1,0:T(8,128)(2,1)S(1)}, bf16[1024,896]{1,0:T(8,128)(2,1)}, u32[]{:S(2)}) copy-start(bf16[1024,896]{1,0:T(8,128)(2,1)} %param.11) | copy-start | bytes 5505028
  35.9 4.5 %copy-start.7 = (bf16[2,8,32,1024]{3,2,1,0:T(8,128)(2,1)S(1)}, bf16[2,8,32,1024]{3,2,1,0:T(8,128)(2,1)}, u32[]{:S(2)}) copy-start(bf16[2,8,32,1024]{3,2,1,0:T(8,128)(2,1)} %get-tuple-element.10) | copy-start | bytes 3145732
  40.4 2.5 %copy-start.6 = (bf16[2,8,32,1024]{3,2,1,0:T(8,128)(2,1)S(1)}, bf16[2,8,32,1024]{3,2,1,0:T(8,128)(2,1)}, u32[]{:S(2)}) copy-start(bf16[2,8,32,1024]{3,2,1,0:T(8,128)(2,1)} %get-tuple-element.11) | copy-start | bytes 3145732
  45.5 53.4 %copy-start.1 = (bf16[64,896]{1,0:T(8,128)(2,1)S(1)}, bf16[64,896]{1,0:T(8,128)(2,1)}, u32[]{:S(2)}) copy-start(bf16[64,896]{1,0:T(8,128)(2,1)} %param.9) | copy-start | bytes 344068
  45.5 53.4 %copy-start.2 = (bf16[64,896]{1,0:T(8,128)(2,1)S(1)}, bf16[64,896]{1,0:T(8,128)(2,1)}, u32[]{:S(2)}) copy-start(bf16[64,896]{1,0:T(8,128)(2,1)} %param.10) | copy-start | bytes 344068
  128.4 2.6 %copy-start.4 = (bf16[1024,896]{1,0:T(8,128)(2,1)S(1)}, bf16[1024,896]{1,0:T(8,128)(2,1)}, u32[]{:S(2)}) copy-start(bf16[1024,896]{1,0:T(8,128)(2,1)} %param.11) | copy-start | bytes 5505028
  128.4 2.6 %copy-start.9 = (bf16[4,2,64,896]{3,2,1,0:T(8,128)(2,1)S(1)}, bf16[4,2,64,896]{3,2,1,0:T(8,128)(2,1)}, u32[]{:S(2)}) copy-start(bf16[4,2,64,896]{3,2,1,0:T(8,128)(2,1)} %get-tuple-element.16) | copy-start | bytes 2752516
  131.0 1.5 copy-start.5
  131.0 1.7 copy-start.8

commit v21 on v20

--- a/solution.py
+++ b/solution.py
@@ -294,7 +294,7 @@
     local_gate_slope, local_up_slope = make_slopes(hidden_grad, stored_gate, stored_up)
 
     hidden, gate_slopes, up_slopes = ring_gather(
-        [hidden_part, local_gate_slope, local_up_slope], "pipe", n_pipe // 2, 2, False, 2
+        [hidden_part, local_gate_slope, local_up_slope], "pipe", n_pipe // 2, 2, False, 2, halves=4
     )
 
     out_part = jnp.dot(hidden, down_weight, preferred_element_type=jnp.float32)

time: 192 us -> 193 us (level)
  Pallas kernels: 116 us -> 118 us
where the time goes in v21:
time: 193 us
  Pallas kernels  118 us (61%)
  blocking collectives  53.9 us (28%)
  matrix products  14.7 us (8%)
  other arithmetic  4.17 us (2%)
    pallas_call x2, Pallas kernels, ring_gather(): pl.pallas_call(functools.partial(_ring_gather_kernel, axis, outer, inner,...  64.5 us
    all_to_all x1, blocking collectives, scatter_sum_rows(): got = lax.all_to_all(sent, axis, 0, 0, tiled=False)  53.9 us
    pallas_call x1, Pallas kernels, ring_sum(): pl.pallas_call(functools.partial(_ring_sum_kernel, axis, outer, chunks, c...  53.3 us
    dot_general x1, matrix products, per_device(): up_part = jnp.dot(whole_acts, up_weight, preferred_element_type=jnp.float32)  4.47 us

profile of v21, /device:TPU:32, one launch (start us, length us, event | category | flops | bytes accessed | tf_op | source)
XLA Modules:
  0.0 192.5 jit_solution(5641156953530853913)
XLA Ops:
  0.6 0.0 copy-start
  0.6 35.3 %shard_map.86 = (bf16[2,8,32,1024]{3,2,1,0:T(8,128)(2,1)}, bf16[2,8,32,1024]{3,2,1,0:T(8,128)(2,1)}) custom-call(bf16[32,1024]{1,0:T(8,128)(2,1)} %refs_0_.1, bf16[32,1024]{1,0:T(8,128)(2,1)} %refs_1_.1), custom_call_target="tpu_custom_call" | custom-call | tf_op jit(solution)/shard_map/pallas_call | solution.py:135
  35.9 0.0 copy-start.3
  35.9 4.5 %fusion.2.refs_1_ = f32[8,64,896]{2,1,0:T(8,128)} fusion(bf16[8,64,1024]{2,1,0:T(8,128)(2,1)} %bitcast.26, bf16[1024,896]{1,0:T(8,128)(2,1)} %param.12), kind=kOutput, calls=%fused_computation.4 | convolution fusion | flops 939524096 | bytes 4718592 | tf_op jit(solution)/shard_map/dot_general | solution.py:283
  40.4 0.0 copy-done.3
  40.4 2.5 %fusion.4.refs_0_ = f32[8,64,896]{2,1,0:T(8,128)} fusion(bf16[8,64,1024]{2,1,0:T(8,128)(2,1)S(1)} %bitcast.27, bf16[1024,896]{1,0:T(8,128)(2,1)S(1)} %copy-done.3), kind=kOutput, calls=%fused_computation.6 | convolution fusion | flops 939524096 | bytes 4718592 | tf_op jit(solution)/shard_map/dot_general | solution.py:282
  42.9 2.6 %fusion.refs_2_ = f32[8,64,896]{2,1,0:T(8,128)} fusion(bf16[8,64,1024]{2,1,0:T(8,128)(2,1)S(1)} %bitcast.25, bf16[896,1024]{1,0:T(8,128)(2,1)S(1)} %copy-done), kind=kOutput, calls=%fused_computation.2 | convolution fusion | flops 939524096 | bytes 4718592 | tf_op jit(solution)/shard_map/dot_general | solution.py:284
  45.5 53.3 %shard_map.87 = (f32[64,896]{1,0:T(8,128)}, f32[64,896]{1,0:T(8,128)}, f32[64,896]{1,0:T(8,128)}) custom-call(f32[8,64,896]{2,1,0:T(8,128)} %fusion.4.refs_0_, f32[8,64,896]{2,1,0:T(8,128)} %fusion.2.refs_1_, f32[8,64,896]{2,1,0:T(8,128)} %fusion.refs_2_), custom_call_target="tpu_custom_call" | custom-call | tf_op jit(solution)/shard_map/pallas_call | solution.py:259
  98.8 0.0 copy-done.1
  98.8 0.0 copy-done.2
  98.8 2.0 %fusion.13 = (bf16[64,896]{1,0:T(8,128)(2,1)}, bf16[64,896]{1,0:T(8,128)(2,1)}, bf16[64,896]{1,0:T(8,128)(2,1)}) fusion(f32[64,896]{1,0:T(8,128)} %get-tuple-element.14, bf16[64,896]{1,0:T(8,128)(2,1)S(1)} %copy-done.1, bf16[64,896]{1,0:T(8,128)(2,1)S(1)} %copy-done.2, f32[64,896]{1,0:T(8,128)} %get-tuple-element.13, f32[64,896]{1,0:T(8,128)} %get-tuple-element.12), kind=kLoop, calls=%fused_computation.19 | loop fusion | flops 1204224 | bytes 1261568 | tf_op jit(solution)/shard_map/convert_element_type | solution.py:22
  100.8 29.3 %shard_map.88 = (bf16[4,2,64,896]{3,2,1,0:T(8,128)(2,1)}, bf16[4,2,64,896]{3,2,1,0:T(8,128)(2,1)}, bf16[4,2,64,896]{3,2,1,0:T(8,128)(2,1)}) custom-call(bf16[64,896]{1,0:T(8,128)(2,1)} %get-tuple-element.22.refs_0_, bf16[64,896]{1,0:T(8,128)(2,1)} %get-tuple-element.19.refs_1_, bf16[64,896]{1,0:T(8,128)(2,1)} %get-tuple-element.18.refs_2_), custom_call_target="tpu_custom_call" | custom-call | tf_op jit(solution)/shard_map/pallas_call | solution.py:135
  130.1 0.0 copy-start.4
  130.2 2.6 %convolution_convert_fusion = bf16[512,1024]{1,0:T(8,128)(2,1)S(1)} fusion(bf16[512,896]{1,0:T(8,128)(2,1)} %bitcast.30, bf16[896,1024]{1,0:T(8,128)(2,1)S(1)} %copy-done), kind=kOutput, calls=%fused_computation.8 | convolution fusion | flops 940048384 | bytes 3801088 | tf_op jit(solution)/shard_map/dot_general | solution.py:300
  132.8 0.0 copy-start.5
  132.8 0.0 copy-start.8
  132.8 1.3 fusion.15
  134.1 0.2 copy-done.5
  134.3 0.2 copy-done.8
  134.5 1.3 add_convert_fusion
  135.8 0.2 pad_maximum_fusion
  136.0 53.9 %all_to_all.5 = bf16[16,32,2048]{2,1,0:T(8,128)(2,1)} all-to-all(bf16[16,32,2048]{2,1,0:T(8,128)(2,1)S(1)} %bitcast.24), channel_id=1, replica_groups=mesh['dp'=2,'pipe'=8,'tensor'=16] {'tensor'}, dimensions={0} | all-to-all | bytes 4194304 | tf_op jit(solution)/shard_map/all_to_all | solution.py:29
  189.9 2.0 %reduce_sum.12 = bf16[32,2048]{1,0:T(8,128)(2,1)S(1)} reduce(bf16[16,32,2048]{2,1,0:T(8,128)(2,1)} %all_to_all.5, bf16[]{:T(256)} %constant.6.clone.1), dimensions={0}, to_apply=%region_0.1 | reduce | flops 983040 | bytes 2228226 | tf_op jit(solution)/shard_map/reduce_sum | solution.py:30
  191.9 0.7 fusion.14
  (10 shorter events, 0.0 us)
Async XLA Ops:
  0.6 42.3 %copy-start = (bf16[896,1024]{1,0:T(8,128)(2,1)S(1)}, bf16[896,1024]{1,0:T(8,128)(2,1)}, u32[]{:S(2)}) copy-start(bf16[896,1024]{1,0:T(8,128)(2,1)} %param.13) | copy-start | bytes 5505028
  35.9 4.5 %copy-start.3 = (bf16[1024,896]{1,0:T(8,128)(2,1)S(1)}, bf16[1024,896]{1,0:T(8,128)(2,1)}, u32[]{:S(2)}) copy-start(bf16[1024,896]{1,0:T(8,128)(2,1)} %param.11) | copy-start | bytes 5505028
  35.9 4.5 %copy-start.7 = (bf16[2,8,32,1024]{3,2,1,0:T(8,128)(2,1)S(1)}, bf16[2,8,32,1024]{3,2,1,0:T(8,128)(2,1)}, u32[]{:S(2)}) copy-start(bf16[2,8,32,1024]{3,2,1,0:T(8,128)(2,1)} %get-tuple-element.10) | copy-start | bytes 3145732
  40.4 2.5 %copy-start.6 = (bf16[2,8,32,1024]{3,2,1,0:T(8,128)(2,1)S(1)}, bf16[2,8,32,1024]{3,2,1,0:T(8,128)(2,1)}, u32[]{:S(2)}) copy-start(bf16[2,8,32,1024]{3,2,1,0:T(8,128)(2,1)} %get-tuple-element.11) | copy-start | bytes 3145732
  45.5 53.4 %copy-start.1 = (bf16[64,896]{1,0:T(8,128)(2,1)S(1)}, bf16[64,896]{1,0:T(8,128)(2,1)}, u32[]{:S(2)}) copy-start(bf16[64,896]{1,0:T(8,128)(2,1)} %param.9) | copy-start | bytes 344068
  45.5 53.4 %copy-start.2 = (bf16[64,896]{1,0:T(8,128)(2,1)S(1)}, bf16[64,896]{1,0:T(8,128)(2,1)}, u32[]{:S(2)}) copy-start(bf16[64,896]{1,0:T(8,128)(2,1)} %param.10) | copy-start | bytes 344068
  130.1 2.6 %copy-start.4 = (bf16[1024,896]{1,0:T(8,128)(2,1)S(1)}, bf16[1024,896]{1,0:T(8,128)(2,1)}, u32[]{:S(2)}) copy-start(bf16[1024,896]{1,0:T(8,128)(2,1)} %param.11) | copy-start | bytes 5505028
  130.2 2.6 %copy-start.9 = (bf16[4,2,64,896]{3,2,1,0:T(8,128)(2,1)S(1)}, bf16[4,2,64,896]{3,2,1,0:T(8,128)(2,1)}, u32[]{:S(2)}) copy-start(bf16[4,2,64,896]{3,2,1,0:T(8,128)(2,1)} %get-tuple-element.16) | copy-start | bytes 2752516
  132.8 1.5 copy-start.5
  132.8 1.7 copy-start.8

commit v22 on v20

--- a/solution.py
+++ b/solution.py
@@ -135,8 +135,8 @@
     got = pl.pallas_call(
         functools.partial(_ring_gather_kernel, axis, outer, inner, ring_on_inner, halves, count),
         out_shape=tuple(jax.ShapeDtypeStruct(s, a.dtype) for s, a in zip(shapes, arrays)),
-        in_specs=[pl.BlockSpec(memory_space=pltpu.VMEM)] * count,
-        out_specs=tuple(pl.BlockSpec(memory_space=pltpu.VMEM) for _ in arrays),
+        in_specs=[pl.BlockSpec(memory_space=pl.ANY)] * count,
+        out_specs=tuple(pl.BlockSpec(memory_space=pl.ANY) for _ in arrays),
         scratch_shapes=[
             pltpu.SemaphoreType.DMA((n_copies,)),
             pltpu.SemaphoreType.DMA((n_copies,)),

time: 192 us -> 187 us (0.974)
  Pallas kernels: 116 us -> 112 us
    pallas_call x2, Pallas kernels: 62.8 us -> 59.4 us  [ring_gather(): pl.pallas_call(functools.partial(_ring_gather_kernel, axis, outer, inner,...]
where the time goes in v22:
time: 187 us
  Pallas kernels  112 us (60%)
  blocking collectives  53.6 us (29%)
  matrix products  14.7 us (8%)
  other arithmetic  4.17 us (2%)
    pallas_call x2, Pallas kernels, ring_gather(): pl.pallas_call(functools.partial(_ring_gather_kernel, axis, outer, inner,...  59.4 us
    all_to_all x1, blocking collectives, scatter_sum_rows(): got = lax.all_to_all(sent, axis, 0, 0, tiled=False)  53.6 us
    pallas_call x1, Pallas kernels, ring_sum(): pl.pallas_call(functools.partial(_ring_sum_kernel, axis, outer, chunks, c...  53.1 us
    dot_general x1, matrix products, per_device(): up_part = jnp.dot(whole_acts, up_weight, preferred_element_type=jnp.float32)  4.47 us

profile of v22, /device:TPU:32, one launch (start us, length us, event | category | flops | bytes accessed | tf_op | source)
XLA Modules:
  0.0 186.8 jit_solution(17792749242416566184)
XLA Ops:
  0.6 0.0 copy-start
  0.6 33.9 %shard_map.86 = (bf16[2,8,32,1024]{3,2,1,0:T(8,128)(2,1)}, bf16[2,8,32,1024]{3,2,1,0:T(8,128)(2,1)}) custom-call(bf16[32,1024]{1,0:T(8,128)(2,1)} %refs_0_.1, bf16[32,1024]{1,0:T(8,128)(2,1)} %refs_1_.1), custom_call_target="tpu_custom_call" | custom-call | tf_op jit(solution)/shard_map/pallas_call | solution.py:135
  34.6 0.0 copy-start.3
  34.6 0.0 copy-start.7
  34.6 4.5 %fusion.2.refs_1_ = f32[8,64,896]{2,1,0:T(8,128)} fusion(bf16[8,64,1024]{2,1,0:T(8,128)(2,1)} %bitcast.26, bf16[1024,896]{1,0:T(8,128)(2,1)} %param.12), kind=kOutput, calls=%fused_computation.4 | convolution fusion | flops 939524096 | bytes 4718592 | tf_op jit(solution)/shard_map/dot_general | solution.py:283
  39.1 0.0 copy-done.3
  39.1 0.0 copy-done.7
  39.1 2.5 %fusion.4.refs_0_ = f32[8,64,896]{2,1,0:T(8,128)} fusion(bf16[8,64,1024]{2,1,0:T(8,128)(2,1)S(1)} %bitcast.27, bf16[1024,896]{1,0:T(8,128)(2,1)S(1)} %copy-done.3), kind=kOutput, calls=%fused_computation.6 | convolution fusion | flops 939524096 | bytes 4718592 | tf_op jit(solution)/shard_map/dot_general | solution.py:282
  41.6 0.0 copy-done
  41.6 2.6 %fusion.refs_2_ = f32[8,64,896]{2,1,0:T(8,128)} fusion(bf16[8,64,1024]{2,1,0:T(8,128)(2,1)S(1)} %bitcast.25, bf16[896,1024]{1,0:T(8,128)(2,1)S(1)} %copy-done), kind=kOutput, calls=%fused_computation.2 | convolution fusion | flops 939524096 | bytes 4718592 | tf_op jit(solution)/shard_map/dot_general | solution.py:284
  44.1 53.1 %shard_map.87 = (f32[64,896]{1,0:T(8,128)}, f32[64,896]{1,0:T(8,128)}, f32[64,896]{1,0:T(8,128)}) custom-call(f32[8,64,896]{2,1,0:T(8,128)} %fusion.4.refs_0_, f32[8,64,896]{2,1,0:T(8,128)} %fusion.2.refs_1_, f32[8,64,896]{2,1,0:T(8,128)} %fusion.refs_2_), custom_call_target="tpu_custom_call" | custom-call | tf_op jit(solution)/shard_map/pallas_call | solution.py:259
  97.3 2.0 %fusion.13 = (bf16[64,896]{1,0:T(8,128)(2,1)}, bf16[64,896]{1,0:T(8,128)(2,1)}, bf16[64,896]{1,0:T(8,128)(2,1)}) fusion(f32[64,896]{1,0:T(8,128)} %get-tuple-element.14, bf16[64,896]{1,0:T(8,128)(2,1)S(1)} %copy-done.1, bf16[64,896]{1,0:T(8,128)(2,1)S(1)} %copy-done.2, f32[64,896]{1,0:T(8,128)} %get-tuple-element.13, f32[64,896]{1,0:T(8,128)} %get-tuple-element.12), kind=kLoop, calls=%fused_computation.19 | loop fusion | flops 1204224 | bytes 1261568 | tf_op jit(solution)/shard_map/convert_element_type | solution.py:22
  99.3 25.4 %shard_map.88 = (bf16[4,2,64,896]{3,2,1,0:T(8,128)(2,1)}, bf16[4,2,64,896]{3,2,1,0:T(8,128)(2,1)}, bf16[4,2,64,896]{3,2,1,0:T(8,128)(2,1)}) custom-call(bf16[64,896]{1,0:T(8,128)(2,1)} %get-tuple-element.22.refs_0_, bf16[64,896]{1,0:T(8,128)(2,1)} %get-tuple-element.19.refs_1_, bf16[64,896]{1,0:T(8,128)(2,1)} %get-tuple-element.18.refs_2_), custom_call_target="tpu_custom_call" | custom-call | tf_op jit(solution)/shard_map/pallas_call | solution.py:135
  124.7 0.0 copy-start.4
  124.7 2.6 %convolution_convert_fusion = bf16[512,1024]{1,0:T(8,128)(2,1)S(1)} fusion(bf16[512,896]{1,0:T(8,128)(2,1)} %bitcast.30, bf16[896,1024]{1,0:T(8,128)(2,1)S(1)} %copy-done), kind=kOutput, calls=%fused_computation.8 | convolution fusion | flops 940048384 | bytes 3801088 | tf_op jit(solution)/shard_map/dot_general | solution.py:300
  127.3 0.0 copy-start.5
  127.4 1.3 fusion.15
  128.6 0.2 copy-done.5
  128.8 0.2 copy-done.8
  129.1 1.3 add_convert_fusion
  130.4 0.2 pad_maximum_fusion
  130.6 53.6 %all_to_all.5 = bf16[16,32,2048]{2,1,0:T(8,128)(2,1)} all-to-all(bf16[16,32,2048]{2,1,0:T(8,128)(2,1)S(1)} %bitcast.24), channel_id=1, replica_groups=mesh['dp'=2,'pipe'=8,'tensor'=16] {'tensor'}, dimensions={0} | all-to-all | bytes 4194304 | tf_op jit(solution)/shard_map/all_to_all | solution.py:29
  184.2 2.0 %reduce_sum.12 = bf16[32,2048]{1,0:T(8,128)(2,1)S(1)} reduce(bf16[16,32,2048]{2,1,0:T(8,128)(2,1)} %all_to_all.5, bf16[]{:T(256)} %constant.6.clone.1), dimensions={0}, to_apply=%region_0.1 | reduce | flops 983040 | bytes 2228226 | tf_op jit(solution)/shard_map/reduce_sum | solution.py:30
  186.2 0.7 fusion.14
  (10 shorter events, 0.0 us)
Async XLA Ops:
  0.6 41.0 %copy-start = (bf16[896,1024]{1,0:T(8,128)(2,1)S(1)}, bf16[896,1024]{1,0:T(8,128)(2,1)}, u32[]{:S(2)}) copy-start(bf16[896,1024]{1,0:T(8,128)(2,1)} %param.13) | copy-start | bytes 5505028
  34.6 4.5 %copy-start.3 = (bf16[1024,896]{1,0:T(8,128)(2,1)S(1)}, bf16[1024,896]{1,0:T(8,128)(2,1)}, u32[]{:S(2)}) copy-start(bf16[1024,896]{1,0:T(8,128)(2,1)} %param.11) | copy-start | bytes 5505028
  34.6 4.5 %copy-start.7 = (bf16[2,8,32,1024]{3,2,1,0:T(8,128)(2,1)S(1)}, bf16[2,8,32,1024]{3,2,1,0:T(8,128)(2,1)}, u32[]{:S(2)}) copy-start(bf16[2,8,32,1024]{3,2,1,0:T(8,128)(2,1)} %get-tuple-element.10) | copy-start | bytes 3145732
  39.1 2.5 %copy-start.6 = (bf16[2,8,32,1024]{3,2,1,0:T(8,128)(2,1)S(1)}, bf16[2,8,32,1024]{3,2,1,0:T(8,128)(2,1)}, u32[]{:S(2)}) copy-start(bf16[2,8,32,1024]{3,2,1,0:T(8,128)(2,1)} %get-tuple-element.11) | copy-start | bytes 3145732
  44.1 53.1 %copy-start.1 = (bf16[64,896]{1,0:T(8,128)(2,1)S(1)}, bf16[64,896]{1,0:T(8,128)(2,1)}, u32[]{:S(2)}) copy-start(bf16[64,896]{1,0:T(8,128)(2,1)} %param.9) | copy-start | bytes 344068
  44.1 53.1 %copy-start.2 = (bf16[64,896]{1,0:T(8,128)(2,1)S(1)}, bf16[64,896]{1,0:T(8,128)(2,1)}, u32[]{:S(2)}) copy-start(bf16[64,896]{1,0:T(8,128)(2,1)} %param.10) | copy-start | bytes 344068
  124.7 2.6 %copy-start.4 = (bf16[1024,896]{1,0:T(8,128)(2,1)S(1)}, bf16[1024,896]{1,0:T(8,128)(2,1)}, u32[]{:S(2)}) copy-start(bf16[1024,896]{1,0:T(8,128)(2,1)} %param.11) | copy-start | bytes 5505028
  124.7 2.6 %copy-start.9 = (bf16[4,2,64,896]{3,2,1,0:T(8,128)(2,1)S(1)}, bf16[4,2,64,896]{3,2,1,0:T(8,128)(2,1)}, u32[]{:S(2)}) copy-start(bf16[4,2,64,896]{3,2,1,0:T(8,128)(2,1)} %get-tuple-element.16) | copy-start | bytes 2752516
  127.3 1.5 copy-start.5
  127.4 1.7 copy-start.8

commit v23 on v22

--- a/solution.py
+++ b/solution.py
@@ -27,6 +27,9 @@
     rows = partial.shape[0] // count
     sent = partial.reshape((count, rows) + partial.shape[1:]).astype(link_dtype)
     got = lax.all_to_all(sent, axis, 0, 0, tiled=False)
+    if count % 4 == 0:
+        grouped = got.reshape((count // 4, 4) + got.shape[1:]).astype(jnp.float32).sum(axis=1)
+        return lax.optimization_barrier(grouped).sum(axis=0)
     return got.astype(jnp.float32).sum(axis=0)
 
 

time: 187 us -> 185 us (0.989)
  no operation moved by 1% of the time
where the time goes in v23:
time: 185 us
  Pallas kernels  112 us (61%)
  blocking collectives  53.5 us (29%)
  matrix products  14.7 us (8%)
  other arithmetic  2.63 us (1%)
    pallas_call x2, Pallas kernels, ring_gather(): pl.pallas_call(functools.partial(_ring_gather_kernel, axis, outer, inner,...  59.4 us
    all_to_all x1, blocking collectives, scatter_sum_rows(): got = lax.all_to_all(sent, axis, 0, 0, tiled=False)  53.5 us
    pallas_call x1, Pallas kernels, ring_sum(): pl.pallas_call(functools.partial(_ring_sum_kernel, axis, outer, chunks, c...  53.1 us
    dot_general x1, matrix products, per_device(): up_part = jnp.dot(whole_acts, up_weight, preferred_element_type=jnp.float32)  4.46 us

profile of v23, /device:TPU:32, one launch (start us, length us, event | category | flops | bytes accessed | tf_op | source)
XLA Modules:
  0.0 185.2 jit_solution(1920709458594938690)
XLA Ops:
  0.6 0.0 copy-start
  0.6 33.9 %shard_map.86 = (bf16[2,8,32,1024]{3,2,1,0:T(8,128)(2,1)}, bf16[2,8,32,1024]{3,2,1,0:T(8,128)(2,1)}) custom-call(bf16[32,1024]{1,0:T(8,128)(2,1)} %refs_0_.1, bf16[32,1024]{1,0:T(8,128)(2,1)} %refs_1_.1), custom_call_target="tpu_custom_call" | custom-call | tf_op jit(solution)/shard_map/pallas_call | solution.py:138
  34.6 0.0 copy-start.3
  34.6 0.0 copy-start.7
  34.6 4.5 %fusion.2.refs_1_ = f32[8,64,896]{2,1,0:T(8,128)} fusion(bf16[8,64,1024]{2,1,0:T(8,128)(2,1)} %bitcast.29, bf16[1024,896]{1,0:T(8,128)(2,1)} %param.12), kind=kOutput, calls=%fused_computation.5 | convolution fusion | flops 939524096 | bytes 4718592 | tf_op jit(solution)/shard_map/dot_general | solution.py:286
  39.1 0.0 copy-done.3
  39.1 2.5 %fusion.4.refs_0_ = f32[8,64,896]{2,1,0:T(8,128)} fusion(bf16[8,64,1024]{2,1,0:T(8,128)(2,1)S(1)} %bitcast.30, bf16[1024,896]{1,0:T(8,128)(2,1)S(1)} %copy-done.3), kind=kOutput, calls=%fused_computation.7 | convolution fusion | flops 939524096 | bytes 4718592 | tf_op jit(solution)/shard_map/dot_general | solution.py:285
  41.6 0.0 copy-done.6
  41.6 2.6 %fusion.refs_2_ = f32[8,64,896]{2,1,0:T(8,128)} fusion(bf16[8,64,1024]{2,1,0:T(8,128)(2,1)S(1)} %bitcast.28, bf16[896,1024]{1,0:T(8,128)(2,1)S(1)} %copy-done), kind=kOutput, calls=%fused_computation.3 | convolution fusion | flops 939524096 | bytes 4718592 | tf_op jit(solution)/shard_map/dot_general | solution.py:287
  44.2 53.1 %shard_map.87 = (f32[64,896]{1,0:T(8,128)}, f32[64,896]{1,0:T(8,128)}, f32[64,896]{1,0:T(8,128)}) custom-call(f32[8,64,896]{2,1,0:T(8,128)} %fusion.4.refs_0_, f32[8,64,896]{2,1,0:T(8,128)} %fusion.2.refs_1_, f32[8,64,896]{2,1,0:T(8,128)} %fusion.refs_2_), custom_call_target="tpu_custom_call" | custom-call | tf_op jit(solution)/shard_map/pallas_call | solution.py:262
  97.2 2.0 %fusion.13 = (bf16[64,896]{1,0:T(8,128)(2,1)}, bf16[64,896]{1,0:T(8,128)(2,1)}, bf16[64,896]{1,0:T(8,128)(2,1)}) fusion(f32[64,896]{1,0:T(8,128)} %get-tuple-element.14, bf16[64,896]{1,0:T(8,128)(2,1)S(1)} %copy-done.1, bf16[64,896]{1,0:T(8,128)(2,1)S(1)} %copy-done.2, f32[64,896]{1,0:T(8,128)} %get-tuple-element.13, f32[64,896]{1,0:T(8,128)} %get-tuple-element.12), kind=kLoop, calls=%fused_computation.20 | loop fusion | flops 1204224 | bytes 1261568 | tf_op jit(solution)/shard_map/convert_element_type | solution.py:22
  99.2 25.4 %shard_map.88 = (bf16[4,2,64,896]{3,2,1,0:T(8,128)(2,1)}, bf16[4,2,64,896]{3,2,1,0:T(8,128)(2,1)}, bf16[4,2,64,896]{3,2,1,0:T(8,128)(2,1)}) custom-call(bf16[64,896]{1,0:T(8,128)(2,1)} %get-tuple-element.22.refs_0_, bf16[64,896]{1,0:T(8,128)(2,1)} %get-tuple-element.19.refs_1_, bf16[64,896]{1,0:T(8,128)(2,1)} %get-tuple-element.18.refs_2_), custom_call_target="tpu_custom_call" | custom-call | tf_op jit(solution)/shard_map/pallas_call | solution.py:138
  124.7 0.0 copy-start.4
  124.7 2.6 %convolution_convert_fusion = bf16[512,1024]{1,0:T(8,128)(2,1)S(1)} fusion(bf16[512,896]{1,0:T(8,128)(2,1)} %bitcast.33, bf16[896,1024]{1,0:T(8,128)(2,1)S(1)} %copy-done), kind=kOutput, calls=%fused_computation.9 | convolution fusion | flops 940048384 | bytes 3801088 | tf_op jit(solution)/shard_map/dot_general | solution.py:303
  127.3 0.0 copy-start.5
  127.3 1.3 fusion.15
  128.6 0.2 copy-done.5
  128.8 0.2 copy-done.8
  129.0 1.3 add_convert_fusion
  130.4 0.2 pad_maximum_fusion
  130.5 53.5 %all_to_all.5 = bf16[16,32,2048]{2,1,0:T(8,128)(2,1)S(1)} all-to-all(bf16[16,32,2048]{2,1,0:T(8,128)(2,1)S(1)} %bitcast.27), channel_id=1, replica_groups=mesh['dp'=2,'pipe'=8,'tensor'=16] {'tensor'}, dimensions={0} | all-to-all | bytes 4194304 | tf_op jit(solution)/shard_map/all_to_all | solution.py:29
  184.0 0.4 convert_reduce_fusion
  184.4 0.1 reduce_sum.19
  184.5 0.7 fusion.14
  (11 shorter events, 0.0 us)
Async XLA Ops:
  0.6 41.0 %copy-start = (bf16[896,1024]{1,0:T(8,128)(2,1)S(1)}, bf16[896,1024]{1,0:T(8,128)(2,1)}, u32[]{:S(2)}) copy-start(bf16[896,1024]{1,0:T(8,128)(2,1)} %param.13) | copy-start | bytes 5505028
  34.6 4.5 %copy-start.3 = (bf16[1024,896]{1,0:T(8,128)(2,1)S(1)}, bf16[1024,896]{1,0:T(8,128)(2,1)}, u32[]{:S(2)}) copy-start(bf16[1024,896]{1,0:T(8,128)(2,1)} %param.11) | copy-start | bytes 5505028
  34.6 4.5 %copy-start.7 = (bf16[2,8,32,1024]{3,2,1,0:T(8,128)(2,1)S(1)}, bf16[2,8,32,1024]{3,2,1,0:T(8,128)(2,1)}, u32[]{:S(2)}) copy-start(bf16[2,8,32,1024]{3,2,1,0:T(8,128)(2,1)} %get-tuple-element.10) | copy-start | bytes 3145732
  39.1 2.5 %copy-start.6 = (bf16[2,8,32,1024]{3,2,1,0:T(8,128)(2,1)S(1)}, bf16[2,8,32,1024]{3,2,1,0:T(8,128)(2,1)}, u32[]{:S(2)}) copy-start(bf16[2,8,32,1024]{3,2,1,0:T(8,128)(2,1)} %get-tuple-element.11) | copy-start | bytes 3145732
  44.1 53.1 %copy-start.1 = (bf16[64,896]{1,0:T(8,128)(2,1)S(1)}, bf16[64,896]{1,0:T(8,128)(2,1)}, u32[]{:S(2)}) copy-start(bf16[64,896]{1,0:T(8,128)(2,1)} %param.9) | copy-start | bytes 344068
  44.2 53.1 %copy-start.2 = (bf16[64,896]{1,0:T(8,128)(2,1)S(1)}, bf16[64,896]{1,0:T(8,128)(2,1)}, u32[]{:S(2)}) copy-start(bf16[64,896]{1,0:T(8,128)(2,1)} %param.10) | copy-start | bytes 344068
  124.7 2.6 %copy-start.4 = (bf16[1024,896]{1,0:T(8,128)(2,1)S(1)}, bf16[1024,896]{1,0:T(8,128)(2,1)}, u32[]{:S(2)}) copy-start(bf16[1024,896]{1,0:T(8,128)(2,1)} %param.11) | copy-start | bytes 5505028
  124.7 2.6 %copy-start.9 = (bf16[4,2,64,896]{3,2,1,0:T(8,128)(2,1)S(1)}, bf16[4,2,64,896]{3,2,1,0:T(8,128)(2,1)}, u32[]{:S(2)}) copy-start(bf16[4,2,64,896]{3,2,1,0:T(8,128)(2,1)} %get-tuple-element.16) | copy-start | bytes 2752516
  127.3 1.5 copy-start.5
  127.3 1.7 copy-start.8
